TPU v7x, 512 devices: a whole 4x8x8 slice. The times are simulated.
512 devices in a mesh: head: 8 (over y_hi, x), blk: 64 (over y_lo, z, core).
Axes of the slice: x: 4, y: 8 (y_hi: 2, y_lo: 4; y = y_hi * 4 + y_lo), z: 8, core: 2. Of those that a mesh axis runs over, the one named last changes fastest.
Arguments:
- queries: bfloat16 [32768, 4096], P(('head', 'blk')), may hold values from -6 to 6
- keys: bfloat16 [32768, 1024], P(('head', 'blk')), may hold values from -6 to 6
- values: bfloat16 [32768, 1024], P(('head', 'blk')), may hold values from -6 to 6
- grad_out: bfloat16 [32768, 4096], P(('head', 'blk')), may hold values from -6 to 6
- order: int32 [512], replicated, may hold values from 0 to 511, each once
Outputs:
- grad_queries: bfloat16 [32768, 4096], P(('head', 'blk'))
- grad_keys: bfloat16 [32768, 1024], P(('head', 'blk'))
- grad_values: bfloat16 [32768, 1024], P(('head', 'blk'))
Inputs may be any that keep to these rules, and one draw needn't show every extreme that they name: `order`: each value names one slot's pair of half-blocks, each exactly once.
All inputs are finite; a program needn't handle non-finite values.
Results may differ from a plain program's by a relative error of at most 0.024.
Values may be sent and summed in bfloat16 or wider, within the bound.
No kernel may reach another device: no remote copies, remote signals or barrier semaphores. Data moves between devices by JAX's collectives and lax.ppermute only.
A program may use at most 64 MiB of HBM per device.

v0:
```python
import jax
import jax.numpy as jnp
from jax import lax
from jax.sharding import PartitionSpec as P

HD = 128


def from_behind(block, axis, distance):
    devices = range(lax.axis_size(axis))
    route = [((i - distance) % len(devices), i) for i in devices]
    return lax.ppermute(block, axis, route)


def inner_dot(left, right):
    return lax.dot_general(
        left, right, (((1,), (1,)), ((), ())), preferred_element_type=jnp.float32
    )


def outer_dot(left, right):
    return lax.dot_general(
        left, right, (((0,), (0,)), ((), ())), preferred_element_type=jnp.float32
    )


def placed(term, start, total_rows):
    if start == 0 and term.shape[0] == total_rows:
        return term
    return jnp.pad(term, ((start, total_rows - start - term.shape[0]), (0, 0)))


def body(queries, keys, values, grad_out, order):
    score_scale = HD ** (-0.5)
    group_count = lax.axis_size("head")
    cycle_count = lax.axis_size("blk")
    cycle_index = lax.axis_index("blk")
    tok_rows = queries.shape[0]
    half_rows = tok_rows // 2
    slot_total = order.shape[0]
    part_rows = group_count * half_rows

    def early_part(array):
        shaped = array.reshape(group_count, tok_rows, array.shape[1])
        return shaped[:, :half_rows].reshape(part_rows, array.shape[1])

    local_query, local_key, local_value, local_grad = (
        lax.all_to_all(queries, "head", split_axis=1, concat_axis=0, tiled=True),
        lax.all_to_all(keys, "head", split_axis=1, concat_axis=0, tiled=True),
        lax.all_to_all(values, "head", split_axis=1, concat_axis=0, tiled=True),
        lax.all_to_all(grad_out, "head", split_axis=1, concat_axis=0, tiled=True),
    )
    moving = (early_part(local_key), early_part(local_value))
    moving = from_behind((moving[0], moving[1]), "blk", 1)
    gathered = [moving]
    kv_here = local_key.shape[1] // HD
    group_size = local_query.shape[1] // local_key.shape[1]
    heads_here = kv_here * group_size
    slot_table = lax.iota(jnp.int32, slot_total)
    group_ids = lax.iota(jnp.int32, group_count)
    own_slots = group_ids * cycle_count + cycle_index
    own_places = jnp.sum(
        jnp.where(own_slots[:, None] == slot_table[None, :], order[None, :], 0), axis=1
    )
    slot_rank = jnp.sum((own_places[None, :] < own_places[:, None]).astype(jnp.int32), axis=1)
    rank_match = slot_rank[None, :] == group_ids[:, None]
    slot_pick = jnp.sum(jnp.where(rank_match, group_ids[None, :], 0), axis=1)
    sorted_places = jnp.sum(jnp.where(rank_match, own_places[None, :], 0), axis=1)
    offset_in = lax.iota(jnp.int32, half_rows)
    early_pos = (sorted_places[:, None] * half_rows + offset_in[None, :]).reshape(part_rows)
    late_pos = (
        (2 * slot_total - 1 - sorted_places)[:, None] * half_rows + offset_in[None, :]
    ).reshape(part_rows)
    positions = [early_pos, late_pos]

    def sorted_halves(array):
        column_count = array.shape[1]
        shaped = jnp.take(array.reshape(group_count, tok_rows, column_count), slot_pick, axis=0)
        return (
            shaped[:, :half_rows].reshape(part_rows, column_count),
            shaped[:, half_rows:].reshape(part_rows, column_count),
        )

    query_halves = sorted_halves(local_query)
    grad_halves = sorted_halves(local_grad)
    key_sources = list(sorted_halves(local_key)) + [block[0] for block in gathered]
    value_sources = list(sorted_halves(local_value)) + [block[1] for block in gathered]
    source_count = len(key_sources)
    split_count = min(4, group_count)
    part_step = part_rows // split_count
    tile_specs = []
    for part_index in range(split_count):
        row_start = part_index * part_step
        row_stop = row_start + part_step
        tile_specs.append((0, row_start, row_stop, 0, 0, row_stop, True))
        tile_specs.append((1, row_start, row_stop, 1, row_start, part_rows, True))
    tile_specs.append((1, 0, part_rows, 0, 0, part_rows, False))
    hop_index = 0
    tile_specs.append((1, 0, part_rows, 2 + hop_index, 0, part_rows, False))
    tile_masks = []
    for tile_spec in tile_specs:
        query_kind, row_start, row_stop, source, key_start, key_stop, masked = tile_spec
        if masked:
            tile_masks.append(
                positions[source][key_start:key_stop][None, :]
                <= positions[query_kind][row_start:row_stop][:, None]
            )
        else:
            tile_masks.append(None)
    query_parts = [[], []]
    key_heads = [[None] * kv_here for source_index in range(source_count)]
    value_heads = [[None] * kv_here for source_index in range(source_count)]
    kv_index = 0
    for source_index in range(source_count):
        key_heads[source_index][kv_index] = jnp.zeros(
            (key_sources[source_index].shape[0], HD), jnp.float32
        )
        value_heads[source_index][kv_index] = jnp.zeros(
            (value_sources[source_index].shape[0], HD), jnp.float32
        )
    for head_index in range(heads_here):
        kv_index = head_index // group_size
        query_head = [half[:, head_index * HD : (head_index + 1) * HD] for half in query_halves]
        grad_head = [half[:, head_index * HD : (head_index + 1) * HD] for half in grad_halves]
        key_head = [source for source in key_sources]
        value_head = [source for source in value_sources]
        row_tops = [jnp.full((part_rows, 1), -jnp.inf, jnp.float32) for kind_index in range(2)]
        totals = [jnp.zeros((part_rows, 1), jnp.float32) for kind_index in range(2)]
        stored = []
        for tile_index in range(len(tile_specs)):
            query_kind, row_start, row_stop, source, key_start, key_stop, masked = tile_specs[
                tile_index
            ]
            visible = tile_masks[tile_index]
            logits = (
                inner_dot(
                    query_head[query_kind][row_start:row_stop], key_head[source][key_start:key_stop]
                )
                * score_scale
            )
            spread = inner_dot(
                grad_head[query_kind][row_start:row_stop], value_head[source][key_start:key_stop]
            )
            if masked:
                block_top = jnp.max(jnp.where(visible, logits, -jnp.inf), axis=1, keepdims=True)
            else:
                block_top = jnp.max(logits, axis=1, keepdims=True)
            old_top = row_tops[query_kind][row_start:row_stop]
            new_top = jnp.maximum(old_top, block_top)
            shifted = jnp.exp(logits - new_top)
            if masked:
                shifted = jnp.where(visible, shifted, 0.0)
            block_mass = jnp.sum(shifted, axis=1, keepdims=True)
            old_total = totals[query_kind][row_start:row_stop]
            totals[query_kind] = (
                totals[query_kind]
                .at[row_start:row_stop]
                .set(old_total * jnp.exp(old_top - new_top) + block_mass)
            )
            row_tops[query_kind] = row_tops[query_kind].at[row_start:row_stop].set(new_top)
            stored.append((logits, spread))
        log_total = [row_tops[kind_index] + jnp.log(totals[kind_index]) for kind_index in range(2)]
        row_delta = [jnp.zeros((part_rows, 1), jnp.float32) for kind_index in range(2)]
        weighted = []
        for tile_index in range(len(tile_specs)):
            query_kind, row_start, row_stop, source, key_start, key_stop, masked = tile_specs[
                tile_index
            ]
            logits, spread = stored[tile_index]
            weights = jnp.exp(logits - log_total[query_kind][row_start:row_stop])
            if masked:
                weights = jnp.where(tile_masks[tile_index], weights, 0.0)
            weights_low = weights.astype(jnp.bfloat16)
            delta_part = jnp.sum(weights_low.astype(jnp.float32) * spread, axis=1, keepdims=True)
            row_delta[query_kind] = row_delta[query_kind] + placed(delta_part, row_start, part_rows)
            weighted.append((weights, weights_low))
        query_head_acc = [jnp.zeros((part_rows, HD), jnp.float32) for kind_index in range(2)]
        for tile_index in range(len(tile_specs)):
            query_kind, row_start, row_stop, source, key_start, key_stop, masked = tile_specs[
                tile_index
            ]
            spread = stored[tile_index][1]
            weights, weights_low = weighted[tile_index]
            slopes = (weights * (spread - row_delta[query_kind][row_start:row_stop])).astype(
                jnp.bfloat16
            )
            added = jnp.dot(
                slopes, key_head[source][key_start:key_stop], preferred_element_type=jnp.float32
            )
            query_head_acc[query_kind] = query_head_acc[query_kind] + placed(
                added, row_start, part_rows
            )
            source_rows = key_sources[source].shape[0]
            key_term = outer_dot(slopes, query_head[query_kind][row_start:row_stop]) * score_scale
            key_heads[source][kv_index] = key_heads[source][kv_index] + placed(
                key_term, key_start, source_rows
            )
            value_term = outer_dot(weights_low, grad_head[query_kind][row_start:row_stop])
            value_heads[source][kv_index] = value_heads[source][kv_index] + placed(
                value_term, key_start, source_rows
            )
        query_parts[0].append(query_head_acc[0])
        query_parts[1].append(query_head_acc[1])
    key_acc = [
        jnp.concatenate(key_heads[source_index], axis=1) for source_index in range(source_count)
    ]
    value_acc = [
        jnp.concatenate(value_heads[source_index], axis=1) for source_index in range(source_count)
    ]

    def unsorted_rows(early, late):
        column_count = early.shape[1]
        joined = jnp.concatenate(
            [
                early.reshape(group_count, half_rows, column_count),
                late.reshape(group_count, half_rows, column_count),
            ],
            axis=1,
        )
        return jnp.take(joined, slot_rank, axis=0).reshape(group_count * tok_rows, column_count)

    def add_early(total, addition, row_span):
        column_count = total.shape[1]
        shaped = total.reshape(-1, row_span, column_count)
        front = shaped[:, :half_rows] + addition.reshape(shaped.shape[0], half_rows, column_count)
        joined = jnp.concatenate([front, shaped[:, half_rows:]], axis=1)
        return joined.reshape(-1, column_count)

    query_early = jnp.concatenate(query_parts[0], axis=1) * score_scale
    query_late = jnp.concatenate(query_parts[1], axis=1) * score_scale
    query_low = unsorted_rows(query_early, query_late).astype(jnp.bfloat16)
    own_key = unsorted_rows(key_acc[0], key_acc[1])
    own_value = unsorted_rows(value_acc[0], value_acc[1])
    key_total, value_total = (own_key, own_value)
    hop_index = 0
    arrived = from_behind(
        (key_acc[2 + hop_index], value_acc[2 + hop_index]), "blk", -(hop_index + 1)
    )
    key_total = add_early(key_total, arrived[0], tok_rows)
    value_total = add_early(value_total, arrived[1], tok_rows)
    grad_queries, grad_keys, grad_values = (
        lax.all_to_all(query_low, "head", split_axis=0, concat_axis=1, tiled=True),
        lax.all_to_all(
            key_total.astype(jnp.bfloat16), "head", split_axis=0, concat_axis=1, tiled=True
        ),
        lax.all_to_all(
            value_total.astype(jnp.bfloat16), "head", split_axis=0, concat_axis=1, tiled=True
        ),
    )
    return (grad_queries, grad_keys, grad_values)


def solution(mesh):
    placed = (
        P(("head", "blk"), None),
        P(("head", "blk"), None),
        P(("head", "blk"), None),
        P(("head", "blk"), None),
        P(),
    )
    return jax.shard_map(
        body,
        mesh=mesh,
        in_specs=placed,
        out_specs=(P(("head", "blk"), None), P(("head", "blk"), None), P(("head", "blk"), None)),
        check_vma=False,
    )
```

profile of v0, /device:TPU:16, one launch (start us, length us, event | category | flops | bytes accessed | tf_op | source)
XLA Modules:
  0.0 351.9 jit_solution(4311280984311436085)
XLA Ops:
  2.2 7.8 %all-to-all-start.3 = ((bf16[64,8,128]{2,0,1:T(8,128)(2,1)}), bf16[64,8,128]{2,0,1:T(8,128)(2,1)S(1)}, u32[]{:S(2)}, u32[]{:S(2)}) async-start(bf16[64,8,128]{2,0,1:T(8,128)(2,1)} %copy_bitcast_fusion.4), calls=%async_computation.3 | async-start | bytes 262144 | tf_op jit(solution)/shard_map/all_to_all | solution.py:50
  12.0 9.1 %all-to-all-done.3 = bf16[64,8,128]{2,0,1:T(8,128)(2,1)S(1)} async-done(((bf16[64,8,128]{2,0,1:T(8,128)(2,1)}), bf16[64,8,128]{2,0,1:T(8,128)(2,1)S(1)}, u32[]{:S(2)}, u32[]{:S(2)}) %all-to-all-start.3) | async-done | bytes 131104 | tf_op jit(solution)/shard_map/all_to_all | solution.py:50
  21.1 3.4 all-to-all-start.1
  25.4 9.6 %all-to-all-done.1 = bf16[64,8,128]{2,0,1:T(8,128)(2,1)S(1)} async-done(((bf16[64,8,128]{2,0,1:T(8,128)(2,1)}), bf16[64,8,128]{2,0,1:T(8,128)(2,1)S(1)}, u32[]{:S(2)}, u32[]{:S(2)}) %all-to-all-start.1) | async-done | bytes 131104 | tf_op jit(solution)/shard_map/all_to_all | solution.py:49
  34.9 3.6 %all-to-all-start = ((bf16[64,8,512]{2,0,1:T(8,128)(2,1)}), bf16[64,8,512]{2,0,1:T(8,128)(2,1)S(1)}, u32[]{:S(2)}, u32[]{:S(2)}) async-start(bf16[64,8,512]{2,0,1:T(8,128)(2,1)} %bitcast.620), calls=%async_computation | async-start | bytes 1048576 | tf_op jit(solution)/shard_map/all_to_all | solution.py:48
  48.7 1.9 collective-permute-start.1
  50.6 4.4 %collective-permute-start = (bf16[256,128]{1,0:T(8,128)(2,1)}, bf16[256,128]{1,0:T(8,128)(2,1)S(1)}, u32[]{:S(2)}, u32[]{:S(2)}) collective-permute-start(bf16[256,128]{1,0:T(8,128)(2,1)} %bitcast.116), channel_id=1, source_target_pairs={{63,0},{0,1},{1,2},{2,3},{3,4},{4,5},{5,6},{6,7},{7,8},{8,9},{9,10... | collective-permute-start | bytes 196616 | tf_op jit(solution)/shard_map/ppermute | solution.py:12
  55.1 9.5 %all-to-all-start.2 = ((bf16[64,8,512]{2,0,1:T(8,128)(2,1)}), bf16[64,8,512]{2,0,1:T(8,128)(2,1)S(1)}, u32[]{:S(2)}, u32[]{:S(2)}) async-start(bf16[64,8,512]{2,0,1:T(8,128)(2,1)} %bitcast.619), calls=%async_computation.2 | async-start | bytes 1048576 | tf_op jit(solution)/shard_map/all_to_all | solution.py:51
  67.2 16.6 %all-to-all-done.2 = bf16[64,8,512]{2,0,1:T(8,128)(2,1)S(1)} async-done(((bf16[64,8,512]{2,0,1:T(8,128)(2,1)}), bf16[64,8,512]{2,0,1:T(8,128)(2,1)S(1)}, u32[]{:S(2)}, u32[]{:S(2)}) %all-to-all-start.2) | async-done | bytes 524320 | tf_op jit(solution)/shard_map/all_to_all | solution.py:51
  96.0 1.3 fusion.189
  106.4 1.3 multiply_reduce_fusion.30
  122.5 1.3 fusion.165
  129.1 1.4 scatter.221
  130.5 1.3 scatter.215
  131.9 2.3 fusion.66
  135.3 1.4 scatter.255
  137.8 1.4 scatter.241
  140.4 1.4 scatter.229
  143.1 1.7 fusion.67
  157.3 1.3 scatter.219
  158.6 1.3 scatter.225
  159.9 1.3 scatter.250
  161.2 1.4 fusion.410
  162.6 1.3 scatter.245
  163.9 1.4 scatter.251
  165.3 1.5 fusion.342
  166.8 1.5 fusion.366
  168.2 1.3 scatter.236
  169.5 1.4 fusion.412
  170.9 1.4 scatter.231
  172.2 1.3 scatter.239
  178.1 2.2 multiply_reduce_fusion.39
  182.7 1.4 scatter.261
  184.7 1.2 fusion.409
  185.9 1.2 scatter.264
  187.8 1.2 fusion.408
  189.0 1.3 scatter.259
  190.3 1.2 scatter.265
  207.5 1.0 fusion.147
  213.2 1.0 fusion.136
  286.0 3.1 collective-permute-start.2
  291.4 5.3 %collective-permute-start.3 = (f32[256,128]{1,0:T(8,128)S(1)}, f32[256,128]{1,0:T(8,128)S(1)}, u32[]{:S(2)}, u32[]{:S(2)}) collective-permute-start(f32[256,128]{1,0:T(8,128)S(1)} %convolution_add_fusion), channel_id=1, source_target_pairs={{1,0},{2,1},{3,2},{4,3},{5,4},{6,5},{7,6},{8,7},{9,8},{10,9},{11,1... | collective-permute-start | bytes 393224 | tf_op jit(solution)/shard_map/ppermute | solution.py:12
  305.9 3.4 all-to-all-start.5
  309.9 9.8 %all-to-all-done.5 = bf16[8,64,128]{2,1,0:T(8,128)(2,1)S(1)} async-done(((bf16[8,64,128]{2,1,0:T(8,128)(2,1)}), bf16[8,64,128]{2,1,0:T(8,128)(2,1)S(1)}, u32[]{:S(2)}, u32[]{:S(2)}) %all-to-all-start.5) | async-done | bytes 131104 | tf_op jit(solution)/shard_map/all_to_all | solution.py:243
  319.8 3.4 all-to-all-start.6
  324.1 9.6 %all-to-all-done.6 = bf16[8,64,128]{2,1,0:T(8,128)(2,1)S(1)} async-done(((bf16[8,64,128]{2,1,0:T(8,128)(2,1)}), bf16[8,64,128]{2,1,0:T(8,128)(2,1)S(1)}, u32[]{:S(2)}, u32[]{:S(2)}) %all-to-all-start.6) | async-done | bytes 131104 | tf_op jit(solution)/shard_map/all_to_all | solution.py:246
  333.7 3.5 all-to-all-start.4
  338.6 12.5 %all-to-all-done.4 = bf16[8,64,512]{2,1,0:T(8,128)(2,1)S(1)} async-done(((bf16[8,64,512]{2,1,0:T(8,128)(2,1)}), bf16[8,64,512]{2,1,0:T(8,128)(2,1)S(1)}, u32[]{:S(2)}, u32[]{:S(2)}) %all-to-all-start.4) | async-done | bytes 524320 | tf_op jit(solution)/shard_map/all_to_all | solution.py:242
  (1028 shorter events, 189.2 us)
Async XLA Ops:
  0.6 10.7 %copy-start.137 = (bf16[64,1024]{1,0:T(8,128)(2,1)S(1)}, bf16[64,1024]{1,0:T(8,128)(2,1)}, u32[]{:S(2)}) copy-start(bf16[64,1024]{1,0:T(8,128)(2,1)} %param.204) | copy-start | bytes 393220
  0.7 23.9 %copy-start.74 = (bf16[64,4096]{1,0:T(8,128)(2,1)S(1)}, bf16[64,4096]{1,0:T(8,128)(2,1)}, u32[]{:S(2)}) copy-start(bf16[64,4096]{1,0:T(8,128)(2,1)} %param.203) | copy-start | bytes 1572868
  2.2 18.9 %all-to-all-start.3 = ((bf16[64,8,128]{2,0,1:T(8,128)(2,1)}), bf16[64,8,128]{2,0,1:T(8,128)(2,1)S(1)}, u32[]{:S(2)}, u32[]{:S(2)}) async-start(bf16[64,8,128]{2,0,1:T(8,128)(2,1)} %copy_bitcast_fusion.4), calls=%async_computation.3 | async-start | bytes 262144 | tf_op jit(solution)/shard_map/all_to_all | solution.py:50
  21.1 13.8 %all-to-all-start.1 = ((bf16[64,8,128]{2,0,1:T(8,128)(2,1)}), bf16[64,8,128]{2,0,1:T(8,128)(2,1)S(1)}, u32[]{:S(2)}, u32[]{:S(2)}) async-start(bf16[64,8,128]{2,0,1:T(8,128)(2,1)} %copy_bitcast_fusion.5), calls=%async_computation.1 | async-start | bytes 262144 | tf_op jit(solution)/shard_map/all_to_all | solution.py:49
  34.9 4.4 %copy-start.75 = (bf16[64,4096]{1,0:T(8,128)(2,1)S(1)}, bf16[64,4096]{1,0:T(8,128)(2,1)}, u32[]{:S(2)}) copy-start(bf16[64,4096]{1,0:T(8,128)(2,1)} %param.206) | copy-start | bytes 1572868
  34.9 20.2 %all-to-all-start = ((bf16[64,8,512]{2,0,1:T(8,128)(2,1)}), bf16[64,8,512]{2,0,1:T(8,128)(2,1)S(1)}, u32[]{:S(2)}, u32[]{:S(2)}) async-start(bf16[64,8,512]{2,0,1:T(8,128)(2,1)} %bitcast.620), calls=%async_computation | async-start | bytes 1048576 | tf_op jit(solution)/shard_map/all_to_all | solution.py:48
  38.7 48.7 %copy-start.156 = (s32[256]{0:T(256)}, s32[256]{0:T(256)S(1)}, u32[]{:S(2)}) copy-start(s32[256]{0:T(256)S(1)} %add.1244) | copy-start | bytes 3076
  40.3 47.1 %copy-start.180 = (s32[64]{0:T(128)}, s32[64]{0:T(128)S(1)}, u32[]{:S(2)}) copy-start(s32[64]{0:T(128)S(1)} %le.167) | copy-start | bytes 772
  40.3 47.9 %copy-start.162 = (s32[192]{0:T(256)}, s32[192]{0:T(256)S(1)}, u32[]{:S(2)}) copy-start(s32[192]{0:T(256)S(1)} %le.170) | copy-start | bytes 2308
  40.4 47.9 %copy-start.178 = (s32[64]{0:T(128)}, s32[64]{0:T(128)S(1)}, u32[]{:S(2)}) copy-start(s32[64]{0:T(128)S(1)} %le.172) | copy-start | bytes 772
  40.5 50.0 %copy-start.191 = (s32[128]{0:T(128)}, s32[128]{0:T(128)S(1)}, u32[]{:S(2)}) copy-start(s32[128]{0:T(128)S(1)} %le.175) | copy-start | bytes 1540
  40.6 49.9 %copy-start.220 = (s32[64]{0:T(128)}, s32[64]{0:T(128)S(1)}, u32[]{:S(2)}) copy-start(s32[64]{0:T(128)S(1)} %le.177) | copy-start | bytes 772
  40.7 55.3 %copy-start.130 = (s32[64]{0:T(128)}, s32[64]{0:T(128)S(1)}, u32[]{:S(2)}) copy-start(s32[64]{0:T(128)S(1)} %le.180) | copy-start | bytes 772
  48.7 158.8 %collective-permute-start.1 = (bf16[256,128]{1,0:T(8,128)(2,1)}, bf16[256,128]{1,0:T(8,128)(2,1)}, u32[]{:S(2)}, u32[]{:S(2)}) collective-permute-start(bf16[256,128]{1,0:T(8,128)(2,1)} %bitcast.143), channel_id=1, source_target_pairs={{63,0},{0,1},{1,2},{2,3},{3,4},{4,5},{5,6},{6,7},{7,8},{8,9},{9,10... | collective-permute-start | bytes 196616 | tf_op jit(solution)/shard_map/ppermute | solution.py:12
  50.6 49.6 %collective-permute-start = (bf16[256,128]{1,0:T(8,128)(2,1)}, bf16[256,128]{1,0:T(8,128)(2,1)S(1)}, u32[]{:S(2)}, u32[]{:S(2)}) collective-permute-start(bf16[256,128]{1,0:T(8,128)(2,1)} %bitcast.116), channel_id=1, source_target_pairs={{63,0},{0,1},{1,2},{2,3},{3,4},{4,5},{5,6},{6,7},{7,8},{8,9},{9,10... | collective-permute-start | bytes 196616 | tf_op jit(solution)/shard_map/ppermute | solution.py:12
  55.1 28.6 %all-to-all-start.2 = ((bf16[64,8,512]{2,0,1:T(8,128)(2,1)}), bf16[64,8,512]{2,0,1:T(8,128)(2,1)S(1)}, u32[]{:S(2)}, u32[]{:S(2)}) async-start(bf16[64,8,512]{2,0,1:T(8,128)(2,1)} %bitcast.619), calls=%async_computation.2 | async-start | bytes 1048576 | tf_op jit(solution)/shard_map/all_to_all | solution.py:51
  65.3 28.4 %copy-start.90 = (bf16[2,32,128]{2,1,0:T(8,128)(2,1)}, bf16[2,32,128]{2,1,0:T(8,128)(2,1)S(1)}, u32[]{:S(2)}) copy-start(bf16[2,32,128]{2,1,0:T(8,128)(2,1)S(1)} %get-tuple-element.1215) | copy-start | bytes 49156
  65.3 30.7 %copy-start.37 = (bf16[2,32,128]{2,1,0:T(8,128)(2,1)}, bf16[2,32,128]{2,1,0:T(8,128)(2,1)S(1)}, u32[]{:S(2)}) copy-start(bf16[2,32,128]{2,1,0:T(8,128)(2,1)S(1)} %get-tuple-element.1394) | copy-start | bytes 49156
  66.6 50.7 %copy-start.27 = (bf16[8,32,128]{2,1,0:T(8,128)(2,1)}, bf16[8,32,128]{2,1,0:T(8,128)(2,1)S(1)}, u32[]{:S(2)}) copy-start(bf16[8,32,128]{2,1,0:T(8,128)(2,1)S(1)} %get-tuple-element.1222) | copy-start | bytes 196612
  85.3 32.9 %copy-start.15 = (bf16[8,32,512]{2,1,0:T(8,128)(2,1)}, bf16[8,32,512]{2,1,0:T(8,128)(2,1)S(1)}, u32[]{:S(2)}) copy-start(bf16[8,32,512]{2,1,0:T(8,128)(2,1)S(1)} %get-tuple-element.1206) | copy-start | bytes 786436
  86.8 9.1 %copy-start.55 = (f32[64,64]{0,1:T(8,128)}, f32[64,64]{0,1:T(8,128)S(1)}, u32[]{:S(2)}) copy-start(f32[64,64]{0,1:T(8,128)S(1)} %convolution_multiply_fusion.62) | copy-start | bytes 49156
  87.0 9.0 %copy-start.58 = (f32[64,64]{0,1:T(8,128)}, f32[64,64]{0,1:T(8,128)S(1)}, u32[]{:S(2)}) copy-start(f32[64,64]{0,1:T(8,128)S(1)} %convolution_multiply_fusion.64) | copy-start | bytes 49156
  106.4 4.6 %copy-start.46 = (bf16[4,32,128]{2,1,0:T(8,128)(2,1)S(1)}, bf16[4,32,128]{2,1,0:T(8,128)(2,1)}, u32[]{:S(2)}) copy-start(bf16[4,32,128]{2,1,0:T(8,128)(2,1)} %get-tuple-element.1211) | copy-start | bytes 98308
  119.2 36.1 %copy-start.1 = (f32[64,256]{1,0:T(8,128)}, f32[64,256]{1,0:T(8,128)S(1)}, u32[]{:S(2)}) copy-start(f32[64,256]{1,0:T(8,128)S(1)} %convolution_multiply_fusion.48) | copy-start | bytes 196612
  121.6 20.8 %copy-start.9 = (f32[64,192]{1,0:T(8,128)}, f32[64,192]{1,0:T(8,128)S(1)}, u32[]{:S(2)}) copy-start(f32[64,192]{1,0:T(8,128)S(1)} %convolution_multiply_fusion.45) | copy-start | bytes 147460
  121.8 20.7 %copy-start.11 = (f32[64,192]{1,0:T(8,128)}, f32[64,192]{1,0:T(8,128)S(1)}, u32[]{:S(2)}) copy-start(f32[64,192]{1,0:T(8,128)S(1)} %convolution_multiply_fusion.47) | copy-start | bytes 147460
  122.3 20.2 %copy-start.13 = (f32[64,192]{1,0:T(8,128)}, f32[64,192]{1,0:T(8,128)S(1)}, u32[]{:S(2)}) copy-start(f32[64,192]{1,0:T(8,128)S(1)} %convolution_multiply_fusion.49) | copy-start | bytes 147460
  122.5 5.5 %copy-start.292 = (f32[64]{0:T(128)}, f32[64]{0:T(128)S(1)}, u32[]{:S(2)}) copy-start(f32[64]{0:T(128)S(1)} %get-tuple-element.1183) | copy-start | bytes 772
  122.5 6.1 %copy-start.290 = (f32[64]{0:T(128)}, f32[64]{0:T(128)S(1)}, u32[]{:S(2)}) copy-start(f32[64]{0:T(128)S(1)} %get-tuple-element.1184) | copy-start | bytes 772
  146.8 8.3 %copy-start.205 = (f32[256,1]{0,1:T(1,128)}, f32[256,1]{0,1:T(1,128)S(1)}, u32[]{:S(2)}) copy-start(f32[256,1]{0,1:T(1,128)S(1)} %scatter.216) | copy-start | bytes 3076
  147.4 7.7 %copy-start.246 = (f32[256,1]{0,1:T(1,128)}, f32[256,1]{0,1:T(1,128)S(1)}, u32[]{:S(2)}) copy-start(f32[256,1]{0,1:T(1,128)S(1)} %scatter.256) | copy-start | bytes 3076
  150.4 4.8 %copy-start.201 = (f32[256,1]{0,1:T(1,128)}, f32[256,1]{0,1:T(1,128)S(1)}, u32[]{:S(2)}) copy-start(f32[256,1]{0,1:T(1,128)S(1)} %scatter.244) | copy-start | bytes 3076
  156.6 34.9 %copy-start.18 = (bf16[8,32,512]{2,1,0:T(8,128)(2,1)S(1)}, bf16[8,32,512]{2,1,0:T(8,128)(2,1)}, u32[]{:S(2)}) copy-start(bf16[8,32,512]{2,1,0:T(8,128)(2,1)} %get-tuple-element.1389) | copy-start | bytes 786436
  197.4 80.1 %copy-start.164 = (f32[256,1]{0,1:T(1,128)}, f32[256,1]{0,1:T(1,128)S(1)}, u32[]{:S(2)}) copy-start(f32[256,1]{0,1:T(1,128)S(1)} %log_add_fusion) | copy-start | bytes 3076
  286.0 18.1 %collective-permute-start.2 = (f32[256,128]{1,0:T(8,128)}, f32[256,128]{1,0:T(8,128)}, u32[]{:S(2)}, u32[]{:S(2)}) collective-permute-start(f32[256,128]{1,0:T(8,128)} %fusion.15), channel_id=1, source_target_pairs={{1,0},{2,1},{3,2},{4,3},{5,4},{6,5},{7,6},{8,7},{9,8},{10,9},{11,1... | collective-permute-start | bytes 393224 | tf_op jit(solution)/shard_map/ppermute | solution.py:12
  291.2 5.6 %copy-start.115 = (f32[64,128]{1,0:T(8,128)S(1)}, f32[64,128]{1,0:T(8,128)}, u32[]{:S(2)}) copy-start(f32[64,128]{1,0:T(8,128)} %fusion.501) | copy-start | bytes 98308
  291.2 5.6 %copy-start.122 = (f32[64,128]{1,0:T(8,128)S(1)}, f32[64,128]{1,0:T(8,128)}, u32[]{:S(2)}) copy-start(f32[64,128]{1,0:T(8,128)} %fusion.503) | copy-start | bytes 98308
  291.2 5.6 %copy-start.123 = (f32[64,128]{1,0:T(8,128)S(1)}, f32[64,128]{1,0:T(8,128)}, u32[]{:S(2)}) copy-start(f32[64,128]{1,0:T(8,128)} %fusion.502) | copy-start | bytes 98308
  291.2 5.6 %copy-start.127 = (f32[64,128]{1,0:T(8,128)S(1)}, f32[64,128]{1,0:T(8,128)}, u32[]{:S(2)}) copy-start(f32[64,128]{1,0:T(8,128)} %fusion.500) | copy-start | bytes 98308
  291.4 5.7 %copy-start.32 = (bf16[256,256]{0,1:T(8,128)(2,1)S(1)}, bf16[256,256]{0,1:T(8,128)(2,1)}, u32[]{:S(2)}) copy-start(bf16[256,256]{0,1:T(8,128)(2,1)} %copy-done.31) | copy-start | bytes 393220
  291.4 5.7 %copy-start.114 = (f32[64,128]{1,0:T(8,128)S(1)}, f32[64,128]{1,0:T(8,128)}, u32[]{:S(2)}) copy-start(f32[64,128]{1,0:T(8,128)} %fusion.497) | copy-start | bytes 98308
  291.4 5.7 %copy-start.120 = (f32[64,128]{1,0:T(8,128)S(1)}, f32[64,128]{1,0:T(8,128)}, u32[]{:S(2)}) copy-start(f32[64,128]{1,0:T(8,128)} %fusion.499) | copy-start | bytes 98308
  291.4 5.7 %copy-start.121 = (f32[64,128]{1,0:T(8,128)S(1)}, f32[64,128]{1,0:T(8,128)}, u32[]{:S(2)}) copy-start(f32[64,128]{1,0:T(8,128)} %fusion.498) | copy-start | bytes 98308
  291.4 5.7 %copy-start.126 = (f32[64,128]{1,0:T(8,128)S(1)}, f32[64,128]{1,0:T(8,128)}, u32[]{:S(2)}) copy-start(f32[64,128]{1,0:T(8,128)} %fusion.496) | copy-start | bytes 98308
  291.4 17.8 %collective-permute-start.3 = (f32[256,128]{1,0:T(8,128)S(1)}, f32[256,128]{1,0:T(8,128)S(1)}, u32[]{:S(2)}, u32[]{:S(2)}) collective-permute-start(f32[256,128]{1,0:T(8,128)S(1)} %convolution_add_fusion), channel_id=1, source_target_pairs={{1,0},{2,1},{3,2},{4,3},{5,4},{6,5},{7,6},{8,7},{9,8},{10,9},{11,1... | collective-permute-start | bytes 393224 | tf_op jit(solution)/shard_map/ppermute | solution.py:12
  305.9 13.9 %all-to-all-start.5 = ((bf16[8,64,128]{2,1,0:T(8,128)(2,1)}), bf16[8,64,128]{2,1,0:T(8,128)(2,1)S(1)}, u32[]{:S(2)}, u32[]{:S(2)}) async-start(bf16[8,64,128]{2,1,0:T(8,128)(2,1)} %pad_maximum_fusion.3), calls=%async_computation.5 | async-start | bytes 262144 | tf_op jit(solution)/shard_map/all_to_all | solution.py:243
  319.8 13.9 %all-to-all-start.6 = ((bf16[8,64,128]{2,1,0:T(8,128)(2,1)}), bf16[8,64,128]{2,1,0:T(8,128)(2,1)S(1)}, u32[]{:S(2)}, u32[]{:S(2)}) async-start(bf16[8,64,128]{2,1,0:T(8,128)(2,1)} %pad_maximum_fusion.4), calls=%async_computation.6 | async-start | bytes 262144 | tf_op jit(solution)/shard_map/all_to_all | solution.py:246
  333.7 17.3 %all-to-all-start.4 = ((bf16[8,64,512]{2,1,0:T(8,128)(2,1)}), bf16[8,64,512]{2,1,0:T(8,128)(2,1)S(1)}, u32[]{:S(2)}, u32[]{:S(2)}) async-start(bf16[8,64,512]{2,1,0:T(8,128)(2,1)} %select_convert_fusion), calls=%async_computation.4 | async-start | bytes 1048576 | tf_op jit(solution)/shard_map/all_to_all | solution.py:242
  (266 other events, 256.3 us)
where the time goes:
time: 357 us; the launch traced here: 352 us
  local copies, waits for them, and re-layouts  115 us (32%)
  matrix products  90.3 us (25%)
  waiting for transfers between devices  67.1 us (19%)
  starting transfers between devices  49.3 us (14%)
  other arithmetic  26.5 us (7%)
    unnamed x607, local copies, waits for them, and re-layouts  59.3 us
    dot_general x80, matrix products, inner_dot(): lax.dot_general(left, right, (((1,), (1,)), ((), ())), preferred_element_...  38.6 us
    dot_general x40, matrix products, body(): jnp.dot(slopes, key_head[source][key_start:key_stop], preferred_element_t...  26 us
    dot_general x80, matrix products, outer_dot(): lax.dot_general(left, right, (((0,), (0,)), ((), ())), preferred_element_...  25.7 us
    all_to_all x1, waiting for transfers between devices, body(): lax.all_to_all(grad_out, 'head', split_axis=1, concat_axis=0, tiled=True)  16.6 us
    scatter x32, local copies, waits for them, and re-layouts, body(): row_tops[query_kind].at[row_start:row_stop].set(new_top)  16.3 us
    scatter x32, local copies, waits for them, and re-layouts, body(): totals[query_kind] = totals[query_kind].at[row_start:row_stop].set(old_to...  16.1 us
    ppermute x4, starting transfers between devices, from_behind(): return lax.ppermute(block, axis, route)  14.8 us
  transfers between devices with their start and end apart: 11, of which 6 were waited for; matrix products, arithmetic and copies ran while one was open for 32% of the time, Pallas kernels for 0%

commit v1 on v0

v1 whole, which is shorter than its diff:
```python
import jax
import jax.numpy as jnp
from jax import lax
from jax.experimental import pallas as pl
from jax.experimental.pallas import tpu as pltpu
from jax.sharding import PartitionSpec as P

HD = 128
XN = 4
KV = 2
GROUP = 4
LOG2E = 1.4426950408889634
NEG = -1e30


def dot(left, right, left_dim, right_dim):
    return lax.dot_general(
        left, right, (((left_dim,), (right_dim,)), ((), ())), preferred_element_type=jnp.float32
    )


def attention_kernel(
    qpos_ref, kpos_ref, qg_ref, own_ref, far_ref, pown_ref, pfar_ref, dq_ref, dkv_ref, dprev_ref
):
    half = qg_ref.shape[1] // 2
    slots = qg_ref.shape[0]
    rows = slots * half
    scale = HD ** (-0.5)
    width = KV * GROUP * HD
    qpos = qpos_ref[...]
    kpos = kpos_ref[...]
    keys = kpos.shape[0]
    early_seen = kpos[:, 0:1] <= qpos[0:1, :]
    late_seen = kpos[:, 1:2] <= qpos[1:2, :]

    def columns(ref, start, stop, column):
        block = ref[:, start:stop, column : column + HD]
        return block.reshape(block.shape[0] * block.shape[1], HD)

    def tile(query, grad, key, value, seen, seen_from):
        logits = dot(key, query, 1, 1) * (scale * LOG2E)
        if seen_from == 0 and seen.shape[0] == key.shape[0]:
            logits = jnp.where(seen, logits, NEG)
        else:
            stop = seen_from + seen.shape[0]
            logits = jnp.concatenate(
                [
                    logits[:seen_from],
                    jnp.where(seen, logits[seen_from:stop], NEG),
                    logits[stop:],
                ],
                axis=0,
            )
        spread = dot(value, grad, 1, 1)
        top = jnp.max(logits, axis=0, keepdims=True)
        mass = jnp.exp2(logits - top)
        weights = mass * (1.0 / jnp.sum(mass, axis=0, keepdims=True))
        low = weights.astype(jnp.bfloat16)
        delta = jnp.sum(low.astype(jnp.float32) * spread, axis=0, keepdims=True)
        slopes = (weights * (spread - delta)).astype(jnp.bfloat16)
        return (
            dot(slopes, key, 0, 0) * scale,
            dot(slopes, query, 1, 0) * scale,
            dot(low, grad, 1, 0),
        )

    for kv in range(KV):
        parts = []
        for column in (kv * HD, (KV + kv) * HD):
            early = [columns(ref, 0, half, column) for ref in (own_ref, far_ref)]
            late = [columns(ref, half, 2 * half, column) for ref in (own_ref, far_ref)]
            before = [columns(ref, 0, half, column) for ref in (pown_ref, pfar_ref)]
            parts.append(jnp.concatenate(early + late + before, axis=0))
        key, value = parts
        key_sum = None
        value_sum = None
        for pair in range(GROUP // 2):
            heads = [kv * GROUP + pair * 2 + i for i in range(2)]
            for kind in range(2):
                start, stop = kind * half, (kind + 1) * half
                query = jnp.concatenate(
                    [columns(qg_ref, start, stop, h * HD) for h in heads], axis=0
                )
                grad = jnp.concatenate(
                    [columns(qg_ref, start, stop, width + h * HD) for h in heads], axis=0
                )
                if kind == 0:
                    dq, dk, dv = tile(query, grad, key[:keys], value[:keys], early_seen, 0)
                    early_key, early_value = dk, dv
                else:
                    dq, dk, dv = tile(query, grad, key, value, late_seen, keys)
                for i, h in enumerate(heads):
                    dq_ref[:, start:stop, h * HD : (h + 1) * HD] = (
                        dq[i * rows : (i + 1) * rows].reshape(slots, half, HD).astype(jnp.bfloat16)
                    )
            dk = jnp.concatenate([dk[:keys] + early_key, dk[keys:]], axis=0)
            dv = jnp.concatenate([dv[:keys] + early_value, dv[keys:]], axis=0)
            key_sum = dk if key_sum is None else key_sum + dk
            value_sum = dv if value_sum is None else value_sum + dv
        for total, column in ((key_sum, kv * HD), (value_sum, (KV + kv) * HD)):
            low = total.astype(jnp.bfloat16)
            for kind in range(2):
                dkv_ref[:, kind * half : (kind + 1) * half, column : column + HD] = low[
                    kind * keys : (kind + 1) * keys
                ].reshape(2 * slots, half, HD)
            dprev_ref[:, :, column : column + HD] = low[2 * keys :].reshape(2 * slots, half, HD)


def attention(qpos, kpos, qg, own, far, pown, pfar):
    slots, tok, _ = qg.shape
    lines = own.shape[2]
    return pl.pallas_call(
        attention_kernel,
        out_shape=(
            jax.ShapeDtypeStruct((slots, tok, KV * GROUP * HD), jnp.bfloat16),
            jax.ShapeDtypeStruct((2 * slots, tok, lines), jnp.bfloat16),
            jax.ShapeDtypeStruct((2 * slots, tok // 2, lines), jnp.bfloat16),
        ),
        compiler_params=pltpu.CompilerParams(vmem_limit_bytes=48 * 1024 * 1024),
    )(qpos, kpos, qg, own, far, pown, pfar)


def body(queries, keys, values, grad_out, order):
    groups = lax.axis_size("head")
    cycle = lax.axis_size("blk")
    mine = lax.axis_index("blk")
    tok = queries.shape[0]
    half = tok // 2
    slot_total = order.shape[0]
    teams = [list(range(t, t + XN)) for t in range(0, groups, XN)]
    ahead = [(i, (i + 1) % cycle) for i in range(cycle)]
    behind = [(j, i) for i, j in ahead]
    across = [(h, (h + XN) % groups) for h in range(groups)]
    across_ahead = [
        (h * cycle + b, ((h + XN) % groups) * cycle + (b + 1) % cycle)
        for h in range(groups)
        for b in range(cycle)
    ]

    def team_exchange(array):
        return lax.all_to_all(array, "head", 0, 0, tiled=True, axis_index_groups=teams)

    def packed(first, second):
        blocks = [a.reshape(tok, XN, a.shape[1] // XN) for a in (first, second)]
        return jnp.concatenate(blocks, axis=2).transpose(1, 0, 2)

    own = team_exchange(packed(keys, values))
    far = lax.ppermute(own, "head", across)
    pown = lax.ppermute(own[:, :half], "blk", ahead)
    pfar = lax.ppermute(own[:, :half], ("head", "blk"), across_ahead)
    qg = team_exchange(packed(queries, grad_out))

    team = lax.axis_index("head") // XN
    places = lax.dynamic_index_in_dim(order.reshape(groups, cycle), mine, axis=1, keepdims=False)
    places = jnp.where(team == 0, places, jnp.roll(places, -XN))
    offset = lax.iota(jnp.int32, half)
    early = (places[:, None] * half + offset[None, :]).reshape(groups * half)
    late = ((2 * slot_total - 1 - places)[:, None] * half + offset[None, :]).reshape(groups * half)
    kpos = jnp.stack([early, late], axis=1)
    qpos = jnp.stack([jnp.tile(p[: XN * half], 2) for p in (early, late)], axis=0)

    dq, dkv, dprev = attention(qpos, kpos, qg, own, far, pown, pfar)

    back = lax.ppermute(dprev, "blk", behind)
    dq = team_exchange(dq)
    front = (dkv[:, :half].astype(jnp.float32) + back.astype(jnp.float32)).astype(jnp.bfloat16)
    dkv = jnp.concatenate([front, dkv[:, half:]], axis=1)
    dkv = jnp.where(team == 0, dkv, jnp.roll(dkv, XN, axis=0))
    dkv = lax.all_to_all(dkv, "head", 0, 0, tiled=True)
    dkv = dkv[:XN].astype(jnp.float32) + dkv[XN:].astype(jnp.float32)
    dkv = dkv.astype(jnp.bfloat16).transpose(1, 0, 2)
    lines = KV * HD
    grad_queries = dq.transpose(1, 0, 2).reshape(queries.shape)
    grad_keys = dkv[:, :, :lines].reshape(keys.shape)
    grad_values = dkv[:, :, lines:].reshape(values.shape)
    return (grad_queries, grad_keys, grad_values)


def solution(mesh):
    rows = P(("head", "blk"), None)
    return jax.shard_map(
        body,
        mesh=mesh,
        in_specs=(rows, rows, rows, rows, P()),
        out_specs=(rows, rows, rows),
        check_vma=False,
    )
```

time: 357 us -> 97 us (0.27)
  the two profiles are of different devices: /device:TPU:16 before, /device:TPU:8 now
where the time goes in v1:
time: 97 us; the launch traced here: 96.5 us
  waiting for transfers between devices  42 us (43%)
  starting transfers between devices  39.9 us (41%)
  Pallas kernels  6.64 us (7%)
  local copies, waits for them, and re-layouts  4 us (4%)
  other arithmetic  3.19 us (3%)
    all_to_all x1, waiting for transfers between devices, body(): dkv = lax.all_to_all(dkv, 'head', 0, 0, tiled=True)  15.9 us
    ppermute x1, waiting for transfers between devices, body(): pfar = lax.ppermute(own[:, :half], ('head', 'blk'), across_ahead)  13.6 us
    all_to_all x3, waiting for transfers between devices, team_exchange(): lax.all_to_all(array, 'head', 0, 0, tiled=True, axis_index_groups=teams)  12.5 us
    all_to_all x3, starting transfers between devices, team_exchange(): lax.all_to_all(array, 'head', 0, 0, tiled=True, axis_index_groups=teams)  11.7 us
    all_to_all x1, starting transfers between devices, body(): dkv = lax.all_to_all(dkv, 'head', 0, 0, tiled=True)  9.4 us
    ppermute x1, starting transfers between devices, body(): far = lax.ppermute(own, 'head', across)  6.83 us
    pallas_call x1, Pallas kernels, attention(): pl.pallas_call(attention_kernel, out_shape=(jax.ShapeDtypeStruct((slots,...  6.64 us
    ppermute x1, starting transfers between devices, body(): back = lax.ppermute(dprev, 'blk', behind)  5.17 us
  transfers between devices with their start and end apart: 8, of which 4 were waited for; matrix products, arithmetic and copies ran while one was open for 4% of the time, Pallas kernels for 0%

profile of v1, /device:TPU:8, one launch (start us, length us, event | category | flops | bytes accessed | tf_op | source)
XLA Modules:
  0.0 96.5 jit_solution(13574596867369746250)
XLA Ops:
  0.6 0.0 copy-start
  0.6 0.0 copy-start.1
  0.7 1.1 %copy_bitcast_fusion.2 = (bf16[64,4,256]{2,0,1:T(8,128)(2,1)S(1)}, bf16[64,4,256]{2,0,1:T(8,128)(2,1)S(1)}) fusion(bf16[8,4,8,256]{3,2,1,0:T(8,128)(2,1)} %bitcast.35, bf16[8,4,8,256]{3,2,1,0:T(8,128)(2,1)} %bitcast.36), kind=kLoop, calls=%fused_computation.15 | loop fusion | bytes 524288 | tf_op jit(solution)/shard_map/reshape | solution.py:144
  1.7 0.7 maximum_bitcast_fusion.1
  2.5 4.3 %all-to-all-start.1 = ((bf16[4,64,512]{2,1,0:T(8,128)(2,1)}), bf16[4,64,512]{2,1,0:T(8,128)(2,1)S(1)}, u32[]{:S(2)}, u32[]{:S(2)}) async-start(bf16[4,64,512]{2,1,0:T(8,128)(2,1)} %maximum_bitcast_fusion.1), calls=%async_computation.1 | async-start | bytes 524288 | tf_op jit(solution)/shard_map/all_to_all | solution.py:141
  6.7 0.0 copy-done
  6.7 0.0 copy-done.1
  6.7 0.1 copy_bitcast_fusion
  6.8 1.1 %maximum_bitcast_fusion = bf16[4,64,2048]{2,1,0:T(8,128)(2,1)} fusion(bf16[64,4,1024]{2,0,1:T(8,128)(2,1)S(1)} %get-tuple-element.19, bf16[64,4,1024]{2,0,1:T(8,128)(2,1)S(1)} %get-tuple-element.20), kind=kLoop, calls=%fused_computation | loop fusion | flops 2097152 | bytes 2097152 | tf_op jit(solution)/shard_map/transpose | solution.py:145
  7.9 0.0 copy-start.2
  7.9 5.5 %all-to-all-done.1.own_ref = bf16[4,64,512]{2,1,0:T(8,128)(2,1)S(1)} async-done(((bf16[4,64,512]{2,1,0:T(8,128)(2,1)}), bf16[4,64,512]{2,1,0:T(8,128)(2,1)S(1)}, u32[]{:S(2)}, u32[]{:S(2)}) %all-to-all-start.1) | async-done | bytes 262176 | tf_op jit(solution)/shard_map/all_to_all | solution.py:141
  13.4 3.5 %all-to-all-start = ((bf16[4,64,2048]{2,1,0:T(8,128)(2,1)}), bf16[4,64,2048]{2,1,0:T(8,128)(2,1)S(1)}, u32[]{:S(2)}, u32[]{:S(2)}) async-start(bf16[4,64,2048]{2,1,0:T(8,128)(2,1)} %maximum_bitcast_fusion), calls=%async_computation | async-start | bytes 2097152 | tf_op jit(solution)/shard_map/all_to_all | solution.py:141
  16.9 0.0 copy-done.2
  17.0 0.1 reshape.94
  17.0 0.1 constant_dynamic-slice_fusion
  17.1 0.2 multiply_reduce_fusion.1
  17.3 6.8 %collective-permute-start = (bf16[4,64,512]{2,1,0:T(8,128)(2,1)S(1)}, bf16[4,64,512]{2,1,0:T(8,128)(2,1)S(1)}, u32[]{:S(2)}, u32[]{:S(2)}) collective-permute-start(bf16[4,64,512]{2,1,0:T(8,128)(2,1)S(1)} %all-to-all-done.1.own_ref), channel_id=1, source_target_pairs={{0,256},{64,320},{128,384},{192,448},{256,0},{320,64},{384,128},{4... | collective-permute-start | bytes 786440 | tf_op jit(solution)/shard_map/ppermute | solution.py:148
  24.1 0.1 iota_add_fusion
  24.2 0.1 add.71
  24.3 0.1 add.70
  24.4 1.9 %collective-permute-start.2 = (bf16[4,32,512]{2,1,0:T(8,128)(2,1)S(1)}, bf16[4,32,512]{2,1,0:T(8,128)(2,1)S(1)}, u32[]{:S(2)}, u32[]{:S(2)}) collective-permute-start(bf16[4,32,512]{2,1,0:T(8,128)(2,1)S(1)} %slice.61), channel_id=1, source_target_pairs={{0,257},{1,258},{2,259},{3,260},{4,261},{5,262},{6,263},{7,264},{8... | collective-permute-start | bytes 393224 | tf_op jit(solution)/shard_map/ppermute | solution.py:150
  26.3 4.8 %collective-permute-start.1 = (bf16[4,32,512]{2,1,0:T(8,128)(2,1)S(1)}, bf16[4,32,512]{2,1,0:T(8,128)(2,1)S(1)}, u32[]{:S(2)}, u32[]{:S(2)}) collective-permute-start(bf16[4,32,512]{2,1,0:T(8,128)(2,1)S(1)} %slice.61), channel_id=1, source_target_pairs={{0,1},{1,2},{2,3},{3,4},{4,5},{5,6},{6,7},{7,8},{8,9},{9,10},{10,1... | collective-permute-start | bytes 393224 | tf_op jit(solution)/shard_map/ppermute | solution.py:149
  31.2 0.1 tile.18
  31.3 0.1 tile.16
  31.4 0.1 copy.41.kpos_ref
  31.5 13.6 %collective-permute-done.2.pfar_ref = bf16[4,32,512]{2,1,0:T(8,128)(2,1)S(1)} collective-permute-done((bf16[4,32,512]{2,1,0:T(8,128)(2,1)S(1)}, bf16[4,32,512]{2,1,0:T(8,128)(2,1)S(1)}, u32[]{:S(2)}, u32[]{:S(2)}) %collective-permute-start.2) | collective-permute-done | bytes 131104 | tf_op jit(solution)/shard_map/ppermute | solution.py:150
  45.1 0.0 collective-permute-done.1.pown_ref
  45.1 0.0 collective-permute-done.far_ref
  45.1 0.0 all-to-all-done.qg_ref
  45.1 6.6 %shard_map.76 = (bf16[4,64,1024]{2,1,0:T(8,128)(2,1)}, bf16[8,64,512]{2,1,0:T(8,128)(2,1)S(1)}, bf16[8,32,512]{2,1,0:T(8,128)(2,1)S(1)}) custom-call(s32[2,256]{1,0:T(2,128)S(1)} %pad_add_fusion.qpos_ref, s32[256,2]{1,0:T(8,128)S(1)} %copy.41.kpos_ref, bf16[4,64,2048]{2,1,0:T(8,128)(2,1)S(1)} %all-to-all-done.qg_ref, ...), custom_call_target="tpu_custom_call" | custom-call | tf_op jit(solution)/shard_map/pallas_call | solution.py:112
  51.8 5.2 %collective-permute-start.3 = (bf16[8,32,512]{2,1,0:T(8,128)(2,1)S(1)}, bf16[8,32,512]{2,1,0:T(8,128)(2,1)S(1)}, u32[]{:S(2)}, u32[]{:S(2)}) collective-permute-start(bf16[8,32,512]{2,1,0:T(8,128)(2,1)S(1)} %get-tuple-element.8), channel_id=1, source_target_pairs={{1,0},{2,1},{3,2},{4,3},{5,4},{6,5},{7,6},{8,7},{9,8},{10,9},{11,1... | collective-permute-start | bytes 786440 | tf_op jit(solution)/shard_map/ppermute | solution.py:164
  57.0 3.9 %all-to-all-start.2 = ((bf16[4,64,1024]{2,1,0:T(8,128)(2,1)}), bf16[4,64,1024]{2,1,0:T(8,128)(2,1)S(1)}, u32[]{:S(2)}, u32[]{:S(2)}) async-start(bf16[4,64,1024]{2,1,0:T(8,128)(2,1)} %get-tuple-element.6), calls=%async_computation.2 | async-start | bytes 1048576 | tf_op jit(solution)/shard_map/all_to_all | solution.py:141
  60.9 0.0 collective-permute-done.3
  60.9 0.1 add_convert_fusion.1
  61.0 0.9 fusion
  62.0 7.0 %all-to-all-done.2 = bf16[4,64,1024]{2,1,0:T(8,128)(2,1)S(1)} async-done(((bf16[4,64,1024]{2,1,0:T(8,128)(2,1)}), bf16[4,64,1024]{2,1,0:T(8,128)(2,1)S(1)}, u32[]{:S(2)}, u32[]{:S(2)}) %all-to-all-start.2) | async-done | bytes 524320 | tf_op jit(solution)/shard_map/all_to_all | solution.py:141
  69.0 9.4 %all-to-all-start.3 = ((bf16[8,64,512]{2,1,0:T(8,128)(2,1)}), bf16[8,64,512]{2,1,0:T(8,128)(2,1)S(1)}, u32[]{:S(2)}, u32[]{:S(2)}) async-start(bf16[8,64,512]{2,1,0:T(8,128)(2,1)} %fusion), calls=%async_computation.3 | async-start | bytes 1048576 | tf_op jit(solution)/shard_map/all_to_all | solution.py:169
  78.4 0.8 copy.49
  79.2 15.9 %all-to-all-done.3 = bf16[8,64,512]{2,1,0:T(8,128)(2,1)S(1)} async-done(((bf16[8,64,512]{2,1,0:T(8,128)(2,1)}), bf16[8,64,512]{2,1,0:T(8,128)(2,1)S(1)}, u32[]{:S(2)}, u32[]{:S(2)}) %all-to-all-start.3) | async-done | bytes 524320 | tf_op jit(solution)/shard_map/all_to_all | solution.py:169
  95.1 0.1 fusion.1
  95.2 0.7 copy.51
  95.8 0.7 copy.50
  (11 shorter events, 0.1 us)
Async XLA Ops:
  0.6 6.1 %copy-start = (bf16[64,4096]{1,0:T(8,128)(2,1)S(1)}, bf16[64,4096]{1,0:T(8,128)(2,1)}, u32[]{:S(2)}) copy-start(bf16[64,4096]{1,0:T(8,128)(2,1)} %param.8) | copy-start | bytes 1572868
  0.6 6.1 %copy-start.1 = (bf16[64,4096]{1,0:T(8,128)(2,1)S(1)}, bf16[64,4096]{1,0:T(8,128)(2,1)}, u32[]{:S(2)}) copy-start(bf16[64,4096]{1,0:T(8,128)(2,1)} %param.5) | copy-start | bytes 1572868
  2.5 11.0 %all-to-all-start.1 = ((bf16[4,64,512]{2,1,0:T(8,128)(2,1)}), bf16[4,64,512]{2,1,0:T(8,128)(2,1)S(1)}, u32[]{:S(2)}, u32[]{:S(2)}) async-start(bf16[4,64,512]{2,1,0:T(8,128)(2,1)} %maximum_bitcast_fusion.1), calls=%async_computation.1 | async-start | bytes 524288 | tf_op jit(solution)/shard_map/all_to_all | solution.py:141
  7.9 9.0 %copy-start.2 = (s32[512]{0:T(512)S(1)}, s32[512]{0:T(512)}, u32[]{:S(2)}) copy-start(s32[512]{0:T(512)} %param.9) | copy-start | bytes 6148
  13.4 31.7 %all-to-all-start = ((bf16[4,64,2048]{2,1,0:T(8,128)(2,1)}), bf16[4,64,2048]{2,1,0:T(8,128)(2,1)S(1)}, u32[]{:S(2)}, u32[]{:S(2)}) async-start(bf16[4,64,2048]{2,1,0:T(8,128)(2,1)} %maximum_bitcast_fusion), calls=%async_computation | async-start | bytes 2097152 | tf_op jit(solution)/shard_map/all_to_all | solution.py:141
  17.3 27.8 %collective-permute-start = (bf16[4,64,512]{2,1,0:T(8,128)(2,1)S(1)}, bf16[4,64,512]{2,1,0:T(8,128)(2,1)S(1)}, u32[]{:S(2)}, u32[]{:S(2)}) collective-permute-start(bf16[4,64,512]{2,1,0:T(8,128)(2,1)S(1)} %all-to-all-done.1.own_ref), channel_id=1, source_target_pairs={{0,256},{64,320},{128,384},{192,448},{256,0},{320,64},{384,128},{4... | collective-permute-start | bytes 786440 | tf_op jit(solution)/shard_map/ppermute | solution.py:148
  24.4 20.7 %collective-permute-start.2 = (bf16[4,32,512]{2,1,0:T(8,128)(2,1)S(1)}, bf16[4,32,512]{2,1,0:T(8,128)(2,1)S(1)}, u32[]{:S(2)}, u32[]{:S(2)}) collective-permute-start(bf16[4,32,512]{2,1,0:T(8,128)(2,1)S(1)} %slice.61), channel_id=1, source_target_pairs={{0,257},{1,258},{2,259},{3,260},{4,261},{5,262},{6,263},{7,264},{8... | collective-permute-start | bytes 393224 | tf_op jit(solution)/shard_map/ppermute | solution.py:150
  26.3 18.8 %collective-permute-start.1 = (bf16[4,32,512]{2,1,0:T(8,128)(2,1)S(1)}, bf16[4,32,512]{2,1,0:T(8,128)(2,1)S(1)}, u32[]{:S(2)}, u32[]{:S(2)}) collective-permute-start(bf16[4,32,512]{2,1,0:T(8,128)(2,1)S(1)} %slice.61), channel_id=1, source_target_pairs={{0,1},{1,2},{2,3},{3,4},{4,5},{5,6},{6,7},{7,8},{8,9},{9,10},{10,1... | collective-permute-start | bytes 393224 | tf_op jit(solution)/shard_map/ppermute | solution.py:149
  51.8 9.1 %collective-permute-start.3 = (bf16[8,32,512]{2,1,0:T(8,128)(2,1)S(1)}, bf16[8,32,512]{2,1,0:T(8,128)(2,1)S(1)}, u32[]{:S(2)}, u32[]{:S(2)}) collective-permute-start(bf16[8,32,512]{2,1,0:T(8,128)(2,1)S(1)} %get-tuple-element.8), channel_id=1, source_target_pairs={{1,0},{2,1},{3,2},{4,3},{5,4},{6,5},{7,6},{8,7},{9,8},{10,9},{11,1... | collective-permute-start | bytes 786440 | tf_op jit(solution)/shard_map/ppermute | solution.py:164
  57.0 12.0 %all-to-all-start.2 = ((bf16[4,64,1024]{2,1,0:T(8,128)(2,1)}), bf16[4,64,1024]{2,1,0:T(8,128)(2,1)S(1)}, u32[]{:S(2)}, u32[]{:S(2)}) async-start(bf16[4,64,1024]{2,1,0:T(8,128)(2,1)} %get-tuple-element.6), calls=%async_computation.2 | async-start | bytes 1048576 | tf_op jit(solution)/shard_map/all_to_all | solution.py:141
  69.0 26.1 %all-to-all-start.3 = ((bf16[8,64,512]{2,1,0:T(8,128)(2,1)}), bf16[8,64,512]{2,1,0:T(8,128)(2,1)S(1)}, u32[]{:S(2)}, u32[]{:S(2)}) async-start(bf16[8,64,512]{2,1,0:T(8,128)(2,1)} %fusion), calls=%async_computation.3 | async-start | bytes 1048576 | tf_op jit(solution)/shard_map/all_to_all | solution.py:169

commit v2 on v1

--- a/solution.py
+++ b/solution.py
@@ -19,9 +19,7 @@
     )
 
 
-def attention_kernel(
-    qpos_ref, kpos_ref, qg_ref, own_ref, far_ref, pown_ref, pfar_ref, dq_ref, dkv_ref, dprev_ref
-):
+def attention_kernel(qpos_ref, kpos_ref, qg_ref, kv_ref, dq_ref, dkv_ref):
     half = qg_ref.shape[1] // 2
     slots = qg_ref.shape[0]
     rows = slots * half
@@ -30,6 +28,7 @@
     qpos = qpos_ref[...]
     kpos = kpos_ref[...]
     keys = kpos.shape[0]
+    places = [0, 2 * half, half, 3 * half, 4 * half, 5 * half]
     early_seen = kpos[:, 0:1] <= qpos[0:1, :]
     late_seen = kpos[:, 1:2] <= qpos[1:2, :]
 
@@ -67,10 +66,9 @@
     for kv in range(KV):
         parts = []
         for column in (kv * HD, (KV + kv) * HD):
-            early = [columns(ref, 0, half, column) for ref in (own_ref, far_ref)]
-            late = [columns(ref, half, 2 * half, column) for ref in (own_ref, far_ref)]
-            before = [columns(ref, 0, half, column) for ref in (pown_ref, pfar_ref)]
-            parts.append(jnp.concatenate(early + late + before, axis=0))
+            parts.append(
+                jnp.concatenate([columns(kv_ref, r, r + half, column) for r in places], axis=0)
+            )
         key, value = parts
         key_sum = None
         value_sum = None
@@ -99,25 +97,77 @@
             value_sum = dv if value_sum is None else value_sum + dv
         for total, column in ((key_sum, kv * HD), (value_sum, (KV + kv) * HD)):
             low = total.astype(jnp.bfloat16)
-            for kind in range(2):
-                dkv_ref[:, kind * half : (kind + 1) * half, column : column + HD] = low[
-                    kind * keys : (kind + 1) * keys
-                ].reshape(2 * slots, half, HD)
-            dprev_ref[:, :, column : column + HD] = low[2 * keys :].reshape(2 * slots, half, HD)
-
-
-def attention(qpos, kpos, qg, own, far, pown, pfar):
+            for i, r in enumerate(places):
+                dkv_ref[:, r : r + half, column : column + HD] = low[
+                    i * rows : (i + 1) * rows
+                ].reshape(slots, half, HD)
+
+
+def attention(qpos, kpos, qg, kv):
     slots, tok, _ = qg.shape
-    lines = own.shape[2]
     return pl.pallas_call(
         attention_kernel,
         out_shape=(
             jax.ShapeDtypeStruct((slots, tok, KV * GROUP * HD), jnp.bfloat16),
-            jax.ShapeDtypeStruct((2 * slots, tok, lines), jnp.bfloat16),
-            jax.ShapeDtypeStruct((2 * slots, tok // 2, lines), jnp.bfloat16),
+            jax.ShapeDtypeStruct(kv.shape, jnp.bfloat16),
         ),
         compiler_params=pltpu.CompilerParams(vmem_limit_bytes=48 * 1024 * 1024),
-    )(qpos, kpos, qg, own, far, pown, pfar)
+    )(qpos, kpos, qg, kv)
+
+
+def pack_kernel(query_ref, key_ref, value_ref, grad_ref, qg_ref, own_ref, early_ref):
+    half = early_ref.shape[1]
+    for x in range(XN):
+        for refs, out in (((query_ref, grad_ref), qg_ref), ((key_ref, value_ref), own_ref)):
+            wide = out.shape[2] // 2
+            for i, ref in enumerate(refs):
+                block = ref[:, x * wide : (x + 1) * wide]
+                out[x, :, i * wide : (i + 1) * wide] = block
+                if out is own_ref:
+                    early_ref[x, :, i * wide : (i + 1) * wide] = block[:half]
+
+
+def pack(queries, keys, values, grad_out):
+    tok = queries.shape[0]
+    wide = 2 * queries.shape[1] // XN
+    lines = 2 * keys.shape[1] // XN
+    return pl.pallas_call(
+        pack_kernel,
+        out_shape=(
+            jax.ShapeDtypeStruct((XN, tok, wide), queries.dtype),
+            jax.ShapeDtypeStruct((XN, tok, lines), keys.dtype),
+            jax.ShapeDtypeStruct((XN, tok // 2, lines), keys.dtype),
+        ),
+        compiler_params=pltpu.CompilerParams(vmem_limit_bytes=16 * 1024 * 1024),
+    )(queries, keys, values, grad_out)
+
+
+def unpack_kernel(dq_ref, own_ref, far_ref, pown_ref, pfar_ref, query_ref, key_ref, value_ref):
+    tok = far_ref.shape[1]
+    half = tok // 2
+    wide = dq_ref.shape[2]
+    lines = KV * HD
+    for x in range(XN):
+        query_ref[:, x * wide : (x + 1) * wide] = dq_ref[x]
+        for i, ref in enumerate((key_ref, value_ref)):
+            source = slice(i * lines, (i + 1) * lines)
+            target = slice(x * lines, (x + 1) * lines)
+            total = own_ref[x, :tok, source].astype(jnp.float32)
+            total = total + far_ref[x, :, source].astype(jnp.float32)
+            before = pown_ref[x, :, source].astype(jnp.float32)
+            before = before + pfar_ref[x, :, source].astype(jnp.float32)
+            ref[:half, target] = (total[:half] + before).astype(ref.dtype)
+            ref[half:, target] = total[half:].astype(ref.dtype)
+
+
+def unpack(dq, own, far, pown, pfar):
+    tok = dq.shape[1]
+    shapes = [(tok, XN * dq.shape[2])] + [(tok, XN * KV * HD)] * 2
+    return pl.pallas_call(
+        unpack_kernel,
+        out_shape=tuple(jax.ShapeDtypeStruct(shape, jnp.bfloat16) for shape in shapes),
+        compiler_params=pltpu.CompilerParams(vmem_limit_bytes=16 * 1024 * 1024),
+    )(dq, own, far, pown, pfar)
 
 
 def body(queries, keys, values, grad_out, order):
@@ -137,18 +187,17 @@
         for b in range(cycle)
     ]
 
+    across_behind = [(j, i) for i, j in across_ahead]
+
     def team_exchange(array):
         return lax.all_to_all(array, "head", 0, 0, tiled=True, axis_index_groups=teams)
 
-    def packed(first, second):
-        blocks = [a.reshape(tok, XN, a.shape[1] // XN) for a in (first, second)]
-        return jnp.concatenate(blocks, axis=2).transpose(1, 0, 2)
-
-    own = team_exchange(packed(keys, values))
+    qg, own, early_rows = pack(queries, keys, values, grad_out)
     far = lax.ppermute(own, "head", across)
-    pown = lax.ppermute(own[:, :half], "blk", ahead)
-    pfar = lax.ppermute(own[:, :half], ("head", "blk"), across_ahead)
-    qg = team_exchange(packed(queries, grad_out))
+    pown = lax.ppermute(early_rows, "blk", ahead)
+    pfar = lax.ppermute(early_rows, ("head", "blk"), across_ahead)
+    qg = team_exchange(qg)
+    kv = team_exchange(jnp.concatenate([own, far, pown, pfar], axis=1))
 
     team = lax.axis_index("head") // XN
     places = lax.dynamic_index_in_dim(order.reshape(groups, cycle), mine, axis=1, keepdims=False)
@@ -159,21 +208,15 @@
     kpos = jnp.stack([early, late], axis=1)
     qpos = jnp.stack([jnp.tile(p[: XN * half], 2) for p in (early, late)], axis=0)
 
-    dq, dkv, dprev = attention(qpos, kpos, qg, own, far, pown, pfar)
-
-    back = lax.ppermute(dprev, "blk", behind)
+    dq, dkv = attention(qpos, kpos, qg, kv)
+
+    dkv = team_exchange(dkv)
+    dq, dkv = lax.optimization_barrier((dq, dkv))
+    far = lax.ppermute(dkv[:, tok : 2 * tok], "head", across)
+    pown = lax.ppermute(dkv[:, 2 * tok : 2 * tok + half], "blk", behind)
+    pfar = lax.ppermute(dkv[:, 2 * tok + half :], ("head", "blk"), across_behind)
     dq = team_exchange(dq)
-    front = (dkv[:, :half].astype(jnp.float32) + back.astype(jnp.float32)).astype(jnp.bfloat16)
-    dkv = jnp.concatenate([front, dkv[:, half:]], axis=1)
-    dkv = jnp.where(team == 0, dkv, jnp.roll(dkv, XN, axis=0))
-    dkv = lax.all_to_all(dkv, "head", 0, 0, tiled=True)
-    dkv = dkv[:XN].astype(jnp.float32) + dkv[XN:].astype(jnp.float32)
-    dkv = dkv.astype(jnp.bfloat16).transpose(1, 0, 2)
-    lines = KV * HD
-    grad_queries = dq.transpose(1, 0, 2).reshape(queries.shape)
-    grad_keys = dkv[:, :, :lines].reshape(keys.shape)
-    grad_values = dkv[:, :, lines:].reshape(values.shape)
-    return (grad_queries, grad_keys, grad_values)
+    return unpack(dq, dkv, far, pown, pfar)
 
 
 def solution(mesh):

time: 97 us -> 106 us (1.093)
  the two profiles are of different devices: /device:TPU:8 before, /device:TPU:251 now
where the time goes in v2:
time: 106 us; the launch traced here: 105 us
  starting transfers between devices  42.1 us (40%)
  waiting for transfers between devices  34.1 us (32%)
  blocking collectives  13.9 us (13%)
  Pallas kernels  8.53 us (8%)
  local copies, waits for them, and re-layouts  4.55 us (4%)
  other arithmetic  1.26 us (1%)
    ppermute x1, waiting for transfers between devices, body(): pfar = lax.ppermute(dkv[:, 2 * tok + half:], ('head', 'blk'), across_behind)  14 us
    all_to_all x1, blocking collectives, team_exchange(): lax.all_to_all(array, 'head', 0, 0, tiled=True, axis_index_groups=teams)  13.9 us
    all_to_all x3, starting transfers between devices, team_exchange(): lax.all_to_all(array, 'head', 0, 0, tiled=True, axis_index_groups=teams)  13.3 us
    all_to_all x3, waiting for transfers between devices, team_exchange(): lax.all_to_all(array, 'head', 0, 0, tiled=True, axis_index_groups=teams)  10.7 us
    ppermute x1, waiting for transfers between devices, body(): pfar = lax.ppermute(early_rows, ('head', 'blk'), across_ahead)  9.38 us
    ppermute x1, starting transfers between devices, body(): pfar = lax.ppermute(early_rows, ('head', 'blk'), across_ahead)  9.18 us
    ppermute x1, starting transfers between devices, body(): pfar = lax.ppermute(dkv[:, 2 * tok + half:], ('head', 'blk'), across_behind)  7.91 us
    pallas_call x1, Pallas kernels, attention(): pl.pallas_call(attention_kernel, out_shape=(jax.ShapeDtypeStruct((slots,...  6.51 us
  transfers between devices with their start and end apart: 9, of which 3 were waited for; matrix products, arithmetic and copies ran while one was open for 2% of the time, Pallas kernels for 0%

profile of v2, /device:TPU:251, one launch (start us, length us, event | category | flops | bytes accessed | tf_op | source)
XLA Modules:
  0.0 105.2 jit_solution(15892533496741179567)
XLA Ops:
  0.6 0.0 copy-start
  0.6 1.0 copy-done
  1.7 0.0 copy-start.1
  1.7 1.0 copy-done.1
  2.7 0.0 copy-start.2
  2.7 0.9 copy-done.2
  3.6 0.0 copy-start.3
  3.6 0.9 copy-done.3
  4.5 1.1 %shard_map.76 = (bf16[4,64,2048]{2,1,0:T(8,128)(2,1)}, bf16[4,64,512]{2,1,0:T(8,128)(2,1)S(1)}, bf16[4,32,512]{2,1,0:T(8,128)(2,1)S(1)}) custom-call(bf16[64,4096]{1,0:T(8,128)(2,1)S(1)} %copy-done, bf16[64,1024]{1,0:T(8,128)(2,1)S(1)} %copy-done.2, bf16[64,1024]{1,0:T(8,128)(2,1)S(1)} %copy-done.3, bf16[64,4096]{1,0:T(8,128)(2,1)S(1)} %copy-done.1), custom_call_target="tpu_custom_call" | custom-call | tf_op jit(solution)/shard_map/pallas_call | solution.py:134
  5.6 0.0 copy-start.4
  5.6 4.4 %all-to-all-start = ((bf16[4,64,2048]{2,1,0:T(8,128)(2,1)}), bf16[4,64,2048]{2,1,0:T(8,128)(2,1)S(1)}, u32[]{:S(2)}, u32[]{:S(2)}) async-start(bf16[4,64,2048]{2,1,0:T(8,128)(2,1)} %get-tuple-element.10), calls=%async_computation | async-start | bytes 2097152 | tf_op jit(solution)/shard_map/all_to_all | solution.py:193
  10.0 4.4 %collective-permute-start = (bf16[4,64,512]{2,1,0:T(8,128)(2,1)S(1)}, bf16[4,64,512]{2,1,0:T(8,128)(2,1)S(1)}, u32[]{:S(2)}, u32[]{:S(2)}) collective-permute-start(bf16[4,64,512]{2,1,0:T(8,128)(2,1)S(1)} %get-tuple-element.11), channel_id=1, source_target_pairs={{0,256},{64,320},{128,384},{192,448},{256,0},{320,64},{384,128},{4... | collective-permute-start | bytes 786440 | tf_op jit(solution)/shard_map/ppermute | solution.py:196
  14.4 9.2 %collective-permute-start.2 = (bf16[4,32,512]{2,1,0:T(8,128)(2,1)S(1)}, bf16[4,32,512]{2,1,0:T(8,128)(2,1)S(1)}, u32[]{:S(2)}, u32[]{:S(2)}) collective-permute-start(bf16[4,32,512]{2,1,0:T(8,128)(2,1)S(1)} %get-tuple-element.12), channel_id=1, source_target_pairs={{0,257},{1,258},{2,259},{3,260},{4,261},{5,262},{6,263},{7,264},{8... | collective-permute-start | bytes 393224 | tf_op jit(solution)/shard_map/ppermute | solution.py:198
  23.6 1.9 %collective-permute-start.1 = (bf16[4,32,512]{2,1,0:T(8,128)(2,1)S(1)}, bf16[4,32,512]{2,1,0:T(8,128)(2,1)S(1)}, u32[]{:S(2)}, u32[]{:S(2)}) collective-permute-start(bf16[4,32,512]{2,1,0:T(8,128)(2,1)S(1)} %get-tuple-element.12), channel_id=1, source_target_pairs={{0,1},{1,2},{2,3},{3,4},{4,5},{5,6},{6,7},{7,8},{8,9},{9,10},{10,1... | collective-permute-start | bytes 393224 | tf_op jit(solution)/shard_map/ppermute | solution.py:197
  25.6 0.0 copy-done.4
  25.6 0.1 reshape.73
  25.7 0.1 constant_dynamic-slice_fusion
  25.7 9.4 %collective-permute-done.2 = bf16[4,32,512]{2,1,0:T(8,128)(2,1)S(1)} collective-permute-done((bf16[4,32,512]{2,1,0:T(8,128)(2,1)S(1)}, bf16[4,32,512]{2,1,0:T(8,128)(2,1)S(1)}, u32[]{:S(2)}, u32[]{:S(2)}) %collective-permute-start.2) | collective-permute-done | bytes 131104 | tf_op jit(solution)/shard_map/ppermute | solution.py:198
  35.1 0.0 collective-permute-done.1
  35.1 0.0 collective-permute-done
  35.1 1.0 pad_maximum_fusion
  36.1 0.0 all-to-all-done.qg_ref
  36.1 4.2 %all-to-all-start.1 = ((bf16[4,192,512]{2,1,0:T(8,128)(2,1)}), bf16[4,192,512]{2,1,0:T(8,128)(2,1)S(1)}, u32[]{:S(2)}, u32[]{:S(2)}) async-start(bf16[4,192,512]{2,1,0:T(8,128)(2,1)} %pad_maximum_fusion), calls=%async_computation.1 | async-start | bytes 1572864 | tf_op jit(solution)/shard_map/all_to_all | solution.py:193
  40.3 0.2 multiply_reduce_fusion.1
  40.5 0.1 iota_add_fusion
  40.6 0.1 add.65
  40.7 0.1 add.64
  40.8 0.1 tile.18
  40.8 0.1 tile.16
  40.9 0.1 copy.16.kpos_ref
  41.1 10.7 %all-to-all-done.1.kv_ref = bf16[4,192,512]{2,1,0:T(8,128)(2,1)S(1)} async-done(((bf16[4,192,512]{2,1,0:T(8,128)(2,1)}), bf16[4,192,512]{2,1,0:T(8,128)(2,1)S(1)}, u32[]{:S(2)}, u32[]{:S(2)}) %all-to-all-start.1) | async-done | bytes 786464 | tf_op jit(solution)/shard_map/all_to_all | solution.py:193
  51.8 6.5 %shard_map.77 = (bf16[4,64,1024]{2,1,0:T(8,128)(2,1)}, bf16[4,192,512]{2,1,0:T(8,128)(2,1)S(1)}) custom-call(s32[2,256]{1,0:T(2,128)S(1)} %pad_add_fusion.qpos_ref, s32[256,2]{1,0:T(8,128)S(1)} %copy.16.kpos_ref, bf16[4,64,2048]{2,1,0:T(8,128)(2,1)S(1)} %all-to-all-done.qg_ref, bf16[4,192,512]{2,1,0:T(8,128)(2,1)S(1)} %all-to-all-done.1.kv_ref), custom_call_target="tpu_custom_call" | custom-call | tf_op jit(solution)/shard_map/pallas_call | solution.py:108
  58.3 13.9 %all_to_all.20.own_ref = bf16[4,192,512]{2,1,0:T(8,128)(2,1)S(1)} all-to-all(bf16[4,192,512]{2,1,0:T(8,128)(2,1)S(1)} %get-tuple-element.14), channel_id=1, replica_groups={{0,64,128,192},{256,320,384,448},{1,65,129,193},{257,321,385,449},{2,66..., dimensions={0} | all-to-all | bytes 1572864 | tf_op jit(solution)/shard_map/all_to_all | solution.py:193
  72.2 4.6 %all-to-all-start.3 = ((bf16[4,64,1024]{2,1,0:T(8,128)(2,1)}), bf16[4,64,1024]{2,1,0:T(8,128)(2,1)S(1)}, u32[]{:S(2)}, u32[]{:S(2)}) async-start(bf16[4,64,1024]{2,1,0:T(8,128)(2,1)} %get-tuple-element.15), calls=%async_computation.3 | async-start | bytes 1048576 | tf_op jit(solution)/shard_map/all_to_all | solution.py:193
  76.8 3.5 %collective-permute-start.3 = (bf16[4,64,512]{2,1,0:T(8,128)(2,1)S(1)}, bf16[4,64,512]{2,1,0:T(8,128)(2,1)S(1)}, u32[]{:S(2)}, u32[]{:S(2)}) collective-permute-start(bf16[4,64,512]{2,1,0:T(8,128)(2,1)S(1)} %slice.31), channel_id=1, source_target_pairs={{0,256},{64,320},{128,384},{192,448},{256,0},{320,64},{384,128},{4... | collective-permute-start | bytes 786440 | tf_op jit(solution)/shard_map/ppermute | solution.py:215
  80.4 7.9 %collective-permute-start.5 = (bf16[4,32,512]{2,1,0:T(8,128)(2,1)S(1)}, bf16[4,32,512]{2,1,0:T(8,128)(2,1)S(1)}, u32[]{:S(2)}, u32[]{:S(2)}) collective-permute-start(bf16[4,32,512]{2,1,0:T(8,128)(2,1)S(1)} %get-tuple-element.19), channel_id=1, source_target_pairs={{257,0},{258,1},{259,2},{260,3},{261,4},{262,5},{263,6},{264,7},{2... | collective-permute-start | bytes 393224 | tf_op jit(solution)/shard_map/ppermute | solution.py:217
  88.3 1.9 %collective-permute-start.4 = (bf16[4,32,512]{2,1,0:T(8,128)(2,1)S(1)}, bf16[4,32,512]{2,1,0:T(8,128)(2,1)S(1)}, u32[]{:S(2)}, u32[]{:S(2)}) collective-permute-start(bf16[4,32,512]{2,1,0:T(8,128)(2,1)S(1)} %get-tuple-element.20), channel_id=1, source_target_pairs={{1,0},{2,1},{3,2},{4,3},{5,4},{6,5},{7,6},{8,7},{9,8},{10,9},{11,1... | collective-permute-start | bytes 393224 | tf_op jit(solution)/shard_map/ppermute | solution.py:216
  90.2 14.0 %collective-permute-done.5.pfar_ref = bf16[4,32,512]{2,1,0:T(8,128)(2,1)S(1)} collective-permute-done((bf16[4,32,512]{2,1,0:T(8,128)(2,1)S(1)}, bf16[4,32,512]{2,1,0:T(8,128)(2,1)S(1)}, u32[]{:S(2)}, u32[]{:S(2)}) %collective-permute-start.5) | collective-permute-done | bytes 131104 | tf_op jit(solution)/shard_map/ppermute | solution.py:217
  104.2 0.0 collective-permute-done.4.pown_ref
  104.2 0.0 collective-permute-done.3.far_ref
  104.2 0.0 all-to-all-done.3.dq_ref
  104.2 0.9 shard_map.78
  (9 shorter events, 0.1 us)
Async XLA Ops:
  0.6 1.0 copy-start
  1.7 1.0 copy-start.1
  2.7 0.9 copy-start.2
  3.6 0.9 copy-start.3
  5.6 20.0 %copy-start.4 = (s32[512]{0:T(512)S(1)}, s32[512]{0:T(512)}, u32[]{:S(2)}) copy-start(s32[512]{0:T(512)} %param.9) | copy-start | bytes 6148
  5.6 30.5 %all-to-all-start = ((bf16[4,64,2048]{2,1,0:T(8,128)(2,1)}), bf16[4,64,2048]{2,1,0:T(8,128)(2,1)S(1)}, u32[]{:S(2)}, u32[]{:S(2)}) async-start(bf16[4,64,2048]{2,1,0:T(8,128)(2,1)} %get-tuple-element.10), calls=%async_computation | async-start | bytes 2097152 | tf_op jit(solution)/shard_map/all_to_all | solution.py:193
  10.0 25.1 %collective-permute-start = (bf16[4,64,512]{2,1,0:T(8,128)(2,1)S(1)}, bf16[4,64,512]{2,1,0:T(8,128)(2,1)S(1)}, u32[]{:S(2)}, u32[]{:S(2)}) collective-permute-start(bf16[4,64,512]{2,1,0:T(8,128)(2,1)S(1)} %get-tuple-element.11), channel_id=1, source_target_pairs={{0,256},{64,320},{128,384},{192,448},{256,0},{320,64},{384,128},{4... | collective-permute-start | bytes 786440 | tf_op jit(solution)/shard_map/ppermute | solution.py:196
  14.4 20.7 %collective-permute-start.2 = (bf16[4,32,512]{2,1,0:T(8,128)(2,1)S(1)}, bf16[4,32,512]{2,1,0:T(8,128)(2,1)S(1)}, u32[]{:S(2)}, u32[]{:S(2)}) collective-permute-start(bf16[4,32,512]{2,1,0:T(8,128)(2,1)S(1)} %get-tuple-element.12), channel_id=1, source_target_pairs={{0,257},{1,258},{2,259},{3,260},{4,261},{5,262},{6,263},{7,264},{8... | collective-permute-start | bytes 393224 | tf_op jit(solution)/shard_map/ppermute | solution.py:198
  23.6 11.5 %collective-permute-start.1 = (bf16[4,32,512]{2,1,0:T(8,128)(2,1)S(1)}, bf16[4,32,512]{2,1,0:T(8,128)(2,1)S(1)}, u32[]{:S(2)}, u32[]{:S(2)}) collective-permute-start(bf16[4,32,512]{2,1,0:T(8,128)(2,1)S(1)} %get-tuple-element.12), channel_id=1, source_target_pairs={{0,1},{1,2},{2,3},{3,4},{4,5},{5,6},{6,7},{7,8},{8,9},{9,10},{10,1... | collective-permute-start | bytes 393224 | tf_op jit(solution)/shard_map/ppermute | solution.py:197
  36.1 15.7 %all-to-all-start.1 = ((bf16[4,192,512]{2,1,0:T(8,128)(2,1)}), bf16[4,192,512]{2,1,0:T(8,128)(2,1)S(1)}, u32[]{:S(2)}, u32[]{:S(2)}) async-start(bf16[4,192,512]{2,1,0:T(8,128)(2,1)} %pad_maximum_fusion), calls=%async_computation.1 | async-start | bytes 1572864 | tf_op jit(solution)/shard_map/all_to_all | solution.py:193
  72.2 32.0 %all-to-all-start.3 = ((bf16[4,64,1024]{2,1,0:T(8,128)(2,1)}), bf16[4,64,1024]{2,1,0:T(8,128)(2,1)S(1)}, u32[]{:S(2)}, u32[]{:S(2)}) async-start(bf16[4,64,1024]{2,1,0:T(8,128)(2,1)} %get-tuple-element.15), calls=%async_computation.3 | async-start | bytes 1048576 | tf_op jit(solution)/shard_map/all_to_all | solution.py:193
  76.8 27.4 %collective-permute-start.3 = (bf16[4,64,512]{2,1,0:T(8,128)(2,1)S(1)}, bf16[4,64,512]{2,1,0:T(8,128)(2,1)S(1)}, u32[]{:S(2)}, u32[]{:S(2)}) collective-permute-start(bf16[4,64,512]{2,1,0:T(8,128)(2,1)S(1)} %slice.31), channel_id=1, source_target_pairs={{0,256},{64,320},{128,384},{192,448},{256,0},{320,64},{384,128},{4... | collective-permute-start | bytes 786440 | tf_op jit(solution)/shard_map/ppermute | solution.py:215
  80.4 23.9 %collective-permute-start.5 = (bf16[4,32,512]{2,1,0:T(8,128)(2,1)S(1)}, bf16[4,32,512]{2,1,0:T(8,128)(2,1)S(1)}, u32[]{:S(2)}, u32[]{:S(2)}) collective-permute-start(bf16[4,32,512]{2,1,0:T(8,128)(2,1)S(1)} %get-tuple-element.19), channel_id=1, source_target_pairs={{257,0},{258,1},{259,2},{260,3},{261,4},{262,5},{263,6},{264,7},{2... | collective-permute-start | bytes 393224 | tf_op jit(solution)/shard_map/ppermute | solution.py:217
  88.3 16.0 %collective-permute-start.4 = (bf16[4,32,512]{2,1,0:T(8,128)(2,1)S(1)}, bf16[4,32,512]{2,1,0:T(8,128)(2,1)S(1)}, u32[]{:S(2)}, u32[]{:S(2)}) collective-permute-start(bf16[4,32,512]{2,1,0:T(8,128)(2,1)S(1)} %get-tuple-element.20), channel_id=1, source_target_pairs={{1,0},{2,1},{3,2},{4,3},{5,4},{6,5},{7,6},{8,7},{9,8},{10,9},{11,1... | collective-permute-start | bytes 393224 | tf_op jit(solution)/shard_map/ppermute | solution.py:216

commit v3 on v1

--- a/solution.py
+++ b/solution.py
@@ -20,7 +20,7 @@
 
 
 def attention_kernel(
-    qpos_ref, kpos_ref, qg_ref, own_ref, far_ref, pown_ref, pfar_ref, dq_ref, dkv_ref, dprev_ref
+    team_ref, qpos_ref, kpos_ref, qg_ref, own_ref, far_ref, pown_ref, pfar_ref, dq_ref, dkv_ref, dprev_ref
 ):
     half = qg_ref.shape[1] // 2
     slots = qg_ref.shape[0]
@@ -99,14 +99,19 @@
             value_sum = dv if value_sum is None else value_sum + dv
         for total, column in ((key_sum, kv * HD), (value_sum, (KV + kv) * HD)):
             low = total.astype(jnp.bfloat16)
-            for kind in range(2):
-                dkv_ref[:, kind * half : (kind + 1) * half, column : column + HD] = low[
-                    kind * keys : (kind + 1) * keys
-                ].reshape(2 * slots, half, HD)
-            dprev_ref[:, :, column : column + HD] = low[2 * keys :].reshape(2 * slots, half, HD)
-
-
-def attention(qpos, kpos, qg, own, far, pown, pfar):
+            for side in range(2):
+                first = pl.multiple_of(jnp.bitwise_xor(team_ref[0], side) * slots, slots)
+                target = pl.ds(first, slots)
+                for kind in range(3):
+                    top = kind * keys + side * rows
+                    block = low[top : top + rows].reshape(slots, half, HD)
+                    if kind < 2:
+                        dkv_ref[target, kind * half : (kind + 1) * half, column : column + HD] = block
+                    else:
+                        dprev_ref[target, :, column : column + HD] = block
+
+
+def attention(team, qpos, kpos, qg, own, far, pown, pfar):
     slots, tok, _ = qg.shape
     lines = own.shape[2]
     return pl.pallas_call(
@@ -116,8 +121,61 @@
             jax.ShapeDtypeStruct((2 * slots, tok, lines), jnp.bfloat16),
             jax.ShapeDtypeStruct((2 * slots, tok // 2, lines), jnp.bfloat16),
         ),
+        in_specs=[pl.BlockSpec(memory_space=pltpu.SMEM)] + [pl.BlockSpec()] * 7,
         compiler_params=pltpu.CompilerParams(vmem_limit_bytes=48 * 1024 * 1024),
-    )(qpos, kpos, qg, own, far, pown, pfar)
+    )(team, qpos, kpos, qg, own, far, pown, pfar)
+
+
+def pack_kernel(first_ref, second_ref, out_ref, sems):
+    wide = out_ref.shape[2] // 2
+    copies = []
+    for x in range(XN):
+        for i, ref in enumerate((first_ref, second_ref)):
+            copies.append(
+                pltpu.make_async_copy(
+                    ref.at[:, x * wide : (x + 1) * wide],
+                    out_ref.at[x, :, i * wide : (i + 1) * wide],
+                    sems.at[2 * x + i],
+                )
+            )
+    for copy in copies:
+        copy.start()
+    for copy in copies:
+        copy.wait()
+
+
+def pack(first, second):
+    tok, columns = first.shape
+    anywhere = pl.BlockSpec(memory_space=pl.ANY)
+    return pl.pallas_call(
+        pack_kernel,
+        out_shape=jax.ShapeDtypeStruct((XN, tok, 2 * columns // XN), first.dtype),
+        in_specs=[anywhere, anywhere],
+        out_specs=anywhere,
+        scratch_shapes=[pltpu.SemaphoreType.DMA((2 * XN,))],
+    )(first, second)
+
+
+def unpack_kernel(dq_ref, dkv_ref, query_ref, key_ref, value_ref):
+    wide = dq_ref.shape[2]
+    lines = KV * HD
+    for x in range(XN):
+        query_ref[:, x * wide : (x + 1) * wide] = dq_ref[x]
+        for i, ref in enumerate((key_ref, value_ref)):
+            source = slice(i * lines, (i + 1) * lines)
+            total = dkv_ref[x, :, source].astype(jnp.float32)
+            total = total + dkv_ref[XN + x, :, source].astype(jnp.float32)
+            ref[:, x * lines : (x + 1) * lines] = total.astype(ref.dtype)
+
+
+def unpack(dq, dkv):
+    tok = dq.shape[1]
+    shapes = [(tok, XN * dq.shape[2])] + [(tok, XN * KV * HD)] * 2
+    return pl.pallas_call(
+        unpack_kernel,
+        out_shape=tuple(jax.ShapeDtypeStruct(shape, jnp.bfloat16) for shape in shapes),
+        compiler_params=pltpu.CompilerParams(vmem_limit_bytes=16 * 1024 * 1024),
+    )(dq, dkv)
 
 
 def body(queries, keys, values, grad_out, order):
@@ -131,24 +189,14 @@
     ahead = [(i, (i + 1) % cycle) for i in range(cycle)]
     behind = [(j, i) for i, j in ahead]
     across = [(h, (h + XN) % groups) for h in range(groups)]
-    across_ahead = [
-        (h * cycle + b, ((h + XN) % groups) * cycle + (b + 1) % cycle)
-        for h in range(groups)
-        for b in range(cycle)
-    ]
-
     def team_exchange(array):
         return lax.all_to_all(array, "head", 0, 0, tiled=True, axis_index_groups=teams)
 
-    def packed(first, second):
-        blocks = [a.reshape(tok, XN, a.shape[1] // XN) for a in (first, second)]
-        return jnp.concatenate(blocks, axis=2).transpose(1, 0, 2)
-
-    own = team_exchange(packed(keys, values))
+    own = team_exchange(pack(keys, values))
     far = lax.ppermute(own, "head", across)
     pown = lax.ppermute(own[:, :half], "blk", ahead)
-    pfar = lax.ppermute(own[:, :half], ("head", "blk"), across_ahead)
-    qg = team_exchange(packed(queries, grad_out))
+    qg = team_exchange(pack(queries, grad_out))
+    pfar = lax.ppermute(far[:, :half], "blk", ahead)
 
     team = lax.axis_index("head") // XN
     places = lax.dynamic_index_in_dim(order.reshape(groups, cycle), mine, axis=1, keepdims=False)
@@ -159,21 +207,15 @@
     kpos = jnp.stack([early, late], axis=1)
     qpos = jnp.stack([jnp.tile(p[: XN * half], 2) for p in (early, late)], axis=0)
 
-    dq, dkv, dprev = attention(qpos, kpos, qg, own, far, pown, pfar)
+    sides = jnp.full((1,), team, jnp.int32)
+    dq, dkv, dprev = attention(sides, qpos, kpos, qg, own, far, pown, pfar)
 
     back = lax.ppermute(dprev, "blk", behind)
     dq = team_exchange(dq)
     front = (dkv[:, :half].astype(jnp.float32) + back.astype(jnp.float32)).astype(jnp.bfloat16)
     dkv = jnp.concatenate([front, dkv[:, half:]], axis=1)
-    dkv = jnp.where(team == 0, dkv, jnp.roll(dkv, XN, axis=0))
     dkv = lax.all_to_all(dkv, "head", 0, 0, tiled=True)
-    dkv = dkv[:XN].astype(jnp.float32) + dkv[XN:].astype(jnp.float32)
-    dkv = dkv.astype(jnp.bfloat16).transpose(1, 0, 2)
-    lines = KV * HD
-    grad_queries = dq.transpose(1, 0, 2).reshape(queries.shape)
-    grad_keys = dkv[:, :, :lines].reshape(keys.shape)
-    grad_values = dkv[:, :, lines:].reshape(values.shape)
-    return (grad_queries, grad_keys, grad_values)
+    return unpack(dq, dkv)
 
 
 def solution(mesh):

time: 97 us -> 130 us (1.34)
  Pallas kernels: 6.64 us -> 49.6 us
  blocking collectives: 0 us -> 22.4 us
  waiting for transfers between devices: 42 us -> 26.9 us
  starting transfers between devices: 39.9 us -> 28.1 us
  other arithmetic: 3.19 us -> 0.38 us
  local copies, waits for them, and re-layouts: 4 us -> 1.34 us
    pallas_call x0 -> x3, Pallas kernels: none -> 43 us  [the longest x2 42 us: pack(): pl.pallas_call(pack_kernel, out_shape=jax.ShapeDtypeStruct((XN, tok, 2 *...]
    all_to_all x0 -> x1, blocking collectives: none -> 22.4 us  [body(): dkv = lax.all_to_all(dkv, 'head', 0, 0, tiled=True)]
    all_to_all x1 -> x0, waiting for transfers between devices: 15.9 us -> none  [body(): dkv = lax.all_to_all(dkv, 'head', 0, 0, tiled=True)]
    ppermute x1, waiting for transfers between devices: 13.6 us -> 1.97 us  [body(): pfar = lax.ppermute(far[:, :half], 'blk', ahead)]
    all_to_all x1 -> x0, starting transfers between devices: 9.4 us -> none  [body(): dkv = lax.all_to_all(dkv, 'head', 0, 0, tiled=True)]
    ppermute x1, waiting for transfers between devices: 0.01 us -> 9.04 us  [body(): far = lax.ppermute(own, 'head', across)]
    ppermute x1, waiting for transfers between devices: 0.01 us -> 7.7 us  [body(): pown = lax.ppermute(own[:, :half], 'blk', ahead)]
    all_to_all x3, waiting for transfers between devices: 12.5 us -> 8.15 us  [team_exchange(): lax.all_to_all(array, 'head', 0, 0, tiled=True, axis_index_groups=teams)]
  transfers between devices with their start and end apart: 8 -> 7, of which waited for: 4 -> 4; matrix products, arithmetic and copies ran while one was open for 4% -> 1% of each run, Pallas kernels for 0% -> 25%
where the time goes in v3:
time: 130 us
  Pallas kernels  49.6 us (38%)
  starting transfers between devices  28.1 us (22%)
  waiting for transfers between devices  26.9 us (21%)
  blocking collectives  22.4 us (17%)
  local copies, waits for them, and re-layouts  1.34 us (1%)
    pallas_call x2, Pallas kernels, pack(): pl.pallas_call(pack_kernel, out_shape=jax.ShapeDtypeStruct((XN, tok, 2 *...  42 us
    all_to_all x1, blocking collectives, body(): dkv = lax.all_to_all(dkv, 'head', 0, 0, tiled=True)  22.4 us
    all_to_all x3, starting transfers between devices, team_exchange(): lax.all_to_all(array, 'head', 0, 0, tiled=True, axis_index_groups=teams)  13.9 us
    ppermute x1, waiting for transfers between devices, body(): far = lax.ppermute(own, 'head', across)  9.04 us
    all_to_all x3, waiting for transfers between devices, team_exchange(): lax.all_to_all(array, 'head', 0, 0, tiled=True, axis_index_groups=teams)  8.15 us
    ppermute x1, waiting for transfers between devices, body(): pown = lax.ppermute(own[:, :half], 'blk', ahead)  7.7 us
    ppermute x1, starting transfers between devices, body(): far = lax.ppermute(own, 'head', across)  6.82 us
    pallas_call x1, Pallas kernels, attention(): pl.pallas_call(attention_kernel, out_shape=(jax.ShapeDtypeStruct((slots,...  6.64 us
  transfers between devices with their start and end apart: 7, of which 4 were waited for; matrix products, arithmetic and copies ran while one was open for 1% of the time, Pallas kernels for 25%

profile of v3, /device:TPU:8, one launch (start us, length us, event | category | flops | bytes accessed | tf_op | source)
XLA Modules:
  0.0 129.5 jit_solution(16663082453102612162)
XLA Ops:
  0.6 9.1 %shard_map.77 = bf16[4,64,512]{2,1,0:T(8,128)(2,1)} custom-call(bf16[64,1024]{1,0:T(8,128)(2,1)} %first_ref.3, bf16[64,1024]{1,0:T(8,128)(2,1)} %second_ref.3), custom_call_target="tpu_custom_call" | custom-call | tf_op jit(solution)/shard_map/pallas_call | solution.py:150
  9.8 4.3 %all-to-all-start.1 = ((bf16[4,64,512]{2,1,0:T(8,128)(2,1)}), bf16[4,64,512]{2,1,0:T(8,128)(2,1)S(1)}, u32[]{:S(2)}, u32[]{:S(2)}) async-start(bf16[4,64,512]{2,1,0:T(8,128)(2,1)} %shard_map.77), calls=%async_computation.1 | async-start | bytes 524288 | tf_op jit(solution)/shard_map/all_to_all | solution.py:193
  14.1 0.0 copy-start
  14.1 0.7 copy-done
  14.7 0.1 reshape.73
  14.8 32.9 %shard_map.76 = bf16[4,64,2048]{2,1,0:T(8,128)(2,1)} custom-call(bf16[64,4096]{1,0:T(8,128)(2,1)} %first_ref.2, bf16[64,4096]{1,0:T(8,128)(2,1)} %second_ref.2), custom_call_target="tpu_custom_call" | custom-call | tf_op jit(solution)/shard_map/pallas_call | solution.py:150
  47.8 0.0 all-to-all-done.1.own_ref
  47.8 4.8 %all-to-all-start = ((bf16[4,64,2048]{2,1,0:T(8,128)(2,1)}), bf16[4,64,2048]{2,1,0:T(8,128)(2,1)S(1)}, u32[]{:S(2)}, u32[]{:S(2)}) async-start(bf16[4,64,2048]{2,1,0:T(8,128)(2,1)} %shard_map.76), calls=%async_computation | async-start | bytes 2097152 | tf_op jit(solution)/shard_map/all_to_all | solution.py:193
  52.6 0.1 constant_dynamic-slice_fusion
  52.6 6.8 %collective-permute-start = (bf16[4,64,512]{2,1,0:T(8,128)(2,1)S(1)}, bf16[4,64,512]{2,1,0:T(8,128)(2,1)S(1)}, u32[]{:S(2)}, u32[]{:S(2)}) collective-permute-start(bf16[4,64,512]{2,1,0:T(8,128)(2,1)S(1)} %all-to-all-done.1.own_ref), channel_id=1, source_target_pairs={{0,256},{64,320},{128,384},{192,448},{256,0},{320,64},{384,128},{4... | collective-permute-start | bytes 786440 | tf_op jit(solution)/shard_map/ppermute | solution.py:196
  59.5 0.2 multiply_reduce_fusion.1
  59.7 0.1 iota_add_fusion
  59.8 0.1 add.68
  59.9 0.1 add.67
  59.9 1.9 %collective-permute-start.1 = (bf16[4,32,512]{2,1,0:T(8,128)(2,1)S(1)}, bf16[4,32,512]{2,1,0:T(8,128)(2,1)S(1)}, u32[]{:S(2)}, u32[]{:S(2)}) collective-permute-start(bf16[4,32,512]{2,1,0:T(8,128)(2,1)S(1)} %slice.38), channel_id=1, source_target_pairs={{0,1},{1,2},{2,3},{3,4},{4,5},{5,6},{6,7},{7,8},{8,9},{9,10},{10,1... | collective-permute-start | bytes 393224 | tf_op jit(solution)/shard_map/ppermute | solution.py:197
  61.9 9.0 %collective-permute-done.far_ref = bf16[4,64,512]{2,1,0:T(8,128)(2,1)S(1)} collective-permute-done((bf16[4,64,512]{2,1,0:T(8,128)(2,1)S(1)}, bf16[4,64,512]{2,1,0:T(8,128)(2,1)S(1)}, u32[]{:S(2)}, u32[]{:S(2)}) %collective-permute-start) | collective-permute-done | bytes 262176 | tf_op jit(solution)/shard_map/ppermute | solution.py:196
  70.9 1.9 %collective-permute-start.2 = (bf16[4,32,512]{2,1,0:T(8,128)(2,1)S(1)}, bf16[4,32,512]{2,1,0:T(8,128)(2,1)S(1)}, u32[]{:S(2)}, u32[]{:S(2)}) collective-permute-start(bf16[4,32,512]{2,1,0:T(8,128)(2,1)S(1)} %slice.39), channel_id=1, source_target_pairs={{0,1},{1,2},{2,3},{3,4},{4,5},{5,6},{6,7},{7,8},{8,9},{9,10},{10,1... | collective-permute-start | bytes 393224 | tf_op jit(solution)/shard_map/ppermute | solution.py:199
  72.9 0.1 tile.18
  73.0 0.1 tile.16
  73.1 0.1 copy.16.kpos_ref
  73.2 7.7 %collective-permute-done.1.pown_ref = bf16[4,32,512]{2,1,0:T(8,128)(2,1)S(1)} collective-permute-done((bf16[4,32,512]{2,1,0:T(8,128)(2,1)S(1)}, bf16[4,32,512]{2,1,0:T(8,128)(2,1)S(1)}, u32[]{:S(2)}, u32[]{:S(2)}) %collective-permute-start.1) | collective-permute-done | bytes 131104 | tf_op jit(solution)/shard_map/ppermute | solution.py:197
  80.9 2.0 %collective-permute-done.2.pfar_ref = bf16[4,32,512]{2,1,0:T(8,128)(2,1)S(1)} collective-permute-done((bf16[4,32,512]{2,1,0:T(8,128)(2,1)S(1)}, bf16[4,32,512]{2,1,0:T(8,128)(2,1)S(1)}, u32[]{:S(2)}, u32[]{:S(2)}) %collective-permute-start.2) | collective-permute-done | bytes 131104 | tf_op jit(solution)/shard_map/ppermute | solution.py:199
  82.9 0.0 all-to-all-done.qg_ref
  82.9 6.6 %shard_map.78 = (bf16[4,64,1024]{2,1,0:T(8,128)(2,1)}, bf16[8,64,512]{2,1,0:T(8,128)(2,1)S(1)}, bf16[8,32,512]{2,1,0:T(8,128)(2,1)S(1)}) custom-call(s32[1]{0:T(128)} %bitcast.team_ref, s32[2,256]{1,0:T(2,128)S(1)} %pad_add_fusion.qpos_ref, s32[256,2]{1,0:T(8,128)S(1)} %copy.16.kpos_ref, bf16[4,64,2048]{2,1,0:T(8,128)(2,1)S(1)} %all-to-all-done.qg_ref, ...), custom_call_target="tpu_custom_call" | custom-call | tf_op jit(solution)/shard_map/pallas_call | solution.py:117
  89.6 3.5 %collective-permute-start.3 = (bf16[8,32,512]{2,1,0:T(8,128)(2,1)S(1)}, bf16[8,32,512]{2,1,0:T(8,128)(2,1)S(1)}, u32[]{:S(2)}, u32[]{:S(2)}) collective-permute-start(bf16[8,32,512]{2,1,0:T(8,128)(2,1)S(1)} %get-tuple-element.8), channel_id=1, source_target_pairs={{1,0},{2,1},{3,2},{4,3},{5,4},{6,5},{7,6},{8,7},{9,8},{10,9},{11,1... | collective-permute-start | bytes 786440 | tf_op jit(solution)/shard_map/ppermute | solution.py:213
  93.0 4.8 %all-to-all-start.2 = ((bf16[4,64,1024]{2,1,0:T(8,128)(2,1)}), bf16[4,64,1024]{2,1,0:T(8,128)(2,1)S(1)}, u32[]{:S(2)}, u32[]{:S(2)}) async-start(bf16[4,64,1024]{2,1,0:T(8,128)(2,1)} %get-tuple-element.6), calls=%async_computation.2 | async-start | bytes 1048576 | tf_op jit(solution)/shard_map/all_to_all | solution.py:193
  97.9 0.0 collective-permute-done.3
  97.9 0.1 add_convert_fusion
  98.0 8.1 %all-to-all-done.2.dq_ref = bf16[4,64,1024]{2,1,0:T(8,128)(2,1)S(1)} async-done(((bf16[4,64,1024]{2,1,0:T(8,128)(2,1)}), bf16[4,64,1024]{2,1,0:T(8,128)(2,1)S(1)}, u32[]{:S(2)}, u32[]{:S(2)}) %all-to-all-start.2) | async-done | bytes 524320 | tf_op jit(solution)/shard_map/all_to_all | solution.py:193
  106.1 22.4 %all_to_all.20.dkv_ref = bf16[8,64,512]{2,1,0:T(8,128)(2,1)S(1)} all-to-all(bf16[8,64,512]{2,1,0:T(8,128)(2,1)S(1)} %pad_maximum_fusion), channel_id=1, replica_groups=mesh['head'=8,'blk'=64] {'head'}, dimensions={0} | all-to-all | bytes 1048576 | tf_op jit(solution)/shard_map/all_to_all | solution.py:217
  128.6 0.9 shard_map.79
  (11 shorter events, 0.1 us)
Async XLA Ops:
  9.8 38.0 %all-to-all-start.1 = ((bf16[4,64,512]{2,1,0:T(8,128)(2,1)}), bf16[4,64,512]{2,1,0:T(8,128)(2,1)S(1)}, u32[]{:S(2)}, u32[]{:S(2)}) async-start(bf16[4,64,512]{2,1,0:T(8,128)(2,1)} %shard_map.77), calls=%async_computation.1 | async-start | bytes 524288 | tf_op jit(solution)/shard_map/all_to_all | solution.py:193
  14.1 0.7 copy-start
  47.8 35.1 %all-to-all-start = ((bf16[4,64,2048]{2,1,0:T(8,128)(2,1)}), bf16[4,64,2048]{2,1,0:T(8,128)(2,1)S(1)}, u32[]{:S(2)}, u32[]{:S(2)}) async-start(bf16[4,64,2048]{2,1,0:T(8,128)(2,1)} %shard_map.76), calls=%async_computation | async-start | bytes 2097152 | tf_op jit(solution)/shard_map/all_to_all | solution.py:193
  52.6 18.3 %collective-permute-start = (bf16[4,64,512]{2,1,0:T(8,128)(2,1)S(1)}, bf16[4,64,512]{2,1,0:T(8,128)(2,1)S(1)}, u32[]{:S(2)}, u32[]{:S(2)}) collective-permute-start(bf16[4,64,512]{2,1,0:T(8,128)(2,1)S(1)} %all-to-all-done.1.own_ref), channel_id=1, source_target_pairs={{0,256},{64,320},{128,384},{192,448},{256,0},{320,64},{384,128},{4... | collective-permute-start | bytes 786440 | tf_op jit(solution)/shard_map/ppermute | solution.py:196
  59.9 21.0 %collective-permute-start.1 = (bf16[4,32,512]{2,1,0:T(8,128)(2,1)S(1)}, bf16[4,32,512]{2,1,0:T(8,128)(2,1)S(1)}, u32[]{:S(2)}, u32[]{:S(2)}) collective-permute-start(bf16[4,32,512]{2,1,0:T(8,128)(2,1)S(1)} %slice.38), channel_id=1, source_target_pairs={{0,1},{1,2},{2,3},{3,4},{4,5},{5,6},{6,7},{7,8},{8,9},{9,10},{10,1... | collective-permute-start | bytes 393224 | tf_op jit(solution)/shard_map/ppermute | solution.py:197
  70.9 12.0 %collective-permute-start.2 = (bf16[4,32,512]{2,1,0:T(8,128)(2,1)S(1)}, bf16[4,32,512]{2,1,0:T(8,128)(2,1)S(1)}, u32[]{:S(2)}, u32[]{:S(2)}) collective-permute-start(bf16[4,32,512]{2,1,0:T(8,128)(2,1)S(1)} %slice.39), channel_id=1, source_target_pairs={{0,1},{1,2},{2,3},{3,4},{4,5},{5,6},{6,7},{7,8},{8,9},{9,10},{10,1... | collective-permute-start | bytes 393224 | tf_op jit(solution)/shard_map/ppermute | solution.py:199
  89.6 8.3 %collective-permute-start.3 = (bf16[8,32,512]{2,1,0:T(8,128)(2,1)S(1)}, bf16[8,32,512]{2,1,0:T(8,128)(2,1)S(1)}, u32[]{:S(2)}, u32[]{:S(2)}) collective-permute-start(bf16[8,32,512]{2,1,0:T(8,128)(2,1)S(1)} %get-tuple-element.8), channel_id=1, source_target_pairs={{1,0},{2,1},{3,2},{4,3},{5,4},{6,5},{7,6},{8,7},{9,8},{10,9},{11,1... | collective-permute-start | bytes 786440 | tf_op jit(solution)/shard_map/ppermute | solution.py:213
  93.0 13.1 %all-to-all-start.2 = ((bf16[4,64,1024]{2,1,0:T(8,128)(2,1)}), bf16[4,64,1024]{2,1,0:T(8,128)(2,1)S(1)}, u32[]{:S(2)}, u32[]{:S(2)}) async-start(bf16[4,64,1024]{2,1,0:T(8,128)(2,1)} %get-tuple-element.6), calls=%async_computation.2 | async-start | bytes 1048576 | tf_op jit(solution)/shard_map/all_to_all | solution.py:193

commit v4 on v1

v4 whole, which is shorter than its diff:
```python
import jax
import jax.numpy as jnp
from jax import lax
from jax.experimental import pallas as pl
from jax.experimental.pallas import tpu as pltpu
from jax.sharding import PartitionSpec as P

HD = 128
GROUP = 4
QCOL = GROUP * HD
KEY, VALUE, GRAD, WIDE = QCOL, QCOL + HD, QCOL + 2 * HD, 2 * QCOL + 2 * HD
BACK = QCOL + 2 * HD
LOG2E = 1.4426950408889634
NEG = -1e30


def dot(left, right, left_dim, right_dim):
    return lax.dot_general(
        left, right, (((left_dim,), (right_dim,)), ((), ())), preferred_element_type=jnp.float32
    )


def params(mib):
    return pltpu.CompilerParams(vmem_limit_bytes=mib * 1024 * 1024)


def attention_kernel(qpos_ref, kpos_ref, data_ref, before_ref, out_ref, dbefore_ref):
    slots, tok, _ = data_ref.shape
    half = tok // 2
    rows = slots * half
    scale = HD ** (-0.5)
    qpos = qpos_ref[...]
    kpos = kpos_ref[...]
    early_seen = kpos[:, 0:1] <= qpos[0:1, :]
    late_seen = kpos[:, 1:2] <= qpos[1:2, :]

    def columns(ref, start, column):
        return ref[:, start : start + half, column : column + HD].reshape(rows, HD)

    def tile(query, grad, key, value, seen, seen_from):
        logits = dot(key, query, 1, 1) * (scale * LOG2E)
        if key.shape[0] == rows:
            logits = jnp.where(seen, logits, NEG)
        else:
            stop = seen_from + rows
            masked = jnp.where(seen, logits[seen_from:stop], NEG)
            logits = jnp.concatenate([logits[:seen_from], masked, logits[stop:]], axis=0)
        spread = dot(value, grad, 1, 1)
        top = jnp.max(logits, axis=0, keepdims=True)
        mass = jnp.exp2(logits - top)
        weights = mass * (1.0 / jnp.sum(mass, axis=0, keepdims=True))
        low = weights.astype(jnp.bfloat16)
        delta = jnp.sum(low.astype(jnp.float32) * spread, axis=0, keepdims=True)
        slopes = (weights * (spread - delta)).astype(jnp.bfloat16)
        return (
            dot(slopes, key, 0, 0) * scale,
            dot(slopes, query, 1, 0) * scale,
            dot(low, grad, 1, 0),
        )

    key, value = [
        jnp.concatenate(
            [
                columns(data_ref, 0, column),
                columns(data_ref, half, column),
                columns(before_ref, 0, column - KEY),
            ],
            axis=0,
        )
        for column in (KEY, VALUE)
    ]
    key_sum = None
    value_sum = None
    for head in range(GROUP):
        column = head * HD
        results = []
        for start in (0, half):
            query = columns(data_ref, start, column)
            grad = columns(data_ref, start, GRAD + column)
            if start == 0:
                result = tile(query, grad, key[:rows], value[:rows], early_seen, 0)
            else:
                result = tile(query, grad, key, value, late_seen, rows)
            out_ref[:, start : start + half, column : column + HD] = (
                result[0].reshape(slots, half, HD).astype(jnp.bfloat16)
            )
            results.append(result)
        (_, early_key, early_value), (_, dk, dv) = results
        dk = jnp.concatenate([dk[:rows] + early_key, dk[rows:]], axis=0)
        dv = jnp.concatenate([dv[:rows] + early_value, dv[rows:]], axis=0)
        key_sum = dk if key_sum is None else key_sum + dk
        value_sum = dv if value_sum is None else value_sum + dv
    for total, column in ((key_sum, KEY), (value_sum, VALUE)):
        low = total.astype(jnp.bfloat16)
        for i in range(2):
            out_ref[:, i * half : (i + 1) * half, column : column + HD] = low[
                i * rows : (i + 1) * rows
            ].reshape(slots, half, HD)
        dbefore_ref[:, :, column - KEY : column - KEY + HD] = low[2 * rows :].reshape(
            slots, half, HD
        )


def attention(qpos, kpos, data, before):
    slots, tok, _ = data.shape
    return pl.pallas_call(
        attention_kernel,
        out_shape=(
            jax.ShapeDtypeStruct((slots, tok, BACK), jnp.bfloat16),
            jax.ShapeDtypeStruct(before.shape, jnp.bfloat16),
        ),
        compiler_params=params(48),
    )(qpos, kpos, data, before)


def pack_kernel(query_ref, key_ref, value_ref, grad_ref, out_ref, q_buf, k_buf, v_buf, g_buf, sems):
    column = 0
    copies = []
    for i, (ref, buf) in enumerate(
        ((query_ref, q_buf), (key_ref, k_buf), (value_ref, v_buf), (grad_ref, g_buf))
    ):
        copies.append((pltpu.make_async_copy(ref, buf, sems.at[i]), buf))
        copies[i][0].start()
    groups = out_ref.shape[0]
    for copy, buf in copies:
        copy.wait()
        wide = buf.shape[1] // groups
        for h in range(groups):
            out_ref[h, :, column : column + wide] = buf[:, h * wide : (h + 1) * wide]
        column += wide


def pack(groups, *arrays):
    tok = arrays[0].shape[0]
    return pl.pallas_call(
        pack_kernel,
        out_shape=jax.ShapeDtypeStruct((groups, tok, WIDE), arrays[0].dtype),
        in_specs=[pl.BlockSpec(memory_space=pltpu.HBM)] * 4,
        scratch_shapes=[pltpu.VMEM(a.shape, a.dtype) for a in arrays]
        + [pltpu.SemaphoreType.DMA((4,))],
        compiler_params=params(16),
    )(*arrays)


def add_kernel(data_ref, back_ref, out_ref):
    half = back_ref.shape[1]
    out_ref[:, :, :KEY] = data_ref[:, :, :KEY]
    out_ref[:, half:, KEY:] = data_ref[:, half:, KEY:]
    total = data_ref[:, :half, KEY:].astype(jnp.float32) + back_ref[...].astype(jnp.float32)
    out_ref[:, :half, KEY:] = total.astype(out_ref.dtype)


def add_back(data, back):
    return pl.pallas_call(
        add_kernel,
        out_shape=jax.ShapeDtypeStruct(data.shape, data.dtype),
        compiler_params=params(16),
    )(data, back)


def unpack_kernel(data_ref, query_ref, key_ref, value_ref):
    for h in range(data_ref.shape[0]):
        query_ref[:, h * QCOL : (h + 1) * QCOL] = data_ref[h, :, :KEY]
        key_ref[:, h * HD : (h + 1) * HD] = data_ref[h, :, KEY:VALUE]
        value_ref[:, h * HD : (h + 1) * HD] = data_ref[h, :, VALUE:BACK]


def unpack(data):
    groups, tok, _ = data.shape
    widths = (groups * QCOL, groups * HD, groups * HD)
    return pl.pallas_call(
        unpack_kernel,
        out_shape=tuple(jax.ShapeDtypeStruct((tok, w), data.dtype) for w in widths),
        compiler_params=params(16),
    )(data)


def body(queries, keys, values, grad_out, order):
    groups = lax.axis_size("head")
    cycle = lax.axis_size("blk")
    mine = lax.axis_index("blk")
    half = queries.shape[0] // 2
    slot_total = order.shape[0]
    ahead = [(i, (i + 1) % cycle) for i in range(cycle)]
    behind = [(j, i) for i, j in ahead]

    def exchange(array):
        return lax.all_to_all(array, "head", 0, 0, tiled=True)

    data = exchange(pack(groups, queries, keys, values, grad_out))
    before = lax.ppermute(data[:, :half, KEY:GRAD], "blk", ahead)

    places = lax.dynamic_index_in_dim(order.reshape(groups, cycle), mine, axis=1, keepdims=False)
    offset = lax.iota(jnp.int32, half)
    early = (places[:, None] * half + offset[None, :]).reshape(groups * half)
    late = ((2 * slot_total - 1 - places)[:, None] * half + offset[None, :]).reshape(groups * half)
    kpos = jnp.stack([early, late], axis=1)
    qpos = jnp.stack([early, late], axis=0)

    out, dbefore = attention(qpos, kpos, data, before)
    back = lax.ppermute(dbefore, "blk", behind)
    return unpack(exchange(add_back(out, back)))


def solution(mesh):
    rows = P(("head", "blk"), None)
    return jax.shard_map(
        body,
        mesh=mesh,
        in_specs=(rows, rows, rows, rows, P()),
        out_specs=(rows, rows, rows),
        check_vma=False,
    )
```

time: 97 us -> 99.7 us (1.028)
  the two profiles are of different devices: /device:TPU:8 before, /device:TPU:16 now
where the time goes in v4:
time: 99.7 us; the launch traced here: 99.3 us
  waiting for transfers between devices  47.8 us (48%)
  blocking collectives  25.9 us (26%)
  starting transfers between devices  11.6 us (12%)
  Pallas kernels  8.58 us (9%)
  local copies, waits for them, and re-layouts  4.42 us (4%)
    all_to_all x1, waiting for transfers between devices, exchange(): return lax.all_to_all(array, 'head', 0, 0, tiled=True)  33.9 us
    all_to_all x1, blocking collectives, exchange(): return lax.all_to_all(array, 'head', 0, 0, tiled=True)  25.9 us
    ppermute x1, waiting for transfers between devices, body(): before = lax.ppermute(data[:, :half, KEY:GRAD], 'blk', ahead)  11.4 us
    all_to_all x1, starting transfers between devices, exchange(): return lax.all_to_all(array, 'head', 0, 0, tiled=True)  7.78 us
    pallas_call x1, Pallas kernels, attention(): pl.pallas_call(attention_kernel, out_shape=(jax.ShapeDtypeStruct((slots,...  5.91 us
    unnamed x10, local copies, waits for them, and re-layouts  3.89 us
    ppermute x1, waiting for transfers between devices, body(): back = lax.ppermute(dbefore, 'blk', behind)  2.5 us
  transfers between devices with their start and end apart: 3, of which 3 were waited for; matrix products, arithmetic and copies ran while one was open for 1% of the time, Pallas kernels for 0%

profile of v4, /device:TPU:16, one launch (start us, length us, event | category | flops | bytes accessed | tf_op | source)
XLA Modules:
  0.0 99.3 jit_solution(13401292953500268553)
XLA Ops:
  0.6 0.0 copy-start
  0.6 1.0 %copy-done = bf16[64,4096]{1,0:T(8,128)(2,1)S(1)} copy-done((bf16[64,4096]{1,0:T(8,128)(2,1)S(1)}, bf16[64,4096]{1,0:T(8,128)(2,1)}, u32[]{:S(2)}) %copy-start) | copy-done | bytes 524312
  1.7 0.0 copy-start.1
  1.7 1.0 %copy-done.1 = bf16[64,4096]{1,0:T(8,128)(2,1)S(1)} copy-done((bf16[64,4096]{1,0:T(8,128)(2,1)S(1)}, bf16[64,4096]{1,0:T(8,128)(2,1)}, u32[]{:S(2)}) %copy-start.1) | copy-done | bytes 524312
  2.7 0.0 copy-start.2
  2.7 0.9 copy-done.2
  3.6 0.0 copy-start.3
  3.6 0.9 copy-done.3
  4.5 1.6 %shard_map.76 = bf16[8,64,1280]{2,1,0:T(8,128)(2,1)} custom-call(bf16[64,4096]{1,0:T(8,128)(2,1)S(1)} %copy-done, bf16[64,1024]{1,0:T(8,128)(2,1)S(1)} %copy-done.2, bf16[64,1024]{1,0:T(8,128)(2,1)S(1)} %copy-done.3, bf16[64,4096]{1,0:T(8,128)(2,1)S(1)} %copy-done.1), custom_call_target="tpu_custom_call" | custom-call | tf_op jit(solution)/shard_map/pallas_call | solution.py:135
  6.2 0.0 copy-start.4
  6.2 7.8 %all-to-all-start = ((bf16[8,64,1280]{2,1,0:T(8,128)(2,1)}), bf16[8,64,1280]{2,1,0:T(8,128)(2,1)S(1)}, u32[]{:S(2)}, u32[]{:S(2)}) async-start(bf16[8,64,1280]{2,1,0:T(8,128)(2,1)} %shard_map.76), calls=%async_computation | async-start | bytes 2621440 | tf_op jit(solution)/shard_map/all_to_all | solution.py:188
  14.0 0.0 copy-done.4
  14.0 0.1 reshape.98
  14.0 0.2 multiply_reduce_fusion.1
  14.2 0.1 iota_add_fusion
  14.3 0.1 add.86
  14.4 0.1 add.85
  14.5 33.9 %all-to-all-done.data_ref = bf16[8,64,1280]{2,1,0:T(8,128)(2,1)S(1)} async-done(((bf16[8,64,1280]{2,1,0:T(8,128)(2,1)}), bf16[8,64,1280]{2,1,0:T(8,128)(2,1)S(1)}, u32[]{:S(2)}, u32[]{:S(2)}) %all-to-all-start) | async-done | bytes 1310752 | tf_op jit(solution)/shard_map/all_to_all | solution.py:188
  48.4 1.9 %collective-permute-start = (bf16[8,32,256]{2,1,0:T(8,128)(2,1)S(1)}, bf16[8,32,256]{2,1,0:T(8,128)(2,1)S(1)}, u32[]{:S(2)}, u32[]{:S(2)}) collective-permute-start(bf16[8,32,256]{2,1,0:T(8,128)(2,1)S(1)} %slice.4), channel_id=1, source_target_pairs={{0,1},{1,2},{2,3},{3,4},{4,5},{5,6},{6,7},{7,8},{8,9},{9,10},{10,1... | collective-permute-start | bytes 393224 | tf_op jit(solution)/shard_map/ppermute | solution.py:191
  50.3 0.1 add.84
  50.4 0.1 add.79
  50.5 0.1 copy.12.kpos_ref
  50.6 11.4 %collective-permute-done.before_ref = bf16[8,32,256]{2,1,0:T(8,128)(2,1)S(1)} collective-permute-done((bf16[8,32,256]{2,1,0:T(8,128)(2,1)S(1)}, bf16[8,32,256]{2,1,0:T(8,128)(2,1)S(1)}, u32[]{:S(2)}, u32[]{:S(2)}) %collective-permute-start) | collective-permute-done | bytes 131104 | tf_op jit(solution)/shard_map/ppermute | solution.py:191
  62.0 5.9 %shard_map.77 = (bf16[8,64,768]{2,1,0:T(8,128)(2,1)S(1)}, bf16[8,32,256]{2,1,0:T(8,128)(2,1)S(1)}) custom-call(s32[2,256]{1,0:T(2,128)S(1)} %pad_add_fusion.qpos_ref, s32[256,2]{1,0:T(8,128)S(1)} %copy.12.kpos_ref, bf16[8,64,1280]{2,1,0:T(8,128)(2,1)S(1)} %all-to-all-done.data_ref, bf16[8,32,256]{2,1,0:T(8,128)(2,1)S(1)} %collective-permute-done.before_ref), custom_call_target="tpu_custom_call" | custom-call | tf_op jit(solution)/shard_map/pallas_call | solution.py:106
  67.9 1.9 %collective-permute-start.1 = (bf16[8,32,256]{2,1,0:T(8,128)(2,1)S(1)}, bf16[8,32,256]{2,1,0:T(8,128)(2,1)S(1)}, u32[]{:S(2)}, u32[]{:S(2)}) collective-permute-start(bf16[8,32,256]{2,1,0:T(8,128)(2,1)S(1)} %get-tuple-element.6), channel_id=1, source_target_pairs={{1,0},{2,1},{3,2},{4,3},{5,4},{6,5},{7,6},{8,7},{9,8},{10,9},{11,1... | collective-permute-start | bytes 393224 | tf_op jit(solution)/shard_map/ppermute | solution.py:201
  69.9 2.5 %collective-permute-done.1.back_ref = bf16[8,32,256]{2,1,0:T(8,128)(2,1)S(1)} collective-permute-done((bf16[8,32,256]{2,1,0:T(8,128)(2,1)S(1)}, bf16[8,32,256]{2,1,0:T(8,128)(2,1)S(1)}, u32[]{:S(2)}, u32[]{:S(2)}) %collective-permute-start.1) | collective-permute-done | bytes 131104 | tf_op jit(solution)/shard_map/ppermute | solution.py:201
  72.4 0.1 shard_map.78
  72.4 25.9 %all_to_all.10.data_ref = bf16[8,64,768]{2,1,0:T(8,128)(2,1)S(1)} all-to-all(bf16[8,64,768]{2,1,0:T(8,128)(2,1)S(1)} %shard_map.78), channel_id=1, replica_groups=mesh['head'=8,'blk'=64] {'head'}, dimensions={0} | all-to-all | bytes 1572864 | tf_op jit(solution)/shard_map/all_to_all | solution.py:188
  98.3 1.0 shard_map.79
  (3 shorter events, 0.0 us)
Async XLA Ops:
  0.6 1.0 %copy-start = (bf16[64,4096]{1,0:T(8,128)(2,1)S(1)}, bf16[64,4096]{1,0:T(8,128)(2,1)}, u32[]{:S(2)}) copy-start(bf16[64,4096]{1,0:T(8,128)(2,1)} %query_ref.1) | copy-start | bytes 1572868
  1.7 1.0 %copy-start.1 = (bf16[64,4096]{1,0:T(8,128)(2,1)S(1)}, bf16[64,4096]{1,0:T(8,128)(2,1)}, u32[]{:S(2)}) copy-start(bf16[64,4096]{1,0:T(8,128)(2,1)} %grad_ref.1) | copy-start | bytes 1572868
  2.7 0.9 copy-start.2
  3.6 0.9 copy-start.3
  6.2 7.8 %copy-start.4 = (s32[512]{0:T(512)S(1)}, s32[512]{0:T(512)}, u32[]{:S(2)}) copy-start(s32[512]{0:T(512)} %param.9) | copy-start | bytes 6148
  6.2 42.2 %all-to-all-start = ((bf16[8,64,1280]{2,1,0:T(8,128)(2,1)}), bf16[8,64,1280]{2,1,0:T(8,128)(2,1)S(1)}, u32[]{:S(2)}, u32[]{:S(2)}) async-start(bf16[8,64,1280]{2,1,0:T(8,128)(2,1)} %shard_map.76), calls=%async_computation | async-start | bytes 2621440 | tf_op jit(solution)/shard_map/all_to_all | solution.py:188
  48.4 13.6 %collective-permute-start = (bf16[8,32,256]{2,1,0:T(8,128)(2,1)S(1)}, bf16[8,32,256]{2,1,0:T(8,128)(2,1)S(1)}, u32[]{:S(2)}, u32[]{:S(2)}) collective-permute-start(bf16[8,32,256]{2,1,0:T(8,128)(2,1)S(1)} %slice.4), channel_id=1, source_target_pairs={{0,1},{1,2},{2,3},{3,4},{4,5},{5,6},{6,7},{7,8},{8,9},{9,10},{10,1... | collective-permute-start | bytes 393224 | tf_op jit(solution)/shard_map/ppermute | solution.py:191
  67.9 4.4 %collective-permute-start.1 = (bf16[8,32,256]{2,1,0:T(8,128)(2,1)S(1)}, bf16[8,32,256]{2,1,0:T(8,128)(2,1)S(1)}, u32[]{:S(2)}, u32[]{:S(2)}) collective-permute-start(bf16[8,32,256]{2,1,0:T(8,128)(2,1)S(1)} %get-tuple-element.6), channel_id=1, source_target_pairs={{1,0},{2,1},{3,2},{4,3},{5,4},{6,5},{7,6},{8,7},{9,8},{10,9},{11,1... | collective-permute-start | bytes 393224 | tf_op jit(solution)/shard_map/ppermute | solution.py:201

commit v5 on v3

v5 whole, which is shorter than its diff:
```python
import jax
import jax.numpy as jnp
from jax import lax
from jax.experimental import pallas as pl
from jax.experimental.pallas import tpu as pltpu
from jax.sharding import PartitionSpec as P

HD = 128
XN = 4
KV = 2
GROUP = 4
QCOL = KV * GROUP * HD
KEY, VALUE, GRAD, WIDE = QCOL, QCOL + KV * HD, QCOL + 2 * KV * HD, 2 * QCOL + 2 * KV * HD
LINES = 2 * KV * HD
LOG2E = 1.4426950408889634
NEG = -1e30


def dot(left, right, left_dim, right_dim):
    return lax.dot_general(
        left, right, (((left_dim,), (right_dim,)), ((), ())), preferred_element_type=jnp.float32
    )


def params(mib):
    return pltpu.CompilerParams(vmem_limit_bytes=mib * 1024 * 1024)


def columns(ref, start, stop, column):
    block = ref[:, start:stop, column : column + HD]
    return block.reshape(block.shape[0] * block.shape[1], HD)


def tile(query, grad, key, value, seen, seen_from):
    scale = HD ** (-0.5)
    logits = dot(key, query, 1, 1) * (scale * LOG2E)
    stop = seen_from + seen.shape[0]
    masked = jnp.where(seen, logits[seen_from:stop], NEG)
    if seen.shape[0] == key.shape[0]:
        logits = masked
    else:
        logits = jnp.concatenate([logits[:seen_from], masked, logits[stop:]], axis=0)
    spread = dot(value, grad, 1, 1)
    top = jnp.max(logits, axis=0, keepdims=True)
    mass = jnp.exp2(logits - top)
    weights = mass * (1.0 / jnp.sum(mass, axis=0, keepdims=True))
    low = weights.astype(jnp.bfloat16)
    delta = jnp.sum(low.astype(jnp.float32) * spread, axis=0, keepdims=True)
    slopes = (weights * (spread - delta)).astype(jnp.bfloat16)
    return (
        dot(slopes, key, 0, 0) * scale,
        dot(slopes, query, 1, 0) * scale,
        dot(low, grad, 1, 0),
    )


def attend(data_ref, dq_ref, kv, start, stop, out_start, key, value, seen, seen_from):
    slots = data_ref.shape[0]
    rows = slots * (stop - start)
    key_sum = None
    value_sum = None
    for pair in range(GROUP // 2):
        heads = [kv * GROUP + pair * 2 + i for i in range(2)]
        query, grad = [
            jnp.concatenate(
                [columns(data_ref, start, stop, first + h * HD) for h in heads], axis=0
            )
            for first in (0, GRAD)
        ]
        dq, dk, dv = tile(query, grad, key, value, seen, seen_from)
        for i, h in enumerate(heads):
            dq_ref[:, out_start : out_start + stop - start, h * HD : (h + 1) * HD] = (
                dq[i * rows : (i + 1) * rows]
                .reshape(slots, stop - start, HD)
                .astype(jnp.bfloat16)
            )
        key_sum = dk if key_sum is None else key_sum + dk
        value_sum = dv if value_sum is None else value_sum + dv
    return key_sum, value_sum


def early_kernel(qpos_ref, kpos_ref, data_ref, far_ref, dq_ref, dkv_ref):
    half = data_ref.shape[1] // 2
    seen = kpos_ref[:, 0:1] <= qpos_ref[0:1, :]
    for kv in range(KV):
        key, value = [
            jnp.concatenate(
                [
                    columns(data_ref, 0, half, KEY + column),
                    columns(far_ref, 0, half, column),
                ],
                axis=0,
            )
            for column in (kv * HD, (KV + kv) * HD)
        ]
        sums = attend(data_ref, dq_ref, kv, 0, half, 0, key, value, seen, 0)
        for i, total in enumerate(sums):
            dkv_ref[2 * kv + i] = total


def late_kernel(
    team_ref,
    qpos_ref,
    kpos_ref,
    data_ref,
    far_ref,
    pown_ref,
    pfar_ref,
    dqe_ref,
    dkve_ref,
    dq_ref,
    dkv_ref,
    dprev_ref,
):
    slots, tok, _ = data_ref.shape
    half = tok // 2
    rows = slots * half
    keys = kpos_ref.shape[0]
    seen = kpos_ref[:, 1:2] <= qpos_ref[1:2, :]
    dq_ref[:, :half, :] = dqe_ref[...]
    for kv in range(KV):
        key, value = [
            jnp.concatenate(
                [
                    columns(data_ref, 0, half, KEY + column),
                    columns(far_ref, 0, half, column),
                    columns(data_ref, half, tok, KEY + column),
                    columns(far_ref, half, tok, column),
                    columns(pown_ref, 0, half, column),
                    columns(pfar_ref, 0, half, column),
                ],
                axis=0,
            )
            for column in (kv * HD, (KV + kv) * HD)
        ]
        sums = attend(data_ref, dq_ref, kv, half, tok, half, key, value, seen, keys)
        for i, total in enumerate(sums):
            column = (i * KV + kv) * HD
            first = (total[:keys] + dkve_ref[2 * kv + i]).astype(jnp.bfloat16)
            low = jnp.concatenate([first, total[keys:].astype(jnp.bfloat16)], axis=0)
            for side in range(2):
                at = pl.multiple_of(jnp.bitwise_xor(team_ref[0], side) * slots, slots)
                target = pl.ds(at, slots)
                for kind in range(3):
                    top = kind * keys + side * rows
                    block = low[top : top + rows].reshape(slots, half, HD)
                    if kind < 2:
                        dkv_ref[target, kind * half : (kind + 1) * half, column : column + HD] = block
                    else:
                        dprev_ref[target, :, column : column + HD] = block


def early_part(qpos, kpos, data, far):
    slots, tok, _ = data.shape
    return pl.pallas_call(
        early_kernel,
        out_shape=(
            jax.ShapeDtypeStruct((slots, tok // 2, QCOL), jnp.bfloat16),
            jax.ShapeDtypeStruct((2 * KV, kpos.shape[0], HD), jnp.float32),
        ),
        compiler_params=params(40),
    )(qpos, kpos, data, far)


def late_part(team, *arrays):
    slots, tok, _ = arrays[2].shape
    return pl.pallas_call(
        late_kernel,
        out_shape=(
            jax.ShapeDtypeStruct((slots, tok, QCOL), jnp.bfloat16),
            jax.ShapeDtypeStruct((2 * slots, tok, LINES), jnp.bfloat16),
            jax.ShapeDtypeStruct((2 * slots, tok // 2, LINES), jnp.bfloat16),
        ),
        in_specs=[pl.BlockSpec(memory_space=pltpu.SMEM)] + [pl.BlockSpec()] * len(arrays),
        compiler_params=params(48),
    )(team, *arrays)


def pack_kernel(query_ref, key_ref, value_ref, grad_ref, out_ref, q_buf, k_buf, v_buf, g_buf, sems):
    column = 0
    copies = []
    for i, (ref, buf) in enumerate(
        ((query_ref, q_buf), (key_ref, k_buf), (value_ref, v_buf), (grad_ref, g_buf))
    ):
        copies.append((pltpu.make_async_copy(ref, buf, sems.at[i]), buf))
        copies[i][0].start()
    groups = out_ref.shape[0]
    for copy, buf in copies:
        copy.wait()
        wide = buf.shape[1] // groups
        for h in range(groups):
            out_ref[h, :, column : column + wide] = buf[:, h * wide : (h + 1) * wide]
        column += wide


def pack(groups, *arrays):
    tok = arrays[0].shape[0]
    return pl.pallas_call(
        pack_kernel,
        out_shape=jax.ShapeDtypeStruct((groups, tok, WIDE), arrays[0].dtype),
        in_specs=[pl.BlockSpec(memory_space=pltpu.HBM)] * 4,
        scratch_shapes=[pltpu.VMEM(a.shape, a.dtype) for a in arrays]
        + [pltpu.SemaphoreType.DMA((4,))],
    )(*arrays)


def unpack_kernel(dq_ref, dkv_ref, query_ref, key_ref, value_ref):
    wide = dq_ref.shape[2]
    lines = KV * HD
    for x in range(XN):
        query_ref[:, x * wide : (x + 1) * wide] = dq_ref[x]
        for i, ref in enumerate((key_ref, value_ref)):
            source = slice(i * lines, (i + 1) * lines)
            total = dkv_ref[x, :, source].astype(jnp.float32)
            total = total + dkv_ref[XN + x, :, source].astype(jnp.float32)
            ref[:, x * lines : (x + 1) * lines] = total.astype(ref.dtype)


def unpack(dq, dkv):
    tok = dq.shape[1]
    shapes = [(tok, XN * dq.shape[2])] + [(tok, XN * KV * HD)] * 2
    return pl.pallas_call(
        unpack_kernel,
        out_shape=tuple(jax.ShapeDtypeStruct(shape, jnp.bfloat16) for shape in shapes),
        compiler_params=params(16),
    )(dq, dkv)


def body(queries, keys, values, grad_out, order):
    groups = lax.axis_size("head")
    cycle = lax.axis_size("blk")
    mine = lax.axis_index("blk")
    tok = queries.shape[0]
    half = tok // 2
    slot_total = order.shape[0]
    teams = [list(range(t, t + XN)) for t in range(0, groups, XN)]
    ahead = [(i, (i + 1) % cycle) for i in range(cycle)]
    behind = [(j, i) for i, j in ahead]
    across = [(h, (h + XN) % groups) for h in range(groups)]
    def team_exchange(array):
        return lax.all_to_all(array, "head", 0, 0, tiled=True, axis_index_groups=teams)

    data = team_exchange(pack(XN, queries, keys, values, grad_out))
    far = lax.ppermute(data[:, :, KEY:GRAD], "head", across)
    pown = lax.ppermute(data[:, :half, KEY:GRAD], "blk", ahead)
    pfar = lax.ppermute(far[:, :half], "blk", ahead)

    team = lax.axis_index("head") // XN
    places = lax.dynamic_index_in_dim(order.reshape(groups, cycle), mine, axis=1, keepdims=False)
    places = jnp.where(team == 0, places, jnp.roll(places, -XN))
    offset = lax.iota(jnp.int32, half)
    early = (places[:, None] * half + offset[None, :]).reshape(groups * half)
    late = ((2 * slot_total - 1 - places)[:, None] * half + offset[None, :]).reshape(groups * half)
    kpos = jnp.stack([early, late], axis=1)
    qpos = jnp.stack([jnp.tile(p[: XN * half], 2) for p in (early, late)], axis=0)

    sides = jnp.full((1,), team, jnp.int32)
    dq_early, dkv_early = early_part(qpos, kpos, data, far)
    dq, dkv, dprev = late_part(
        sides, qpos, kpos, data, far, pown, pfar, dq_early, dkv_early
    )

    back = lax.ppermute(dprev, "blk", behind)
    dq = team_exchange(dq)
    front = (dkv[:, :half].astype(jnp.float32) + back.astype(jnp.float32)).astype(jnp.bfloat16)
    dkv = jnp.concatenate([front, dkv[:, half:]], axis=1)
    dkv = lax.all_to_all(dkv, "head", 0, 0, tiled=True)
    return unpack(dq, dkv)


def solution(mesh):
    rows = P(("head", "blk"), None)
    return jax.shard_map(
        body,
        mesh=mesh,
        in_specs=(rows, rows, rows, rows, P()),
        out_specs=(rows, rows, rows),
        check_vma=False,
    )
```

time: 130 us -> 100 us (0.77)
  Pallas kernels: 49.6 us -> 10.3 us
  waiting for transfers between devices: 26.9 us -> 42.4 us
  starting transfers between devices: 28.1 us -> 22.3 us
    pallas_call x3, Pallas kernels: 48.7 us -> 9.41 us  [the longest x1 4.96 us: late_part(): pl.pallas_call(late_kernel, out_shape=(jax.ShapeDtypeStruct((slots, tok,...]
    all_to_all x3 -> x2, waiting for transfers between devices: 8.15 us -> 25.7 us  [team_exchange(): lax.all_to_all(array, 'head', 0, 0, tiled=True, axis_index_groups=teams)]
    all_to_all x3 -> x2, starting transfers between devices: 13.9 us -> 7.79 us  [team_exchange(): lax.all_to_all(array, 'head', 0, 0, tiled=True, axis_index_groups=teams)]
    ppermute x2, waiting for transfers between devices: 16.7 us -> 14 us  [the longest x1 8.69 us: body(): far = lax.ppermute(data[:, :, KEY:GRAD], 'head', across)]
  transfers between devices with their start and end apart: 7 -> 6, of which waited for: 4 -> 6; matrix products, arithmetic and copies ran while one was open for 1% -> 1% of each run, Pallas kernels for 25% -> 2%
where the time goes in v5:
time: 100 us; the launch traced here: 99.7 us
  waiting for transfers between devices  42.4 us (42%)
  blocking collectives  22.8 us (23%)
  starting transfers between devices  22.3 us (22%)
  Pallas kernels  10.3 us (10%)
    all_to_all x2, waiting for transfers between devices, team_exchange(): lax.all_to_all(array, 'head', 0, 0, tiled=True, axis_index_groups=teams)  25.7 us
    all_to_all x1, blocking collectives, body(): dkv = lax.all_to_all(dkv, 'head', 0, 0, tiled=True)  22.8 us
    ppermute x1, waiting for transfers between devices, body(): far = lax.ppermute(data[:, :, KEY:GRAD], 'head', across)  8.69 us
    all_to_all x2, starting transfers between devices, team_exchange(): lax.all_to_all(array, 'head', 0, 0, tiled=True, axis_index_groups=teams)  7.79 us
    ppermute x1, starting transfers between devices, body(): far = lax.ppermute(data[:, :, KEY:GRAD], 'head', across)  6.83 us
    ppermute x1, waiting for transfers between devices, body(): pown = lax.ppermute(data[:, :half, KEY:GRAD], 'blk', ahead)  5.31 us
    pallas_call x1, Pallas kernels, late_part(): pl.pallas_call(late_kernel, out_shape=(jax.ShapeDtypeStruct((slots, tok,...  4.96 us
    ppermute x1, starting transfers between devices, body(): back = lax.ppermute(dprev, 'blk', behind)  3.82 us
  transfers between devices with their start and end apart: 6, of which 6 were waited for; matrix products, arithmetic and copies ran while one was open for 1% of the time, Pallas kernels for 2%

profile of v5, /device:TPU:8, one launch (start us, length us, event | category | flops | bytes accessed | tf_op | source)
XLA Modules:
  0.0 99.7 jit_solution(1126593525449368269)
XLA Ops:
  0.6 2.4 %shard_map.76 = bf16[4,64,2560]{2,1,0:T(8,128)(2,1)} custom-call(bf16[64,4096]{1,0:T(8,128)(2,1)} %query_ref.1, bf16[64,1024]{1,0:T(8,128)(2,1)} %key_ref.1, bf16[64,1024]{1,0:T(8,128)(2,1)} %value_ref.1, bf16[64,4096]{1,0:T(8,128)(2,1)} %grad_ref.1), custom_call_target="tpu_custom_call" | custom-call | tf_op jit(solution)/shard_map/pallas_call | solution.py:198
  3.1 0.0 copy-start
  3.1 4.3 %all-to-all-start = ((bf16[4,64,2560]{2,1,0:T(8,128)(2,1)}), bf16[4,64,2560]{2,1,0:T(8,128)(2,1)S(1)}, u32[]{:S(2)}, u32[]{:S(2)}) async-start(bf16[4,64,2560]{2,1,0:T(8,128)(2,1)} %shard_map.76), calls=%async_computation | async-start | bytes 2621440 | tf_op jit(solution)/shard_map/all_to_all | solution.py:241
  7.4 0.0 copy-done
  7.4 0.1 reshape.73
  7.4 0.1 constant_dynamic-slice_fusion
  7.5 17.8 %all-to-all-done.data_ref = bf16[4,64,2560]{2,1,0:T(8,128)(2,1)S(1)} async-done(((bf16[4,64,2560]{2,1,0:T(8,128)(2,1)}), bf16[4,64,2560]{2,1,0:T(8,128)(2,1)S(1)}, u32[]{:S(2)}, u32[]{:S(2)}) %all-to-all-start) | async-done | bytes 1310752 | tf_op jit(solution)/shard_map/all_to_all | solution.py:241
  25.3 6.8 %collective-permute-start = (bf16[4,64,512]{2,1,0:T(8,128)(2,1)S(1)}, bf16[4,64,512]{2,1,0:T(8,128)(2,1)S(1)}, u32[]{:S(2)}, u32[]{:S(2)}) collective-permute-start(bf16[4,64,512]{2,1,0:T(8,128)(2,1)S(1)} %slice.42), channel_id=1, source_target_pairs={{0,256},{64,320},{128,384},{192,448},{256,0},{320,64},{384,128},{4... | collective-permute-start | bytes 786440 | tf_op jit(solution)/shard_map/ppermute | solution.py:244
  32.2 0.2 multiply_reduce_fusion.1
  32.4 0.1 iota_add_fusion
  32.4 0.1 add.68
  32.5 0.1 add.67
  32.6 1.9 %collective-permute-start.1 = (bf16[4,32,512]{2,1,0:T(8,128)(2,1)S(1)}, bf16[4,32,512]{2,1,0:T(8,128)(2,1)S(1)}, u32[]{:S(2)}, u32[]{:S(2)}) collective-permute-start(bf16[4,32,512]{2,1,0:T(8,128)(2,1)S(1)} %slice.43), channel_id=1, source_target_pairs={{0,1},{1,2},{2,3},{3,4},{4,5},{5,6},{6,7},{7,8},{8,9},{9,10},{10,1... | collective-permute-start | bytes 393224 | tf_op jit(solution)/shard_map/ppermute | solution.py:245
  34.5 8.7 %collective-permute-done.far_ref = bf16[4,64,512]{2,1,0:T(8,128)(2,1)S(1)} collective-permute-done((bf16[4,64,512]{2,1,0:T(8,128)(2,1)S(1)}, bf16[4,64,512]{2,1,0:T(8,128)(2,1)S(1)}, u32[]{:S(2)}, u32[]{:S(2)}) %collective-permute-start) | collective-permute-done | bytes 262176 | tf_op jit(solution)/shard_map/ppermute | solution.py:244
  43.2 1.9 %collective-permute-start.2 = (bf16[4,32,512]{2,1,0:T(8,128)(2,1)S(1)}, bf16[4,32,512]{2,1,0:T(8,128)(2,1)S(1)}, u32[]{:S(2)}, u32[]{:S(2)}) collective-permute-start(bf16[4,32,512]{2,1,0:T(8,128)(2,1)S(1)} %slice.44), channel_id=1, source_target_pairs={{0,1},{1,2},{2,3},{3,4},{4,5},{5,6},{6,7},{7,8},{8,9},{9,10},{10,1... | collective-permute-start | bytes 393224 | tf_op jit(solution)/shard_map/ppermute | solution.py:246
  45.2 0.1 tile.18
  45.3 0.1 tile.16
  45.4 0.1 copy.18.kpos_ref
  45.5 2.0 %shard_map.77 = (bf16[4,32,1024]{2,1,0:T(8,128)(2,1)S(1)}, f32[4,256,128]{2,1,0:T(8,128)S(1)}) custom-call(s32[2,256]{1,0:T(2,128)S(1)} %pad_add_fusion.qpos_ref, s32[256,2]{1,0:T(8,128)S(1)} %copy.18.kpos_ref, bf16[4,64,2560]{2,1,0:T(8,128)(2,1)S(1)} %all-to-all-done.data_ref, bf16[4,64,512]{2,1,0:T(8,128)(2,1)S(1)} %collective-permute-done.far_ref), custom_call_target="tpu_custom_call" | custom-call | tf_op jit(solution)/shard_map/pallas_call | solution.py:155
  47.6 5.3 %collective-permute-done.1.pown_ref = bf16[4,32,512]{2,1,0:T(8,128)(2,1)S(1)} collective-permute-done((bf16[4,32,512]{2,1,0:T(8,128)(2,1)S(1)}, bf16[4,32,512]{2,1,0:T(8,128)(2,1)S(1)}, u32[]{:S(2)}, u32[]{:S(2)}) %collective-permute-start.1) | collective-permute-done | bytes 131104 | tf_op jit(solution)/shard_map/ppermute | solution.py:245
  52.9 2.3 %collective-permute-done.2.pfar_ref = bf16[4,32,512]{2,1,0:T(8,128)(2,1)S(1)} collective-permute-done((bf16[4,32,512]{2,1,0:T(8,128)(2,1)S(1)}, bf16[4,32,512]{2,1,0:T(8,128)(2,1)S(1)}, u32[]{:S(2)}, u32[]{:S(2)}) %collective-permute-start.2) | collective-permute-done | bytes 131104 | tf_op jit(solution)/shard_map/ppermute | solution.py:246
  55.2 5.0 %shard_map.78 = (bf16[4,64,1024]{2,1,0:T(8,128)(2,1)}, bf16[8,64,512]{2,1,0:T(8,128)(2,1)S(1)}, bf16[8,32,512]{2,1,0:T(8,128)(2,1)S(1)}) custom-call(s32[1]{0:T(128)} %bitcast.team_ref, s32[2,256]{1,0:T(2,128)S(1)} %pad_add_fusion.qpos_ref, s32[256,2]{1,0:T(8,128)S(1)} %copy.18.kpos_ref, bf16[4,64,2560]{2,1,0:T(8,128)(2,1)S(1)} %all-to-all-done.data_ref, ...), custom_call_target="tpu_custom_call" | custom-call | tf_op jit(solution)/shard_map/pallas_call | solution.py:167
  60.2 3.8 %collective-permute-start.3 = (bf16[8,32,512]{2,1,0:T(8,128)(2,1)S(1)}, bf16[8,32,512]{2,1,0:T(8,128)(2,1)S(1)}, u32[]{:S(2)}, u32[]{:S(2)}) collective-permute-start(bf16[8,32,512]{2,1,0:T(8,128)(2,1)S(1)} %get-tuple-element.12), channel_id=1, source_target_pairs={{1,0},{2,1},{3,2},{4,3},{5,4},{6,5},{7,6},{8,7},{9,8},{10,9},{11,1... | collective-permute-start | bytes 786440 | tf_op jit(solution)/shard_map/ppermute | solution.py:263
  64.0 3.5 %all-to-all-start.1 = ((bf16[4,64,1024]{2,1,0:T(8,128)(2,1)}), bf16[4,64,1024]{2,1,0:T(8,128)(2,1)S(1)}, u32[]{:S(2)}, u32[]{:S(2)}) async-start(bf16[4,64,1024]{2,1,0:T(8,128)(2,1)} %get-tuple-element.10), calls=%async_computation.1 | async-start | bytes 1048576 | tf_op jit(solution)/shard_map/all_to_all | solution.py:241
  67.5 0.3 collective-permute-done.3
  67.9 0.1 add_convert_fusion
  68.0 8.0 %all-to-all-done.1.dq_ref = bf16[4,64,1024]{2,1,0:T(8,128)(2,1)S(1)} async-done(((bf16[4,64,1024]{2,1,0:T(8,128)(2,1)}), bf16[4,64,1024]{2,1,0:T(8,128)(2,1)S(1)}, u32[]{:S(2)}, u32[]{:S(2)}) %all-to-all-start.1) | async-done | bytes 524320 | tf_op jit(solution)/shard_map/all_to_all | solution.py:241
  76.0 22.8 %all_to_all.15.dkv_ref = bf16[8,64,512]{2,1,0:T(8,128)(2,1)S(1)} all-to-all(bf16[8,64,512]{2,1,0:T(8,128)(2,1)S(1)} %pad_maximum_fusion), channel_id=1, replica_groups=mesh['head'=8,'blk'=64] {'head'}, dimensions={0} | all-to-all | bytes 1048576 | tf_op jit(solution)/shard_map/all_to_all | solution.py:267
  98.7 0.9 shard_map.79
  (12 shorter events, 0.1 us)
Async XLA Ops:
  3.1 4.3 %copy-start = (s32[512]{0:T(512)S(1)}, s32[512]{0:T(512)}, u32[]{:S(2)}) copy-start(s32[512]{0:T(512)} %param.9) | copy-start | bytes 6148
  3.1 22.2 %all-to-all-start = ((bf16[4,64,2560]{2,1,0:T(8,128)(2,1)}), bf16[4,64,2560]{2,1,0:T(8,128)(2,1)S(1)}, u32[]{:S(2)}, u32[]{:S(2)}) async-start(bf16[4,64,2560]{2,1,0:T(8,128)(2,1)} %shard_map.76), calls=%async_computation | async-start | bytes 2621440 | tf_op jit(solution)/shard_map/all_to_all | solution.py:241
  25.3 17.9 %collective-permute-start = (bf16[4,64,512]{2,1,0:T(8,128)(2,1)S(1)}, bf16[4,64,512]{2,1,0:T(8,128)(2,1)S(1)}, u32[]{:S(2)}, u32[]{:S(2)}) collective-permute-start(bf16[4,64,512]{2,1,0:T(8,128)(2,1)S(1)} %slice.42), channel_id=1, source_target_pairs={{0,256},{64,320},{128,384},{192,448},{256,0},{320,64},{384,128},{4... | collective-permute-start | bytes 786440 | tf_op jit(solution)/shard_map/ppermute | solution.py:244
  32.6 20.3 %collective-permute-start.1 = (bf16[4,32,512]{2,1,0:T(8,128)(2,1)S(1)}, bf16[4,32,512]{2,1,0:T(8,128)(2,1)S(1)}, u32[]{:S(2)}, u32[]{:S(2)}) collective-permute-start(bf16[4,32,512]{2,1,0:T(8,128)(2,1)S(1)} %slice.43), channel_id=1, source_target_pairs={{0,1},{1,2},{2,3},{3,4},{4,5},{5,6},{6,7},{7,8},{8,9},{9,10},{10,1... | collective-permute-start | bytes 393224 | tf_op jit(solution)/shard_map/ppermute | solution.py:245
  43.2 12.0 %collective-permute-start.2 = (bf16[4,32,512]{2,1,0:T(8,128)(2,1)S(1)}, bf16[4,32,512]{2,1,0:T(8,128)(2,1)S(1)}, u32[]{:S(2)}, u32[]{:S(2)}) collective-permute-start(bf16[4,32,512]{2,1,0:T(8,128)(2,1)S(1)} %slice.44), channel_id=1, source_target_pairs={{0,1},{1,2},{2,3},{3,4},{4,5},{5,6},{6,7},{7,8},{8,9},{9,10},{10,1... | collective-permute-start | bytes 393224 | tf_op jit(solution)/shard_map/ppermute | solution.py:246
  60.2 7.7 %collective-permute-start.3 = (bf16[8,32,512]{2,1,0:T(8,128)(2,1)S(1)}, bf16[8,32,512]{2,1,0:T(8,128)(2,1)S(1)}, u32[]{:S(2)}, u32[]{:S(2)}) collective-permute-start(bf16[8,32,512]{2,1,0:T(8,128)(2,1)S(1)} %get-tuple-element.12), channel_id=1, source_target_pairs={{1,0},{2,1},{3,2},{4,3},{5,4},{6,5},{7,6},{8,7},{9,8},{10,9},{11,1... | collective-permute-start | bytes 786440 | tf_op jit(solution)/shard_map/ppermute | solution.py:263
  64.0 12.0 %all-to-all-start.1 = ((bf16[4,64,1024]{2,1,0:T(8,128)(2,1)}), bf16[4,64,1024]{2,1,0:T(8,128)(2,1)S(1)}, u32[]{:S(2)}, u32[]{:S(2)}) async-start(bf16[4,64,1024]{2,1,0:T(8,128)(2,1)} %get-tuple-element.10), calls=%async_computation.1 | async-start | bytes 1048576 | tf_op jit(solution)/shard_map/all_to_all | solution.py:241

commit v6 on v3

--- a/solution.py
+++ b/solution.py
@@ -19,9 +19,7 @@
     )
 
 
-def attention_kernel(
-    team_ref, qpos_ref, kpos_ref, qg_ref, own_ref, far_ref, pown_ref, pfar_ref, dq_ref, dkv_ref, dprev_ref
-):
+def attention_kernel(qpos_ref, kpos_ref, qg_ref, kv_ref, prev_ref, dq_ref, dkv_ref, dprev_ref):
     half = qg_ref.shape[1] // 2
     slots = qg_ref.shape[0]
     rows = slots * half
@@ -67,10 +65,16 @@
     for kv in range(KV):
         parts = []
         for column in (kv * HD, (KV + kv) * HD):
-            early = [columns(ref, 0, half, column) for ref in (own_ref, far_ref)]
-            late = [columns(ref, half, 2 * half, column) for ref in (own_ref, far_ref)]
-            before = [columns(ref, 0, half, column) for ref in (pown_ref, pfar_ref)]
-            parts.append(jnp.concatenate(early + late + before, axis=0))
+            parts.append(
+                jnp.concatenate(
+                    [
+                        columns(kv_ref, 0, half, column),
+                        columns(kv_ref, half, 2 * half, column),
+                        columns(prev_ref, 0, half, column),
+                    ],
+                    axis=0,
+                )
+            )
         key, value = parts
         key_sum = None
         value_sum = None
@@ -99,60 +103,51 @@
             value_sum = dv if value_sum is None else value_sum + dv
         for total, column in ((key_sum, kv * HD), (value_sum, (KV + kv) * HD)):
             low = total.astype(jnp.bfloat16)
-            for side in range(2):
-                first = pl.multiple_of(jnp.bitwise_xor(team_ref[0], side) * slots, slots)
-                target = pl.ds(first, slots)
-                for kind in range(3):
-                    top = kind * keys + side * rows
-                    block = low[top : top + rows].reshape(slots, half, HD)
-                    if kind < 2:
-                        dkv_ref[target, kind * half : (kind + 1) * half, column : column + HD] = block
-                    else:
-                        dprev_ref[target, :, column : column + HD] = block
-
-
-def attention(team, qpos, kpos, qg, own, far, pown, pfar):
+            for kind in range(3):
+                block = low[kind * keys : (kind + 1) * keys].reshape(2 * slots, half, HD)
+                if kind < 2:
+                    dkv_ref[:, kind * half : (kind + 1) * half, column : column + HD] = block
+                else:
+                    dprev_ref[:, :, column : column + HD] = block
+
+
+def attention(qpos, kpos, qg, kv, prev):
     slots, tok, _ = qg.shape
-    lines = own.shape[2]
     return pl.pallas_call(
         attention_kernel,
         out_shape=(
             jax.ShapeDtypeStruct((slots, tok, KV * GROUP * HD), jnp.bfloat16),
-            jax.ShapeDtypeStruct((2 * slots, tok, lines), jnp.bfloat16),
-            jax.ShapeDtypeStruct((2 * slots, tok // 2, lines), jnp.bfloat16),
+            jax.ShapeDtypeStruct(kv.shape, jnp.bfloat16),
+            jax.ShapeDtypeStruct(prev.shape, jnp.bfloat16),
         ),
-        in_specs=[pl.BlockSpec(memory_space=pltpu.SMEM)] + [pl.BlockSpec()] * 7,
         compiler_params=pltpu.CompilerParams(vmem_limit_bytes=48 * 1024 * 1024),
-    )(team, qpos, kpos, qg, own, far, pown, pfar)
-
-
-def pack_kernel(first_ref, second_ref, out_ref, sems):
-    wide = out_ref.shape[2] // 2
-    copies = []
-    for x in range(XN):
-        for i, ref in enumerate((first_ref, second_ref)):
-            copies.append(
-                pltpu.make_async_copy(
-                    ref.at[:, x * wide : (x + 1) * wide],
-                    out_ref.at[x, :, i * wide : (i + 1) * wide],
-                    sems.at[2 * x + i],
-                )
-            )
+    )(qpos, kpos, qg, kv, prev)
+
+
+def pack_kernel(first_ref, second_ref, out_ref, first_buf, second_buf, sems):
+    pairs = ((first_ref, first_buf), (second_ref, second_buf))
+    copies = [pltpu.make_async_copy(ref, buf, sems.at[i]) for i, (ref, buf) in enumerate(pairs)]
     for copy in copies:
         copy.start()
-    for copy in copies:
-        copy.wait()
-
-
-def pack(first, second):
-    tok, columns = first.shape
-    anywhere = pl.BlockSpec(memory_space=pl.ANY)
+    wide = out_ref.shape[2] // 2
+    for i, (_, buf) in enumerate(pairs):
+        copies[i].wait()
+        for block in range(out_ref.shape[0]):
+            x = block % XN
+            out_ref[block, :, i * wide : (i + 1) * wide] = buf[:, x * wide : (x + 1) * wide]
+
+
+def pack(blocks, first, second):
+    tok, total = first.shape
     return pl.pallas_call(
         pack_kernel,
-        out_shape=jax.ShapeDtypeStruct((XN, tok, 2 * columns // XN), first.dtype),
-        in_specs=[anywhere, anywhere],
-        out_specs=anywhere,
-        scratch_shapes=[pltpu.SemaphoreType.DMA((2 * XN,))],
+        out_shape=jax.ShapeDtypeStruct((blocks, tok, 2 * total // XN), first.dtype),
+        in_specs=[pl.BlockSpec(memory_space=pl.ANY)] * 2,
+        scratch_shapes=[
+            pltpu.VMEM(first.shape, first.dtype),
+            pltpu.VMEM(second.shape, second.dtype),
+            pltpu.SemaphoreType.DMA((2,)),
+        ],
     )(first, second)
 
 
@@ -188,34 +183,35 @@
     teams = [list(range(t, t + XN)) for t in range(0, groups, XN)]
     ahead = [(i, (i + 1) % cycle) for i in range(cycle)]
     behind = [(j, i) for i, j in ahead]
-    across = [(h, (h + XN) % groups) for h in range(groups)]
+
     def team_exchange(array):
         return lax.all_to_all(array, "head", 0, 0, tiled=True, axis_index_groups=teams)
 
-    own = team_exchange(pack(keys, values))
-    far = lax.ppermute(own, "head", across)
-    pown = lax.ppermute(own[:, :half], "blk", ahead)
-    qg = team_exchange(pack(queries, grad_out))
-    pfar = lax.ppermute(far[:, :half], "blk", ahead)
-
-    team = lax.axis_index("head") // XN
+    def exchange(array):
+        return lax.all_to_all(array, "head", 0, 0, tiled=True)
+
+    kv = exchange(pack(groups, keys, values))
+    prev = lax.ppermute(kv[:, :half], "blk", ahead)
+    qg = pack(XN, queries, grad_out)
+    qg, kv = lax.optimization_barrier((qg, kv))
+    qg = team_exchange(qg)
+
     places = lax.dynamic_index_in_dim(order.reshape(groups, cycle), mine, axis=1, keepdims=False)
-    places = jnp.where(team == 0, places, jnp.roll(places, -XN))
     offset = lax.iota(jnp.int32, half)
     early = (places[:, None] * half + offset[None, :]).reshape(groups * half)
     late = ((2 * slot_total - 1 - places)[:, None] * half + offset[None, :]).reshape(groups * half)
     kpos = jnp.stack([early, late], axis=1)
-    qpos = jnp.stack([jnp.tile(p[: XN * half], 2) for p in (early, late)], axis=0)
-
-    sides = jnp.full((1,), team, jnp.int32)
-    dq, dkv, dprev = attention(sides, qpos, kpos, qg, own, far, pown, pfar)
+    team = lax.axis_index("head") // XN
+    here = [lax.dynamic_slice_in_dim(p, team * XN * half, XN * half) for p in (early, late)]
+    qpos = jnp.stack([jnp.tile(p, 2) for p in here], axis=0)
+
+    dq, dkv, dprev = attention(qpos, kpos, qg, kv, prev)
 
     back = lax.ppermute(dprev, "blk", behind)
     dq = team_exchange(dq)
     front = (dkv[:, :half].astype(jnp.float32) + back.astype(jnp.float32)).astype(jnp.bfloat16)
     dkv = jnp.concatenate([front, dkv[:, half:]], axis=1)
-    dkv = lax.all_to_all(dkv, "head", 0, 0, tiled=True)
-    return unpack(dq, dkv)
+    return unpack(dq, exchange(dkv))
 
 
 def solution(mesh):

time: 130 us -> 92 us (0.71)
  the two profiles are of different devices: /device:TPU:8 before, /device:TPU:16 now
where the time goes in v6:
time: 92 us; the launch traced here: 91.5 us
  waiting for transfers between devices  36.7 us (40%)
  starting transfers between devices  25.7 us (28%)
  blocking collectives  14.9 us (16%)
  Pallas kernels  11.6 us (13%)
  local copies, waits for them, and re-layouts  1.39 us (2%)
    all_to_all x1, waiting for transfers between devices, exchange(): return lax.all_to_all(array, 'head', 0, 0, tiled=True)  16.9 us
    all_to_all x1, blocking collectives, exchange(): return lax.all_to_all(array, 'head', 0, 0, tiled=True)  14.9 us
    ppermute x1, waiting for transfers between devices, body(): prev = lax.ppermute(kv[:, :half], 'blk', ahead)  11.6 us
    ppermute x1, starting transfers between devices, body(): back = lax.ppermute(dprev, 'blk', behind)  9.01 us
    all_to_all x2, waiting for transfers between devices, team_exchange(): lax.all_to_all(array, 'head', 0, 0, tiled=True, axis_index_groups=teams)  7.9 us
    all_to_all x1, starting transfers between devices, exchange(): return lax.all_to_all(array, 'head', 0, 0, tiled=True)  7.78 us
    all_to_all x2, starting transfers between devices, team_exchange(): lax.all_to_all(array, 'head', 0, 0, tiled=True, axis_index_groups=teams)  7 us
    pallas_call x1, Pallas kernels, attention(): pl.pallas_call(attention_kernel, out_shape=(jax.ShapeDtypeStruct((slots,...  6.63 us
  transfers between devices with their start and end apart: 5, of which 4 were waited for; matrix products, arithmetic and copies ran while one was open for 1% of the time, Pallas kernels for 2%

profile of v6, /device:TPU:16, one launch (start us, length us, event | category | flops | bytes accessed | tf_op | source)
XLA Modules:
  0.0 91.5 jit_solution(16010136905402590927)
XLA Ops:
  0.6 1.8 %shard_map.77 = bf16[8,64,512]{2,1,0:T(8,128)(2,1)} custom-call(bf16[64,1024]{1,0:T(8,128)(2,1)} %first_ref.3, bf16[64,1024]{1,0:T(8,128)(2,1)} %second_ref.3), custom_call_target="tpu_custom_call" | custom-call | tf_op jit(solution)/shard_map/pallas_call | solution.py:142
  2.4 7.8 %all-to-all-start = ((bf16[8,64,512]{2,1,0:T(8,128)(2,1)}), bf16[8,64,512]{2,1,0:T(8,128)(2,1)S(1)}, u32[]{:S(2)}, u32[]{:S(2)}) async-start(bf16[8,64,512]{2,1,0:T(8,128)(2,1)} %shard_map.77), calls=%async_computation | async-start | bytes 1048576 | tf_op jit(solution)/shard_map/all_to_all | solution.py:191
  10.2 2.2 %shard_map.76 = bf16[4,64,2048]{2,1,0:T(8,128)(2,1)} custom-call(bf16[64,4096]{1,0:T(8,128)(2,1)} %first_ref.2, bf16[64,4096]{1,0:T(8,128)(2,1)} %second_ref.2), custom_call_target="tpu_custom_call" | custom-call | tf_op jit(solution)/shard_map/pallas_call | solution.py:142
  12.4 16.9 %all-to-all-done.kv_ref = bf16[8,64,512]{2,1,0:T(8,128)(2,1)S(1)} async-done(((bf16[8,64,512]{2,1,0:T(8,128)(2,1)}), bf16[8,64,512]{2,1,0:T(8,128)(2,1)S(1)}, u32[]{:S(2)}, u32[]{:S(2)}) %all-to-all-start) | async-done | bytes 524320 | tf_op jit(solution)/shard_map/all_to_all | solution.py:191
  29.3 3.5 %all-to-all-start.1 = ((bf16[4,64,2048]{2,1,0:T(8,128)(2,1)}), bf16[4,64,2048]{2,1,0:T(8,128)(2,1)S(1)}, u32[]{:S(2)}, u32[]{:S(2)}) async-start(bf16[4,64,2048]{2,1,0:T(8,128)(2,1)} %shard_map.76), calls=%async_computation.1 | async-start | bytes 2097152 | tf_op jit(solution)/shard_map/all_to_all | solution.py:188
  32.8 0.0 copy-start
  32.8 0.7 copy-done
  33.5 0.1 reshape.64
  33.6 0.2 multiply_reduce_fusion.1
  33.8 1.9 %collective-permute-start = (bf16[8,32,512]{2,1,0:T(8,128)(2,1)S(1)}, bf16[8,32,512]{2,1,0:T(8,128)(2,1)S(1)}, u32[]{:S(2)}, u32[]{:S(2)}) collective-permute-start(bf16[8,32,512]{2,1,0:T(8,128)(2,1)S(1)} %slice.12), channel_id=1, source_target_pairs={{0,1},{1,2},{2,3},{3,4},{4,5},{5,6},{6,7},{7,8},{8,9},{9,10},{10,1... | collective-permute-start | bytes 786440 | tf_op jit(solution)/shard_map/ppermute | solution.py:194
  35.7 0.1 iota_add_fusion
  35.8 0.1 add.83
  35.9 0.1 add.81
  36.0 0.1 add.82
  36.0 0.1 add.75
  36.1 0.1 dynamic_slice.12
  36.2 0.1 dynamic_slice.11
  36.3 0.1 copy.12.kpos_ref
  36.5 11.6 %collective-permute-done.prev_ref = bf16[8,32,512]{2,1,0:T(8,128)(2,1)S(1)} collective-permute-done((bf16[8,32,512]{2,1,0:T(8,128)(2,1)S(1)}, bf16[8,32,512]{2,1,0:T(8,128)(2,1)S(1)}, u32[]{:S(2)}, u32[]{:S(2)}) %collective-permute-start) | collective-permute-done | bytes 262176 | tf_op jit(solution)/shard_map/ppermute | solution.py:194
  48.1 0.0 all-to-all-done.1.qg_ref
  48.1 6.6 %shard_map.78 = (bf16[4,64,1024]{2,1,0:T(8,128)(2,1)}, bf16[8,64,512]{2,1,0:T(8,128)(2,1)S(1)}, bf16[8,32,512]{2,1,0:T(8,128)(2,1)S(1)}) custom-call(s32[2,256]{1,0:T(2,128)S(1)} %pad_add_fusion.qpos_ref, s32[256,2]{1,0:T(8,128)S(1)} %copy.12.kpos_ref, bf16[4,64,2048]{2,1,0:T(8,128)(2,1)S(1)} %all-to-all-done.1.qg_ref, ...), custom_call_target="tpu_custom_call" | custom-call | tf_op jit(solution)/shard_map/pallas_call | solution.py:116
  54.7 9.0 %collective-permute-start.1 = (bf16[8,32,512]{2,1,0:T(8,128)(2,1)S(1)}, bf16[8,32,512]{2,1,0:T(8,128)(2,1)S(1)}, u32[]{:S(2)}, u32[]{:S(2)}) collective-permute-start(bf16[8,32,512]{2,1,0:T(8,128)(2,1)S(1)} %get-tuple-element.12), channel_id=1, source_target_pairs={{1,0},{2,1},{3,2},{4,3},{5,4},{6,5},{7,6},{8,7},{9,8},{10,9},{11,1... | collective-permute-start | bytes 786440 | tf_op jit(solution)/shard_map/ppermute | solution.py:210
  63.7 3.5 %all-to-all-start.2 = ((bf16[4,64,1024]{2,1,0:T(8,128)(2,1)}), bf16[4,64,1024]{2,1,0:T(8,128)(2,1)S(1)}, u32[]{:S(2)}, u32[]{:S(2)}) async-start(bf16[4,64,1024]{2,1,0:T(8,128)(2,1)} %get-tuple-element.10), calls=%async_computation.2 | async-start | bytes 1048576 | tf_op jit(solution)/shard_map/all_to_all | solution.py:188
  67.3 0.3 collective-permute-done.1
  67.6 0.1 add_convert_fusion
  67.7 7.9 %all-to-all-done.2.dq_ref = bf16[4,64,1024]{2,1,0:T(8,128)(2,1)S(1)} async-done(((bf16[4,64,1024]{2,1,0:T(8,128)(2,1)}), bf16[4,64,1024]{2,1,0:T(8,128)(2,1)S(1)}, u32[]{:S(2)}, u32[]{:S(2)}) %all-to-all-start.2) | async-done | bytes 524320 | tf_op jit(solution)/shard_map/all_to_all | solution.py:188
  75.6 14.9 %all_to_all.20.dkv_ref = bf16[8,64,512]{2,1,0:T(8,128)(2,1)S(1)} all-to-all(bf16[8,64,512]{2,1,0:T(8,128)(2,1)S(1)} %pad_maximum_fusion), channel_id=1, replica_groups=mesh['head'=8,'blk'=64] {'head'}, dimensions={0} | all-to-all | bytes 1048576 | tf_op jit(solution)/shard_map/all_to_all | solution.py:191
  90.6 0.9 %shard_map.79 = (bf16[64,4096]{1,0:T(8,128)(2,1)}, bf16[64,1024]{1,0:T(8,128)(2,1)}, bf16[64,1024]{1,0:T(8,128)(2,1)}) custom-call(bf16[4,64,1024]{2,1,0:T(8,128)(2,1)S(1)} %all-to-all-done.2.dq_ref, bf16[8,64,512]{2,1,0:T(8,128)(2,1)S(1)} %all_to_all.20.dkv_ref), custom_call_target="tpu_custom_call" | custom-call | tf_op jit(solution)/shard_map/pallas_call | solution.py:169
  (7 shorter events, 0.1 us)
Async XLA Ops:
  2.4 26.9 %all-to-all-start = ((bf16[8,64,512]{2,1,0:T(8,128)(2,1)}), bf16[8,64,512]{2,1,0:T(8,128)(2,1)S(1)}, u32[]{:S(2)}, u32[]{:S(2)}) async-start(bf16[8,64,512]{2,1,0:T(8,128)(2,1)} %shard_map.77), calls=%async_computation | async-start | bytes 1048576 | tf_op jit(solution)/shard_map/all_to_all | solution.py:191
  29.3 18.8 %all-to-all-start.1 = ((bf16[4,64,2048]{2,1,0:T(8,128)(2,1)}), bf16[4,64,2048]{2,1,0:T(8,128)(2,1)S(1)}, u32[]{:S(2)}, u32[]{:S(2)}) async-start(bf16[4,64,2048]{2,1,0:T(8,128)(2,1)} %shard_map.76), calls=%async_computation.1 | async-start | bytes 2097152 | tf_op jit(solution)/shard_map/all_to_all | solution.py:188
  32.8 0.7 copy-start
  33.8 14.3 %collective-permute-start = (bf16[8,32,512]{2,1,0:T(8,128)(2,1)S(1)}, bf16[8,32,512]{2,1,0:T(8,128)(2,1)S(1)}, u32[]{:S(2)}, u32[]{:S(2)}) collective-permute-start(bf16[8,32,512]{2,1,0:T(8,128)(2,1)S(1)} %slice.12), channel_id=1, source_target_pairs={{0,1},{1,2},{2,3},{3,4},{4,5},{5,6},{6,7},{7,8},{8,9},{9,10},{10,1... | collective-permute-start | bytes 786440 | tf_op jit(solution)/shard_map/ppermute | solution.py:194
  54.7 12.9 %collective-permute-start.1 = (bf16[8,32,512]{2,1,0:T(8,128)(2,1)S(1)}, bf16[8,32,512]{2,1,0:T(8,128)(2,1)S(1)}, u32[]{:S(2)}, u32[]{:S(2)}) collective-permute-start(bf16[8,32,512]{2,1,0:T(8,128)(2,1)S(1)} %get-tuple-element.12), channel_id=1, source_target_pairs={{1,0},{2,1},{3,2},{4,3},{5,4},{6,5},{7,6},{8,7},{9,8},{10,9},{11,1... | collective-permute-start | bytes 786440 | tf_op jit(solution)/shard_map/ppermute | solution.py:210
  63.7 11.9 %all-to-all-start.2 = ((bf16[4,64,1024]{2,1,0:T(8,128)(2,1)}), bf16[4,64,1024]{2,1,0:T(8,128)(2,1)S(1)}, u32[]{:S(2)}, u32[]{:S(2)}) async-start(bf16[4,64,1024]{2,1,0:T(8,128)(2,1)} %get-tuple-element.10), calls=%async_computation.2 | async-start | bytes 1048576 | tf_op jit(solution)/shard_map/all_to_all | solution.py:188

commit v7 on v6

--- a/solution.py
+++ b/solution.py
@@ -151,6 +151,21 @@
     )(first, second)
 
 
+def add_kernel(dkv_ref, back_ref, out_ref):
+    half = back_ref.shape[1]
+    total = dkv_ref[:, :half].astype(jnp.float32) + back_ref[...].astype(jnp.float32)
+    out_ref[:, :half] = total.astype(out_ref.dtype)
+    out_ref[:, half:] = dkv_ref[:, half:]
+
+
+def add_back(dkv, back):
+    return pl.pallas_call(
+        add_kernel,
+        out_shape=jax.ShapeDtypeStruct(dkv.shape, dkv.dtype),
+        compiler_params=pltpu.CompilerParams(vmem_limit_bytes=16 * 1024 * 1024),
+    )(dkv, back)
+
+
 def unpack_kernel(dq_ref, dkv_ref, query_ref, key_ref, value_ref):
     wide = dq_ref.shape[2]
     lines = KV * HD
@@ -209,8 +224,8 @@
 
     back = lax.ppermute(dprev, "blk", behind)
     dq = team_exchange(dq)
-    front = (dkv[:, :half].astype(jnp.float32) + back.astype(jnp.float32)).astype(jnp.bfloat16)
-    dkv = jnp.concatenate([front, dkv[:, half:]], axis=1)
+    dq, back = lax.optimization_barrier((dq, back))
+    dkv = add_back(dkv, back)
     return unpack(dq, exchange(dkv))
 
 

time: 92 us -> 91.3 us (level)
  waiting for transfers between devices: 36.7 us -> 34.3 us
  blocking collectives: 14.9 us -> 16.8 us
    all_to_all x2, waiting for transfers between devices: 7.9 us -> 0.01 us  [team_exchange(): lax.all_to_all(array, 'head', 0, 0, tiled=True, axis_index_groups=teams)]
    ppermute x1, waiting for transfers between devices: 0.35 us -> 5.8 us  [body(): back = lax.ppermute(dprev, 'blk', behind)]
    all_to_all x1, blocking collectives: 14.9 us -> 16.8 us  [exchange(): return lax.all_to_all(array, 'head', 0, 0, tiled=True)]
    all_to_all x2, starting transfers between devices: 7 us -> 7.99 us  [team_exchange(): lax.all_to_all(array, 'head', 0, 0, tiled=True, axis_index_groups=teams)]
    ppermute x1, starting transfers between devices: 9.01 us -> 8.03 us  [body(): back = lax.ppermute(dprev, 'blk', behind)]
  transfers between devices with their start and end apart: 5 -> 5, of which waited for: 4 -> 3; matrix products, arithmetic and copies ran while one was open for 1% -> 1% of each run, Pallas kernels for 2% -> 2%
where the time goes in v7:
time: 91.3 us; the launch traced here: 90.9 us
  waiting for transfers between devices  34.3 us (38%)
  starting transfers between devices  25.7 us (28%)
  blocking collectives  16.8 us (18%)
  Pallas kernels  11.6 us (13%)
  local copies, waits for them, and re-layouts  1.37 us (2%)
    all_to_all x1, waiting for transfers between devices, exchange(): return lax.all_to_all(array, 'head', 0, 0, tiled=True)  16.9 us
    all_to_all x1, blocking collectives, exchange(): return lax.all_to_all(array, 'head', 0, 0, tiled=True)  16.8 us
    ppermute x1, waiting for transfers between devices, body(): prev = lax.ppermute(kv[:, :half], 'blk', ahead)  11.6 us
    ppermute x1, starting transfers between devices, body(): back = lax.ppermute(dprev, 'blk', behind)  8.03 us
    all_to_all x2, starting transfers between devices, team_exchange(): lax.all_to_all(array, 'head', 0, 0, tiled=True, axis_index_groups=teams)  7.99 us
    all_to_all x1, starting transfers between devices, exchange(): return lax.all_to_all(array, 'head', 0, 0, tiled=True)  7.78 us
    pallas_call x1, Pallas kernels, attention(): pl.pallas_call(attention_kernel, out_shape=(jax.ShapeDtypeStruct((slots,...  6.63 us
    ppermute x1, waiting for transfers between devices, body(): back = lax.ppermute(dprev, 'blk', behind)  5.8 us
  transfers between devices with their start and end apart: 5, of which 3 were waited for; matrix products, arithmetic and copies ran while one was open for 1% of the time, Pallas kernels for 2%

profile of v7, /device:TPU:16, one launch (start us, length us, event | category | flops | bytes accessed | tf_op | source)
XLA Modules:
  0.0 90.9 jit_solution(1580647548952345228)
XLA Ops:
  0.6 1.8 %shard_map.77 = bf16[8,64,512]{2,1,0:T(8,128)(2,1)} custom-call(bf16[64,1024]{1,0:T(8,128)(2,1)} %first_ref.3, bf16[64,1024]{1,0:T(8,128)(2,1)} %second_ref.3), custom_call_target="tpu_custom_call" | custom-call | tf_op jit(solution)/shard_map/pallas_call | solution.py:142
  2.4 7.8 %all-to-all-start = ((bf16[8,64,512]{2,1,0:T(8,128)(2,1)}), bf16[8,64,512]{2,1,0:T(8,128)(2,1)S(1)}, u32[]{:S(2)}, u32[]{:S(2)}) async-start(bf16[8,64,512]{2,1,0:T(8,128)(2,1)} %shard_map.77), calls=%async_computation | async-start | bytes 1048576 | tf_op jit(solution)/shard_map/all_to_all | solution.py:206
  10.2 2.2 %shard_map.76 = bf16[4,64,2048]{2,1,0:T(8,128)(2,1)} custom-call(bf16[64,4096]{1,0:T(8,128)(2,1)} %first_ref.2, bf16[64,4096]{1,0:T(8,128)(2,1)} %second_ref.2), custom_call_target="tpu_custom_call" | custom-call | tf_op jit(solution)/shard_map/pallas_call | solution.py:142
  12.4 16.9 %all-to-all-done.kv_ref = bf16[8,64,512]{2,1,0:T(8,128)(2,1)S(1)} async-done(((bf16[8,64,512]{2,1,0:T(8,128)(2,1)}), bf16[8,64,512]{2,1,0:T(8,128)(2,1)S(1)}, u32[]{:S(2)}, u32[]{:S(2)}) %all-to-all-start) | async-done | bytes 524320 | tf_op jit(solution)/shard_map/all_to_all | solution.py:206
  29.3 3.5 %all-to-all-start.1 = ((bf16[4,64,2048]{2,1,0:T(8,128)(2,1)}), bf16[4,64,2048]{2,1,0:T(8,128)(2,1)S(1)}, u32[]{:S(2)}, u32[]{:S(2)}) async-start(bf16[4,64,2048]{2,1,0:T(8,128)(2,1)} %shard_map.76), calls=%async_computation.1 | async-start | bytes 2097152 | tf_op jit(solution)/shard_map/all_to_all | solution.py:203
  32.8 0.0 copy-start
  32.8 0.7 copy-done
  33.5 0.1 reshape.64
  33.6 0.2 multiply_reduce_fusion.1
  33.8 1.9 %collective-permute-start = (bf16[8,32,512]{2,1,0:T(8,128)(2,1)S(1)}, bf16[8,32,512]{2,1,0:T(8,128)(2,1)S(1)}, u32[]{:S(2)}, u32[]{:S(2)}) collective-permute-start(bf16[8,32,512]{2,1,0:T(8,128)(2,1)S(1)} %slice.4), channel_id=1, source_target_pairs={{0,1},{1,2},{2,3},{3,4},{4,5},{5,6},{6,7},{7,8},{8,9},{9,10},{10,1... | collective-permute-start | bytes 786440 | tf_op jit(solution)/shard_map/ppermute | solution.py:209
  35.7 0.1 iota_add_fusion
  35.8 0.1 add.80
  35.9 0.1 add.78
  36.0 0.1 add.79
  36.0 0.1 add.72
  36.1 0.1 dynamic_slice.12
  36.2 0.1 dynamic_slice.11
  36.3 0.1 copy.12.kpos_ref
  36.5 11.6 %collective-permute-done.prev_ref = bf16[8,32,512]{2,1,0:T(8,128)(2,1)S(1)} collective-permute-done((bf16[8,32,512]{2,1,0:T(8,128)(2,1)S(1)}, bf16[8,32,512]{2,1,0:T(8,128)(2,1)S(1)}, u32[]{:S(2)}, u32[]{:S(2)}) %collective-permute-start) | collective-permute-done | bytes 262176 | tf_op jit(solution)/shard_map/ppermute | solution.py:209
  48.1 0.0 all-to-all-done.1.qg_ref
  48.1 6.6 %shard_map.78 = (bf16[4,64,1024]{2,1,0:T(8,128)(2,1)}, bf16[8,64,512]{2,1,0:T(8,128)(2,1)S(1)}, bf16[8,32,512]{2,1,0:T(8,128)(2,1)S(1)}) custom-call(s32[2,256]{1,0:T(2,128)S(1)} %pad_add_fusion.qpos_ref, s32[256,2]{1,0:T(8,128)S(1)} %copy.12.kpos_ref, bf16[4,64,2048]{2,1,0:T(8,128)(2,1)S(1)} %all-to-all-done.1.qg_ref, ...), custom_call_target="tpu_custom_call" | custom-call | tf_op jit(solution)/shard_map/pallas_call | solution.py:116
  54.7 4.5 %all-to-all-start.2 = ((bf16[4,64,1024]{2,1,0:T(8,128)(2,1)}), bf16[4,64,1024]{2,1,0:T(8,128)(2,1)S(1)}, u32[]{:S(2)}, u32[]{:S(2)}) async-start(bf16[4,64,1024]{2,1,0:T(8,128)(2,1)} %get-tuple-element.12), calls=%async_computation.2 | async-start | bytes 1048576 | tf_op jit(solution)/shard_map/all_to_all | solution.py:203
  59.2 8.0 %collective-permute-start.1 = (bf16[8,32,512]{2,1,0:T(8,128)(2,1)S(1)}, bf16[8,32,512]{2,1,0:T(8,128)(2,1)S(1)}, u32[]{:S(2)}, u32[]{:S(2)}) collective-permute-start(bf16[8,32,512]{2,1,0:T(8,128)(2,1)S(1)} %get-tuple-element.13), channel_id=1, source_target_pairs={{1,0},{2,1},{3,2},{4,3},{5,4},{6,5},{7,6},{8,7},{9,8},{10,9},{11,1... | collective-permute-start | bytes 786440 | tf_op jit(solution)/shard_map/ppermute | solution.py:225
  67.2 5.8 %collective-permute-done.1.back_ref = bf16[8,32,512]{2,1,0:T(8,128)(2,1)S(1)} collective-permute-done((bf16[8,32,512]{2,1,0:T(8,128)(2,1)S(1)}, bf16[8,32,512]{2,1,0:T(8,128)(2,1)S(1)}, u32[]{:S(2)}, u32[]{:S(2)}) %collective-permute-start.1) | collective-permute-done | bytes 262176 | tf_op jit(solution)/shard_map/ppermute | solution.py:225
  73.0 0.0 all-to-all-done.2.dq_ref
  73.0 0.1 shard_map.79
  73.1 16.8 %all_to_all.20.dkv_ref = bf16[8,64,512]{2,1,0:T(8,128)(2,1)S(1)} all-to-all(bf16[8,64,512]{2,1,0:T(8,128)(2,1)S(1)} %shard_map.79), channel_id=1, replica_groups=mesh['head'=8,'blk'=64] {'head'}, dimensions={0} | all-to-all | bytes 1048576 | tf_op jit(solution)/shard_map/all_to_all | solution.py:206
  89.9 0.9 %shard_map.80 = (bf16[64,4096]{1,0:T(8,128)(2,1)}, bf16[64,1024]{1,0:T(8,128)(2,1)}, bf16[64,1024]{1,0:T(8,128)(2,1)}) custom-call(bf16[4,64,1024]{2,1,0:T(8,128)(2,1)S(1)} %all-to-all-done.2.dq_ref, bf16[8,64,512]{2,1,0:T(8,128)(2,1)S(1)} %all_to_all.20.dkv_ref), custom_call_target="tpu_custom_call" | custom-call | tf_op jit(solution)/shard_map/pallas_call | solution.py:184
  (5 shorter events, 0.0 us)
Async XLA Ops:
  2.4 26.9 %all-to-all-start = ((bf16[8,64,512]{2,1,0:T(8,128)(2,1)}), bf16[8,64,512]{2,1,0:T(8,128)(2,1)S(1)}, u32[]{:S(2)}, u32[]{:S(2)}) async-start(bf16[8,64,512]{2,1,0:T(8,128)(2,1)} %shard_map.77), calls=%async_computation | async-start | bytes 1048576 | tf_op jit(solution)/shard_map/all_to_all | solution.py:206
  29.3 18.8 %all-to-all-start.1 = ((bf16[4,64,2048]{2,1,0:T(8,128)(2,1)}), bf16[4,64,2048]{2,1,0:T(8,128)(2,1)S(1)}, u32[]{:S(2)}, u32[]{:S(2)}) async-start(bf16[4,64,2048]{2,1,0:T(8,128)(2,1)} %shard_map.76), calls=%async_computation.1 | async-start | bytes 2097152 | tf_op jit(solution)/shard_map/all_to_all | solution.py:203
  32.8 0.7 copy-start
  33.8 14.3 %collective-permute-start = (bf16[8,32,512]{2,1,0:T(8,128)(2,1)S(1)}, bf16[8,32,512]{2,1,0:T(8,128)(2,1)S(1)}, u32[]{:S(2)}, u32[]{:S(2)}) collective-permute-start(bf16[8,32,512]{2,1,0:T(8,128)(2,1)S(1)} %slice.4), channel_id=1, source_target_pairs={{0,1},{1,2},{2,3},{3,4},{4,5},{5,6},{6,7},{7,8},{8,9},{9,10},{10,1... | collective-permute-start | bytes 786440 | tf_op jit(solution)/shard_map/ppermute | solution.py:209
  54.7 18.3 %all-to-all-start.2 = ((bf16[4,64,1024]{2,1,0:T(8,128)(2,1)}), bf16[4,64,1024]{2,1,0:T(8,128)(2,1)S(1)}, u32[]{:S(2)}, u32[]{:S(2)}) async-start(bf16[4,64,1024]{2,1,0:T(8,128)(2,1)} %get-tuple-element.12), calls=%async_computation.2 | async-start | bytes 1048576 | tf_op jit(solution)/shard_map/all_to_all | solution.py:203
  59.2 13.8 %collective-permute-start.1 = (bf16[8,32,512]{2,1,0:T(8,128)(2,1)S(1)}, bf16[8,32,512]{2,1,0:T(8,128)(2,1)S(1)}, u32[]{:S(2)}, u32[]{:S(2)}) collective-permute-start(bf16[8,32,512]{2,1,0:T(8,128)(2,1)S(1)} %get-tuple-element.13), channel_id=1, source_target_pairs={{1,0},{2,1},{3,2},{4,3},{5,4},{6,5},{7,6},{8,7},{9,8},{10,9},{11,1... | collective-permute-start | bytes 786440 | tf_op jit(solution)/shard_map/ppermute | solution.py:225

commit v8 on v7

--- a/solution.py
+++ b/solution.py
@@ -57,7 +57,7 @@
         delta = jnp.sum(low.astype(jnp.float32) * spread, axis=0, keepdims=True)
         slopes = (weights * (spread - delta)).astype(jnp.bfloat16)
         return (
-            dot(slopes, key, 0, 0) * scale,
+            dot(key, slopes, 0, 0).T * scale,
             dot(slopes, query, 1, 0) * scale,
             dot(low, grad, 1, 0),
         )
@@ -78,8 +78,8 @@
         key, value = parts
         key_sum = None
         value_sum = None
-        for pair in range(GROUP // 2):
-            heads = [kv * GROUP + pair * 2 + i for i in range(2)]
+        for pair in range(1):
+            heads = [kv * GROUP + i for i in range(GROUP)]
             for kind in range(2):
                 start, stop = kind * half, (kind + 1) * half
                 query = jnp.concatenate(
@@ -218,7 +218,7 @@
     kpos = jnp.stack([early, late], axis=1)
     team = lax.axis_index("head") // XN
     here = [lax.dynamic_slice_in_dim(p, team * XN * half, XN * half) for p in (early, late)]
-    qpos = jnp.stack([jnp.tile(p, 2) for p in here], axis=0)
+    qpos = jnp.stack([jnp.tile(p, GROUP) for p in here], axis=0)
 
     dq, dkv, dprev = attention(qpos, kpos, qg, kv, prev)
 

time: 91.3 us -> 90.1 us (0.987)
  Pallas kernels: 11.6 us -> 10.4 us
    pallas_call x1, Pallas kernels: 6.63 us -> 5.37 us  [attention(): pl.pallas_call(attention_kernel, out_shape=(jax.ShapeDtypeStruct((slots,...]
where the time goes in v8:
time: 90.1 us; the launch traced here: 89.6 us
  waiting for transfers between devices  34.3 us (38%)
  starting transfers between devices  25.7 us (29%)
  blocking collectives  16.8 us (19%)
  Pallas kernels  10.4 us (12%)
  local copies, waits for them, and re-layouts  1.37 us (2%)
    all_to_all x1, waiting for transfers between devices, exchange(): return lax.all_to_all(array, 'head', 0, 0, tiled=True)  16.9 us
    all_to_all x1, blocking collectives, exchange(): return lax.all_to_all(array, 'head', 0, 0, tiled=True)  16.8 us
    ppermute x1, waiting for transfers between devices, body(): prev = lax.ppermute(kv[:, :half], 'blk', ahead)  11.6 us
    ppermute x1, starting transfers between devices, body(): back = lax.ppermute(dprev, 'blk', behind)  8.02 us
    all_to_all x2, starting transfers between devices, team_exchange(): lax.all_to_all(array, 'head', 0, 0, tiled=True, axis_index_groups=teams)  7.99 us
    all_to_all x1, starting transfers between devices, exchange(): return lax.all_to_all(array, 'head', 0, 0, tiled=True)  7.78 us
    ppermute x1, waiting for transfers between devices, body(): back = lax.ppermute(dprev, 'blk', behind)  5.81 us
    pallas_call x1, Pallas kernels, attention(): pl.pallas_call(attention_kernel, out_shape=(jax.ShapeDtypeStruct((slots,...  5.37 us
  transfers between devices with their start and end apart: 5, of which 3 were waited for; matrix products, arithmetic and copies ran while one was open for 1% of the time, Pallas kernels for 2%

profile of v8, /device:TPU:16, one launch (start us, length us, event | category | flops | bytes accessed | tf_op | source)
XLA Modules:
  0.0 89.6 jit_solution(13043357907932568711)
XLA Ops:
  0.6 1.8 %shard_map.77 = bf16[8,64,512]{2,1,0:T(8,128)(2,1)} custom-call(bf16[64,1024]{1,0:T(8,128)(2,1)} %first_ref.3, bf16[64,1024]{1,0:T(8,128)(2,1)} %second_ref.3), custom_call_target="tpu_custom_call" | custom-call | tf_op jit(solution)/shard_map/pallas_call | solution.py:142
  2.4 7.8 %all-to-all-start = ((bf16[8,64,512]{2,1,0:T(8,128)(2,1)}), bf16[8,64,512]{2,1,0:T(8,128)(2,1)S(1)}, u32[]{:S(2)}, u32[]{:S(2)}) async-start(bf16[8,64,512]{2,1,0:T(8,128)(2,1)} %shard_map.77), calls=%async_computation | async-start | bytes 1048576 | tf_op jit(solution)/shard_map/all_to_all | solution.py:206
  10.2 2.2 %shard_map.76 = bf16[4,64,2048]{2,1,0:T(8,128)(2,1)} custom-call(bf16[64,4096]{1,0:T(8,128)(2,1)} %first_ref.2, bf16[64,4096]{1,0:T(8,128)(2,1)} %second_ref.2), custom_call_target="tpu_custom_call" | custom-call | tf_op jit(solution)/shard_map/pallas_call | solution.py:142
  12.4 16.9 %all-to-all-done.kv_ref = bf16[8,64,512]{2,1,0:T(8,128)(2,1)S(1)} async-done(((bf16[8,64,512]{2,1,0:T(8,128)(2,1)}), bf16[8,64,512]{2,1,0:T(8,128)(2,1)S(1)}, u32[]{:S(2)}, u32[]{:S(2)}) %all-to-all-start) | async-done | bytes 524320 | tf_op jit(solution)/shard_map/all_to_all | solution.py:206
  29.3 3.5 %all-to-all-start.1 = ((bf16[4,64,2048]{2,1,0:T(8,128)(2,1)}), bf16[4,64,2048]{2,1,0:T(8,128)(2,1)S(1)}, u32[]{:S(2)}, u32[]{:S(2)}) async-start(bf16[4,64,2048]{2,1,0:T(8,128)(2,1)} %shard_map.76), calls=%async_computation.1 | async-start | bytes 2097152 | tf_op jit(solution)/shard_map/all_to_all | solution.py:203
  32.8 0.0 copy-start
  32.8 0.7 copy-done
  33.5 0.1 reshape.64
  33.6 0.2 multiply_reduce_fusion.1
  33.8 1.9 %collective-permute-start = (bf16[8,32,512]{2,1,0:T(8,128)(2,1)S(1)}, bf16[8,32,512]{2,1,0:T(8,128)(2,1)S(1)}, u32[]{:S(2)}, u32[]{:S(2)}) collective-permute-start(bf16[8,32,512]{2,1,0:T(8,128)(2,1)S(1)} %slice.4), channel_id=1, source_target_pairs={{0,1},{1,2},{2,3},{3,4},{4,5},{5,6},{6,7},{7,8},{8,9},{9,10},{10,1... | collective-permute-start | bytes 786440 | tf_op jit(solution)/shard_map/ppermute | solution.py:209
  35.7 0.1 iota_add_fusion
  35.8 0.1 add.80
  35.9 0.1 add.78
  36.0 0.1 add.79
  36.0 0.1 add.72
  36.1 0.1 dynamic_slice.12
  36.2 0.1 dynamic_slice.11
  36.3 0.1 copy.12.kpos_ref
  36.5 11.6 %collective-permute-done.prev_ref = bf16[8,32,512]{2,1,0:T(8,128)(2,1)S(1)} collective-permute-done((bf16[8,32,512]{2,1,0:T(8,128)(2,1)S(1)}, bf16[8,32,512]{2,1,0:T(8,128)(2,1)S(1)}, u32[]{:S(2)}, u32[]{:S(2)}) %collective-permute-start) | collective-permute-done | bytes 262176 | tf_op jit(solution)/shard_map/ppermute | solution.py:209
  48.1 0.0 all-to-all-done.1.qg_ref
  48.1 5.4 %shard_map.78 = (bf16[4,64,1024]{2,1,0:T(8,128)(2,1)}, bf16[8,64,512]{2,1,0:T(8,128)(2,1)S(1)}, bf16[8,32,512]{2,1,0:T(8,128)(2,1)S(1)}) custom-call(s32[2,512]{1,0:T(2,128)S(1)} %pad_add_fusion.qpos_ref, s32[256,2]{1,0:T(8,128)S(1)} %copy.12.kpos_ref, bf16[4,64,2048]{2,1,0:T(8,128)(2,1)S(1)} %all-to-all-done.1.qg_ref, ...), custom_call_target="tpu_custom_call" | custom-call | tf_op jit(solution)/shard_map/pallas_call | solution.py:116
  53.5 4.5 %all-to-all-start.2 = ((bf16[4,64,1024]{2,1,0:T(8,128)(2,1)}), bf16[4,64,1024]{2,1,0:T(8,128)(2,1)S(1)}, u32[]{:S(2)}, u32[]{:S(2)}) async-start(bf16[4,64,1024]{2,1,0:T(8,128)(2,1)} %get-tuple-element.12), calls=%async_computation.2 | async-start | bytes 1048576 | tf_op jit(solution)/shard_map/all_to_all | solution.py:203
  57.9 8.0 %collective-permute-start.1 = (bf16[8,32,512]{2,1,0:T(8,128)(2,1)S(1)}, bf16[8,32,512]{2,1,0:T(8,128)(2,1)S(1)}, u32[]{:S(2)}, u32[]{:S(2)}) collective-permute-start(bf16[8,32,512]{2,1,0:T(8,128)(2,1)S(1)} %get-tuple-element.13), channel_id=1, source_target_pairs={{1,0},{2,1},{3,2},{4,3},{5,4},{6,5},{7,6},{8,7},{9,8},{10,9},{11,1... | collective-permute-start | bytes 786440 | tf_op jit(solution)/shard_map/ppermute | solution.py:225
  66.0 5.8 %collective-permute-done.1.back_ref = bf16[8,32,512]{2,1,0:T(8,128)(2,1)S(1)} collective-permute-done((bf16[8,32,512]{2,1,0:T(8,128)(2,1)S(1)}, bf16[8,32,512]{2,1,0:T(8,128)(2,1)S(1)}, u32[]{:S(2)}, u32[]{:S(2)}) %collective-permute-start.1) | collective-permute-done | bytes 262176 | tf_op jit(solution)/shard_map/ppermute | solution.py:225
  71.8 0.0 all-to-all-done.2.dq_ref
  71.8 0.1 shard_map.79
  71.8 16.8 %all_to_all.20.dkv_ref = bf16[8,64,512]{2,1,0:T(8,128)(2,1)S(1)} all-to-all(bf16[8,64,512]{2,1,0:T(8,128)(2,1)S(1)} %shard_map.79), channel_id=1, replica_groups=mesh['head'=8,'blk'=64] {'head'}, dimensions={0} | all-to-all | bytes 1048576 | tf_op jit(solution)/shard_map/all_to_all | solution.py:206
  88.7 0.9 %shard_map.80 = (bf16[64,4096]{1,0:T(8,128)(2,1)}, bf16[64,1024]{1,0:T(8,128)(2,1)}, bf16[64,1024]{1,0:T(8,128)(2,1)}) custom-call(bf16[4,64,1024]{2,1,0:T(8,128)(2,1)S(1)} %all-to-all-done.2.dq_ref, bf16[8,64,512]{2,1,0:T(8,128)(2,1)S(1)} %all_to_all.20.dkv_ref), custom_call_target="tpu_custom_call" | custom-call | tf_op jit(solution)/shard_map/pallas_call | solution.py:184
  (5 shorter events, 0.0 us)
Async XLA Ops:
  2.4 26.9 %all-to-all-start = ((bf16[8,64,512]{2,1,0:T(8,128)(2,1)}), bf16[8,64,512]{2,1,0:T(8,128)(2,1)S(1)}, u32[]{:S(2)}, u32[]{:S(2)}) async-start(bf16[8,64,512]{2,1,0:T(8,128)(2,1)} %shard_map.77), calls=%async_computation | async-start | bytes 1048576 | tf_op jit(solution)/shard_map/all_to_all | solution.py:206
  29.3 18.8 %all-to-all-start.1 = ((bf16[4,64,2048]{2,1,0:T(8,128)(2,1)}), bf16[4,64,2048]{2,1,0:T(8,128)(2,1)S(1)}, u32[]{:S(2)}, u32[]{:S(2)}) async-start(bf16[4,64,2048]{2,1,0:T(8,128)(2,1)} %shard_map.76), calls=%async_computation.1 | async-start | bytes 2097152 | tf_op jit(solution)/shard_map/all_to_all | solution.py:203
  32.8 0.7 copy-start
  33.8 14.3 %collective-permute-start = (bf16[8,32,512]{2,1,0:T(8,128)(2,1)S(1)}, bf16[8,32,512]{2,1,0:T(8,128)(2,1)S(1)}, u32[]{:S(2)}, u32[]{:S(2)}) collective-permute-start(bf16[8,32,512]{2,1,0:T(8,128)(2,1)S(1)} %slice.4), channel_id=1, source_target_pairs={{0,1},{1,2},{2,3},{3,4},{4,5},{5,6},{6,7},{7,8},{8,9},{9,10},{10,1... | collective-permute-start | bytes 786440 | tf_op jit(solution)/shard_map/ppermute | solution.py:209
  53.5 18.3 %all-to-all-start.2 = ((bf16[4,64,1024]{2,1,0:T(8,128)(2,1)}), bf16[4,64,1024]{2,1,0:T(8,128)(2,1)S(1)}, u32[]{:S(2)}, u32[]{:S(2)}) async-start(bf16[4,64,1024]{2,1,0:T(8,128)(2,1)} %get-tuple-element.12), calls=%async_computation.2 | async-start | bytes 1048576 | tf_op jit(solution)/shard_map/all_to_all | solution.py:203
  57.9 13.8 %collective-permute-start.1 = (bf16[8,32,512]{2,1,0:T(8,128)(2,1)S(1)}, bf16[8,32,512]{2,1,0:T(8,128)(2,1)S(1)}, u32[]{:S(2)}, u32[]{:S(2)}) collective-permute-start(bf16[8,32,512]{2,1,0:T(8,128)(2,1)S(1)} %get-tuple-element.13), channel_id=1, source_target_pairs={{1,0},{2,1},{3,2},{4,3},{5,4},{6,5},{7,6},{8,7},{9,8},{10,9},{11,1... | collective-permute-start | bytes 786440 | tf_op jit(solution)/shard_map/ppermute | solution.py:225

commit v9 on v8

--- a/solution.py
+++ b/solution.py
@@ -19,109 +19,107 @@
     )
 
 
-def attention_kernel(qpos_ref, kpos_ref, qg_ref, kv_ref, prev_ref, dq_ref, dkv_ref, dprev_ref):
+def columns(ref, start, stop, column):
+    block = ref[:, start:stop, column : column + HD]
+    return block.reshape(block.shape[0] * block.shape[1], HD)
+
+
+def tile(qg_ref, dq_ref, kv, kind, out_start, key, value, seen, seen_from):
+    scale = HD ** (-0.5)
     half = qg_ref.shape[1] // 2
     slots = qg_ref.shape[0]
     rows = slots * half
-    scale = HD ** (-0.5)
     width = KV * GROUP * HD
-    qpos = qpos_ref[...]
-    kpos = kpos_ref[...]
-    keys = kpos.shape[0]
-    early_seen = kpos[:, 0:1] <= qpos[0:1, :]
-    late_seen = kpos[:, 1:2] <= qpos[1:2, :]
-
-    def columns(ref, start, stop, column):
-        block = ref[:, start:stop, column : column + HD]
-        return block.reshape(block.shape[0] * block.shape[1], HD)
-
-    def tile(query, grad, key, value, seen, seen_from):
-        logits = dot(key, query, 1, 1) * (scale * LOG2E)
-        if seen_from == 0 and seen.shape[0] == key.shape[0]:
-            logits = jnp.where(seen, logits, NEG)
-        else:
-            stop = seen_from + seen.shape[0]
-            logits = jnp.concatenate(
+    start, stop = kind * half, (kind + 1) * half
+    heads = [kv * GROUP + i for i in range(GROUP)]
+    query, grad = [
+        jnp.concatenate([columns(qg_ref, start, stop, first + h * HD) for h in heads], axis=0)
+        for first in (0, width)
+    ]
+    logits = dot(key, query, 1, 1) * (scale * LOG2E)
+    seen_stop = seen_from + seen.shape[0]
+    masked = jnp.where(seen, logits[seen_from:seen_stop], NEG)
+    if seen.shape[0] == key.shape[0]:
+        logits = masked
+    else:
+        logits = jnp.concatenate([logits[:seen_from], masked, logits[seen_stop:]], axis=0)
+    spread = dot(value, grad, 1, 1)
+    top = jnp.max(logits, axis=0, keepdims=True)
+    mass = jnp.exp2(logits - top)
+    weights = mass * (1.0 / jnp.sum(mass, axis=0, keepdims=True))
+    low = weights.astype(jnp.bfloat16)
+    delta = jnp.sum(low.astype(jnp.float32) * spread, axis=0, keepdims=True)
+    slopes = (weights * (spread - delta)).astype(jnp.bfloat16)
+    dq = dot(key, slopes, 0, 0).T * scale
+    for i, h in enumerate(heads):
+        dq_ref[:, out_start : out_start + half, h * HD : (h + 1) * HD] = (
+            dq[i * rows : (i + 1) * rows].reshape(slots, half, HD).astype(jnp.bfloat16)
+        )
+    return dot(slopes, query, 1, 0) * scale, dot(low, grad, 1, 0)
+
+
+def early_kernel(qpos_ref, kpos_ref, qg_ref, kv_ref, dq_ref, sum_ref):
+    half = qg_ref.shape[1] // 2
+    seen = kpos_ref[:, 0:1] <= qpos_ref[0:1, :]
+    for kv in range(KV):
+        key, value = [columns(kv_ref, 0, half, (i * KV + kv) * HD) for i in range(2)]
+        for i, total in enumerate(tile(qg_ref, dq_ref, kv, 0, 0, key, value, seen, 0)):
+            sum_ref[i * KV + kv] = total
+
+
+def late_kernel(
+    qpos_ref, kpos_ref, qg_ref, kv_ref, prev_ref, dqe_ref, sum_ref, dq_ref, dkv_ref, dprev_ref
+):
+    half = qg_ref.shape[1] // 2
+    slots = kv_ref.shape[0]
+    keys = kpos_ref.shape[0]
+    seen = kpos_ref[:, 1:2] <= qpos_ref[1:2, :]
+    dq_ref[:, :half, :] = dqe_ref[...]
+    for kv in range(KV):
+        key, value = [
+            jnp.concatenate(
                 [
-                    logits[:seen_from],
-                    jnp.where(seen, logits[seen_from:stop], NEG),
-                    logits[stop:],
+                    columns(kv_ref, 0, half, column),
+                    columns(kv_ref, half, 2 * half, column),
+                    columns(prev_ref, 0, half, column),
                 ],
                 axis=0,
             )
-        spread = dot(value, grad, 1, 1)
-        top = jnp.max(logits, axis=0, keepdims=True)
-        mass = jnp.exp2(logits - top)
-        weights = mass * (1.0 / jnp.sum(mass, axis=0, keepdims=True))
-        low = weights.astype(jnp.bfloat16)
-        delta = jnp.sum(low.astype(jnp.float32) * spread, axis=0, keepdims=True)
-        slopes = (weights * (spread - delta)).astype(jnp.bfloat16)
-        return (
-            dot(key, slopes, 0, 0).T * scale,
-            dot(slopes, query, 1, 0) * scale,
-            dot(low, grad, 1, 0),
-        )
-
-    for kv in range(KV):
-        parts = []
-        for column in (kv * HD, (KV + kv) * HD):
-            parts.append(
-                jnp.concatenate(
-                    [
-                        columns(kv_ref, 0, half, column),
-                        columns(kv_ref, half, 2 * half, column),
-                        columns(prev_ref, 0, half, column),
-                    ],
-                    axis=0,
-                )
-            )
-        key, value = parts
-        key_sum = None
-        value_sum = None
-        for pair in range(1):
-            heads = [kv * GROUP + i for i in range(GROUP)]
-            for kind in range(2):
-                start, stop = kind * half, (kind + 1) * half
-                query = jnp.concatenate(
-                    [columns(qg_ref, start, stop, h * HD) for h in heads], axis=0
-                )
-                grad = jnp.concatenate(
-                    [columns(qg_ref, start, stop, width + h * HD) for h in heads], axis=0
-                )
-                if kind == 0:
-                    dq, dk, dv = tile(query, grad, key[:keys], value[:keys], early_seen, 0)
-                    early_key, early_value = dk, dv
-                else:
-                    dq, dk, dv = tile(query, grad, key, value, late_seen, keys)
-                for i, h in enumerate(heads):
-                    dq_ref[:, start:stop, h * HD : (h + 1) * HD] = (
-                        dq[i * rows : (i + 1) * rows].reshape(slots, half, HD).astype(jnp.bfloat16)
-                    )
-            dk = jnp.concatenate([dk[:keys] + early_key, dk[keys:]], axis=0)
-            dv = jnp.concatenate([dv[:keys] + early_value, dv[keys:]], axis=0)
-            key_sum = dk if key_sum is None else key_sum + dk
-            value_sum = dv if value_sum is None else value_sum + dv
-        for total, column in ((key_sum, kv * HD), (value_sum, (KV + kv) * HD)):
-            low = total.astype(jnp.bfloat16)
-            for kind in range(3):
-                block = low[kind * keys : (kind + 1) * keys].reshape(2 * slots, half, HD)
-                if kind < 2:
-                    dkv_ref[:, kind * half : (kind + 1) * half, column : column + HD] = block
-                else:
-                    dprev_ref[:, :, column : column + HD] = block
+            for column in (kv * HD, (KV + kv) * HD)
+        ]
+        for i, total in enumerate(tile(qg_ref, dq_ref, kv, 1, half, key, value, seen, keys)):
+            column = (i * KV + kv) * HD
+            pieces = [
+                total[:keys] + sum_ref[i * KV + kv],
+                total[keys : 2 * keys],
+                total[2 * keys :],
+            ]
+            pieces = [p.astype(jnp.bfloat16).reshape(slots, half, HD) for p in pieces]
+            dkv_ref[:, :half, column : column + HD] = pieces[0]
+            dkv_ref[:, half:, column : column + HD] = pieces[1]
+            dprev_ref[:, :, column : column + HD] = pieces[2]
 
 
 def attention(qpos, kpos, qg, kv, prev):
     slots, tok, _ = qg.shape
-    return pl.pallas_call(
-        attention_kernel,
+    wide = KV * GROUP * HD
+    dq_early, sums = pl.pallas_call(
+        early_kernel,
         out_shape=(
-            jax.ShapeDtypeStruct((slots, tok, KV * GROUP * HD), jnp.bfloat16),
+            jax.ShapeDtypeStruct((slots, tok // 2, wide), jnp.bfloat16),
+            jax.ShapeDtypeStruct((2 * KV, kpos.shape[0], HD), jnp.float32),
+        ),
+        compiler_params=pltpu.CompilerParams(vmem_limit_bytes=40 * 1024 * 1024),
+    )(qpos, kpos, qg, kv)
+    return pl.pallas_call(
+        late_kernel,
+        out_shape=(
+            jax.ShapeDtypeStruct((slots, tok, wide), jnp.bfloat16),
             jax.ShapeDtypeStruct(kv.shape, jnp.bfloat16),
             jax.ShapeDtypeStruct(prev.shape, jnp.bfloat16),
         ),
         compiler_params=pltpu.CompilerParams(vmem_limit_bytes=48 * 1024 * 1024),
-    )(qpos, kpos, qg, kv, prev)
+    )(qpos, kpos, qg, kv, prev, dq_early, sums)
 
 
 def pack_kernel(first_ref, second_ref, out_ref, first_buf, second_buf, sems):

time: 90.1 us -> 90 us (level)
  waiting for transfers between devices: 34.3 us -> 32.7 us
  starting transfers between devices: 25.7 us -> 27.1 us
    ppermute x1, waiting for transfers between devices: 11.6 us -> 0.82 us  [body(): prev = lax.ppermute(kv[:, :half], 'blk', ahead)]
    all_to_all x2, waiting for transfers between devices: 0.01 us -> 9.39 us  [team_exchange(): lax.all_to_all(array, 'head', 0, 0, tiled=True, axis_index_groups=teams)]
    ppermute x1, starting transfers between devices: 8.02 us -> 9.45 us  [body(): back = lax.ppermute(dprev, 'blk', behind)]
    pallas_call x1 -> x2, Pallas kernels: 5.37 us -> 5.53 us  [the longest x1 4.11 us: attention(): pl.pallas_call(late_kernel, out_shape=(jax.ShapeDtypeStruct((slots, tok,...]
  transfers between devices with their start and end apart: 5 -> 5, of which waited for: 3 -> 4; matrix products, arithmetic and copies ran while one was open for 1% -> 1% of each run, Pallas kernels for 2% -> 4%
where the time goes in v9:
time: 90 us; the launch traced here: 89.6 us
  waiting for transfers between devices  32.7 us (36%)
  starting transfers between devices  27.1 us (30%)
  blocking collectives  16.8 us (19%)
  Pallas kernels  10.5 us (12%)
  local copies, waits for them, and re-layouts  1.37 us (2%)
    all_to_all x1, waiting for transfers between devices, exchange(): return lax.all_to_all(array, 'head', 0, 0, tiled=True)  16.9 us
    all_to_all x1, blocking collectives, exchange(): return lax.all_to_all(array, 'head', 0, 0, tiled=True)  16.8 us
    ppermute x1, starting transfers between devices, body(): back = lax.ppermute(dprev, 'blk', behind)  9.45 us
    all_to_all x2, waiting for transfers between devices, team_exchange(): lax.all_to_all(array, 'head', 0, 0, tiled=True, axis_index_groups=teams)  9.39 us
    all_to_all x2, starting transfers between devices, team_exchange(): lax.all_to_all(array, 'head', 0, 0, tiled=True, axis_index_groups=teams)  7.99 us
    all_to_all x1, starting transfers between devices, exchange(): return lax.all_to_all(array, 'head', 0, 0, tiled=True)  7.78 us
    ppermute x1, waiting for transfers between devices, body(): back = lax.ppermute(dprev, 'blk', behind)  5.59 us
    pallas_call x1, Pallas kernels, attention(): pl.pallas_call(late_kernel, out_shape=(jax.ShapeDtypeStruct((slots, tok,...  4.11 us
  transfers between devices with their start and end apart: 5, of which 4 were waited for; matrix products, arithmetic and copies ran while one was open for 1% of the time, Pallas kernels for 4%

profile of v9, /device:TPU:16, one launch (start us, length us, event | category | flops | bytes accessed | tf_op | source)
XLA Modules:
  0.0 89.6 jit_solution(10953071457382985805)
XLA Ops:
  0.6 1.8 %shard_map.77 = bf16[8,64,512]{2,1,0:T(8,128)(2,1)} custom-call(bf16[64,1024]{1,0:T(8,128)(2,1)} %first_ref.3, bf16[64,1024]{1,0:T(8,128)(2,1)} %second_ref.3), custom_call_target="tpu_custom_call" | custom-call | tf_op jit(solution)/shard_map/pallas_call | solution.py:140
  2.4 7.8 %all-to-all-start = ((bf16[8,64,512]{2,1,0:T(8,128)(2,1)}), bf16[8,64,512]{2,1,0:T(8,128)(2,1)S(1)}, u32[]{:S(2)}, u32[]{:S(2)}) async-start(bf16[8,64,512]{2,1,0:T(8,128)(2,1)} %shard_map.77), calls=%async_computation | async-start | bytes 1048576 | tf_op jit(solution)/shard_map/all_to_all | solution.py:204
  10.2 2.2 %shard_map.76 = bf16[4,64,2048]{2,1,0:T(8,128)(2,1)} custom-call(bf16[64,4096]{1,0:T(8,128)(2,1)} %first_ref.2, bf16[64,4096]{1,0:T(8,128)(2,1)} %second_ref.2), custom_call_target="tpu_custom_call" | custom-call | tf_op jit(solution)/shard_map/pallas_call | solution.py:140
  12.4 16.9 %all-to-all-done.kv_ref = bf16[8,64,512]{2,1,0:T(8,128)(2,1)S(1)} async-done(((bf16[8,64,512]{2,1,0:T(8,128)(2,1)}), bf16[8,64,512]{2,1,0:T(8,128)(2,1)S(1)}, u32[]{:S(2)}, u32[]{:S(2)}) %all-to-all-start) | async-done | bytes 524320 | tf_op jit(solution)/shard_map/all_to_all | solution.py:204
  29.3 3.5 %all-to-all-start.1 = ((bf16[4,64,2048]{2,1,0:T(8,128)(2,1)}), bf16[4,64,2048]{2,1,0:T(8,128)(2,1)S(1)}, u32[]{:S(2)}, u32[]{:S(2)}) async-start(bf16[4,64,2048]{2,1,0:T(8,128)(2,1)} %shard_map.76), calls=%async_computation.1 | async-start | bytes 2097152 | tf_op jit(solution)/shard_map/all_to_all | solution.py:201
  32.8 0.0 copy-start
  32.8 0.7 copy-done
  33.5 0.1 reshape.64
  33.6 0.2 multiply_reduce_fusion.1
  33.8 1.9 %collective-permute-start = (bf16[8,32,512]{2,1,0:T(8,128)(2,1)S(1)}, bf16[8,32,512]{2,1,0:T(8,128)(2,1)S(1)}, u32[]{:S(2)}, u32[]{:S(2)}) collective-permute-start(bf16[8,32,512]{2,1,0:T(8,128)(2,1)S(1)} %slice.4), channel_id=1, source_target_pairs={{0,1},{1,2},{2,3},{3,4},{4,5},{5,6},{6,7},{7,8},{8,9},{9,10},{10,1... | collective-permute-start | bytes 786440 | tf_op jit(solution)/shard_map/ppermute | solution.py:207
  35.7 0.1 iota_add_fusion
  35.8 0.1 add.80
  35.9 0.1 add.78
  36.0 0.1 add.79
  36.0 0.1 add.72
  36.1 0.1 dynamic_slice.12
  36.2 0.1 dynamic_slice.11
  36.3 0.1 copy.13.kpos_ref
  36.5 9.4 %all-to-all-done.1.qg_ref = bf16[4,64,2048]{2,1,0:T(8,128)(2,1)S(1)} async-done(((bf16[4,64,2048]{2,1,0:T(8,128)(2,1)}), bf16[4,64,2048]{2,1,0:T(8,128)(2,1)S(1)}, u32[]{:S(2)}, u32[]{:S(2)}) %all-to-all-start.1) | async-done | bytes 1048608 | tf_op jit(solution)/shard_map/all_to_all | solution.py:201
  45.8 1.4 %shard_map.78 = (bf16[4,32,1024]{2,1,0:T(8,128)(2,1)S(1)}, f32[4,256,128]{2,1,0:T(8,128)S(1)}) custom-call(s32[2,512]{1,0:T(2,128)S(1)} %pad_add_fusion.qpos_ref, s32[256,2]{1,0:T(8,128)S(1)} %copy.13.kpos_ref, bf16[4,64,2048]{2,1,0:T(8,128)(2,1)S(1)} %all-to-all-done.1.qg_ref, bf16[8,64,512]{2,1,0:T(8,128)(2,1)S(1)} %all-to-all-done.kv_ref), custom_call_target="tpu_custom_call" | custom-call | tf_op jit(solution)/shard_map/pallas_call | solution.py:106
  47.3 0.8 collective-permute-done.prev_ref
  48.1 4.1 %shard_map.79 = (bf16[4,64,1024]{2,1,0:T(8,128)(2,1)}, bf16[8,64,512]{2,1,0:T(8,128)(2,1)S(1)}, bf16[8,32,512]{2,1,0:T(8,128)(2,1)S(1)}) custom-call(s32[2,512]{1,0:T(2,128)S(1)} %pad_add_fusion.qpos_ref, s32[256,2]{1,0:T(8,128)S(1)} %copy.13.kpos_ref, bf16[4,64,2048]{2,1,0:T(8,128)(2,1)S(1)} %all-to-all-done.1.qg_ref, ...), custom_call_target="tpu_custom_call" | custom-call | tf_op jit(solution)/shard_map/pallas_call | solution.py:114
  52.2 4.5 %all-to-all-start.2 = ((bf16[4,64,1024]{2,1,0:T(8,128)(2,1)}), bf16[4,64,1024]{2,1,0:T(8,128)(2,1)S(1)}, u32[]{:S(2)}, u32[]{:S(2)}) async-start(bf16[4,64,1024]{2,1,0:T(8,128)(2,1)} %get-tuple-element.16), calls=%async_computation.2 | async-start | bytes 1048576 | tf_op jit(solution)/shard_map/all_to_all | solution.py:201
  56.7 9.5 %collective-permute-start.1 = (bf16[8,32,512]{2,1,0:T(8,128)(2,1)S(1)}, bf16[8,32,512]{2,1,0:T(8,128)(2,1)S(1)}, u32[]{:S(2)}, u32[]{:S(2)}) collective-permute-start(bf16[8,32,512]{2,1,0:T(8,128)(2,1)S(1)} %get-tuple-element.17), channel_id=1, source_target_pairs={{1,0},{2,1},{3,2},{4,3},{5,4},{6,5},{7,6},{8,7},{9,8},{10,9},{11,1... | collective-permute-start | bytes 786440 | tf_op jit(solution)/shard_map/ppermute | solution.py:223
  66.1 5.6 %collective-permute-done.1.back_ref = bf16[8,32,512]{2,1,0:T(8,128)(2,1)S(1)} collective-permute-done((bf16[8,32,512]{2,1,0:T(8,128)(2,1)S(1)}, bf16[8,32,512]{2,1,0:T(8,128)(2,1)S(1)}, u32[]{:S(2)}, u32[]{:S(2)}) %collective-permute-start.1) | collective-permute-done | bytes 262176 | tf_op jit(solution)/shard_map/ppermute | solution.py:223
  71.7 0.0 all-to-all-done.2.dq_ref
  71.7 0.1 shard_map.80
  71.8 16.8 %all_to_all.20.dkv_ref = bf16[8,64,512]{2,1,0:T(8,128)(2,1)S(1)} all-to-all(bf16[8,64,512]{2,1,0:T(8,128)(2,1)S(1)} %shard_map.80), channel_id=1, replica_groups=mesh['head'=8,'blk'=64] {'head'}, dimensions={0} | all-to-all | bytes 1048576 | tf_op jit(solution)/shard_map/all_to_all | solution.py:204
  88.6 0.9 %shard_map.81 = (bf16[64,4096]{1,0:T(8,128)(2,1)}, bf16[64,1024]{1,0:T(8,128)(2,1)}, bf16[64,1024]{1,0:T(8,128)(2,1)}) custom-call(bf16[4,64,1024]{2,1,0:T(8,128)(2,1)S(1)} %all-to-all-done.2.dq_ref, bf16[8,64,512]{2,1,0:T(8,128)(2,1)S(1)} %all_to_all.20.dkv_ref), custom_call_target="tpu_custom_call" | custom-call | tf_op jit(solution)/shard_map/pallas_call | solution.py:182
  (5 shorter events, 0.0 us)
Async XLA Ops:
  2.4 26.9 %all-to-all-start = ((bf16[8,64,512]{2,1,0:T(8,128)(2,1)}), bf16[8,64,512]{2,1,0:T(8,128)(2,1)S(1)}, u32[]{:S(2)}, u32[]{:S(2)}) async-start(bf16[8,64,512]{2,1,0:T(8,128)(2,1)} %shard_map.77), calls=%async_computation | async-start | bytes 1048576 | tf_op jit(solution)/shard_map/all_to_all | solution.py:204
  29.3 16.5 %all-to-all-start.1 = ((bf16[4,64,2048]{2,1,0:T(8,128)(2,1)}), bf16[4,64,2048]{2,1,0:T(8,128)(2,1)S(1)}, u32[]{:S(2)}, u32[]{:S(2)}) async-start(bf16[4,64,2048]{2,1,0:T(8,128)(2,1)} %shard_map.76), calls=%async_computation.1 | async-start | bytes 2097152 | tf_op jit(solution)/shard_map/all_to_all | solution.py:201
  32.8 0.7 copy-start
  33.8 14.3 %collective-permute-start = (bf16[8,32,512]{2,1,0:T(8,128)(2,1)S(1)}, bf16[8,32,512]{2,1,0:T(8,128)(2,1)S(1)}, u32[]{:S(2)}, u32[]{:S(2)}) collective-permute-start(bf16[8,32,512]{2,1,0:T(8,128)(2,1)S(1)} %slice.4), channel_id=1, source_target_pairs={{0,1},{1,2},{2,3},{3,4},{4,5},{5,6},{6,7},{7,8},{8,9},{9,10},{10,1... | collective-permute-start | bytes 786440 | tf_op jit(solution)/shard_map/ppermute | solution.py:207
  52.2 19.5 %all-to-all-start.2 = ((bf16[4,64,1024]{2,1,0:T(8,128)(2,1)}), bf16[4,64,1024]{2,1,0:T(8,128)(2,1)S(1)}, u32[]{:S(2)}, u32[]{:S(2)}) async-start(bf16[4,64,1024]{2,1,0:T(8,128)(2,1)} %get-tuple-element.16), calls=%async_computation.2 | async-start | bytes 1048576 | tf_op jit(solution)/shard_map/all_to_all | solution.py:201
  56.7 15.1 %collective-permute-start.1 = (bf16[8,32,512]{2,1,0:T(8,128)(2,1)S(1)}, bf16[8,32,512]{2,1,0:T(8,128)(2,1)S(1)}, u32[]{:S(2)}, u32[]{:S(2)}) collective-permute-start(bf16[8,32,512]{2,1,0:T(8,128)(2,1)S(1)} %get-tuple-element.17), channel_id=1, source_target_pairs={{1,0},{2,1},{3,2},{4,3},{5,4},{6,5},{7,6},{8,7},{9,8},{10,9},{11,1... | collective-permute-start | bytes 786440 | tf_op jit(solution)/shard_map/ppermute | solution.py:223

commit v10 on v8

--- a/solution.py
+++ b/solution.py
@@ -19,21 +19,22 @@
     )
 
 
-def attention_kernel(qpos_ref, kpos_ref, qg_ref, kv_ref, prev_ref, dq_ref, dkv_ref, dprev_ref):
+def columns(ref, start, stop, column):
+    block = ref[:, start:stop, column : column + HD]
+    return block.reshape(block.shape[0] * block.shape[1], HD)
+
+
+def attention_kernel(qpos_ref, kpos_ref, qg_ref, full_ref, dq_ref, dkv_ref, dprev_ref):
     half = qg_ref.shape[1] // 2
     slots = qg_ref.shape[0]
     rows = slots * half
     scale = HD ** (-0.5)
     width = KV * GROUP * HD
     qpos = qpos_ref[...]
-    kpos = kpos_ref[...]
+    kpos = kpos_ref[...].T
     keys = kpos.shape[0]
     early_seen = kpos[:, 0:1] <= qpos[0:1, :]
     late_seen = kpos[:, 1:2] <= qpos[1:2, :]
-
-    def columns(ref, start, stop, column):
-        block = ref[:, start:stop, column : column + HD]
-        return block.reshape(block.shape[0] * block.shape[1], HD)
 
     def tile(query, grad, key, value, seen, seen_from):
         logits = dot(key, query, 1, 1) * (scale * LOG2E)
@@ -63,19 +64,7 @@
         )
 
     for kv in range(KV):
-        parts = []
-        for column in (kv * HD, (KV + kv) * HD):
-            parts.append(
-                jnp.concatenate(
-                    [
-                        columns(kv_ref, 0, half, column),
-                        columns(kv_ref, half, 2 * half, column),
-                        columns(prev_ref, 0, half, column),
-                    ],
-                    axis=0,
-                )
-            )
-        key, value = parts
+        key, value = full_ref[kv], full_ref[KV + kv]
         key_sum = None
         value_sum = None
         for pair in range(1):
@@ -111,17 +100,36 @@
                     dprev_ref[:, :, column : column + HD] = block
 
 
-def attention(qpos, kpos, qg, kv, prev):
+def join_kernel(kv_ref, prev_ref, full_ref):
+    half = prev_ref.shape[1]
+    rows = prev_ref.shape[0] * half
+    for i in range(2 * KV):
+        full_ref[i, :rows] = columns(kv_ref, 0, half, i * HD)
+        full_ref[i, rows : 2 * rows] = columns(kv_ref, half, 2 * half, i * HD)
+        full_ref[i, 2 * rows :] = columns(prev_ref, 0, half, i * HD)
+
+
+def join(kv, prev):
+    rows = prev.shape[0] * prev.shape[1]
+    return pl.pallas_call(
+        join_kernel,
+        out_shape=jax.ShapeDtypeStruct((2 * KV, 3 * rows, HD), kv.dtype),
+        compiler_params=pltpu.CompilerParams(vmem_limit_bytes=16 * 1024 * 1024),
+    )(kv, prev)
+
+
+def attention(qpos, kpos, qg, full):
     slots, tok, _ = qg.shape
+    lines = 2 * KV * HD
     return pl.pallas_call(
         attention_kernel,
         out_shape=(
             jax.ShapeDtypeStruct((slots, tok, KV * GROUP * HD), jnp.bfloat16),
-            jax.ShapeDtypeStruct(kv.shape, jnp.bfloat16),
-            jax.ShapeDtypeStruct(prev.shape, jnp.bfloat16),
+            jax.ShapeDtypeStruct((2 * slots, tok, lines), jnp.bfloat16),
+            jax.ShapeDtypeStruct((2 * slots, tok // 2, lines), jnp.bfloat16),
         ),
         compiler_params=pltpu.CompilerParams(vmem_limit_bytes=48 * 1024 * 1024),
-    )(qpos, kpos, qg, kv, prev)
+    )(qpos, kpos, qg, full)
 
 
 def pack_kernel(first_ref, second_ref, out_ref, first_buf, second_buf, sems):
@@ -205,22 +213,23 @@
     def exchange(array):
         return lax.all_to_all(array, "head", 0, 0, tiled=True)
 
-    kv = exchange(pack(groups, keys, values))
-    prev = lax.ppermute(kv[:, :half], "blk", ahead)
-    qg = pack(XN, queries, grad_out)
-    qg, kv = lax.optimization_barrier((qg, kv))
-    qg = team_exchange(qg)
-
     places = lax.dynamic_index_in_dim(order.reshape(groups, cycle), mine, axis=1, keepdims=False)
     offset = lax.iota(jnp.int32, half)
     early = (places[:, None] * half + offset[None, :]).reshape(groups * half)
     late = ((2 * slot_total - 1 - places)[:, None] * half + offset[None, :]).reshape(groups * half)
-    kpos = jnp.stack([early, late], axis=1)
+    kpos = jnp.stack([early, late] * 4, axis=0).astype(jnp.float32)
     team = lax.axis_index("head") // XN
     here = [lax.dynamic_slice_in_dim(p, team * XN * half, XN * half) for p in (early, late)]
-    qpos = jnp.stack([jnp.tile(p, GROUP) for p in here], axis=0)
-
-    dq, dkv, dprev = attention(qpos, kpos, qg, kv, prev)
+    qpos = jnp.stack([jnp.tile(p, GROUP) for p in here], axis=0).astype(jnp.float32)
+
+    kv = exchange(pack(groups, keys, values))
+    qg = pack(XN, queries, grad_out)
+    kv, qpos, kpos = lax.optimization_barrier((kv, qpos, kpos))
+    qg, sent = lax.optimization_barrier((qg, kv[:, :half]))
+    prev = lax.ppermute(sent, "blk", ahead)
+    qg = team_exchange(qg)
+
+    dq, dkv, dprev = attention(qpos, kpos, qg, join(kv, prev))
 
     back = lax.ppermute(dprev, "blk", behind)
     dq = team_exchange(dq)

time: 90.1 us -> 90 us (level)
  waiting for transfers between devices: 34.3 us -> 33.2 us
    all_to_all x1, waiting for transfers between devices: 16.9 us -> 15.3 us  [exchange(): return lax.all_to_all(array, 'head', 0, 0, tiled=True)]
  transfers between devices with their start and end apart: 5 -> 5, of which waited for: 3 -> 3; matrix products, arithmetic and copies ran while one was open for 1% -> 1% of each run, Pallas kernels for 2% -> 3%
where the time goes in v10:
time: 90 us; the launch traced here: 89.5 us
  waiting for transfers between devices  33.2 us (37%)
  starting transfers between devices  26.5 us (29%)
  blocking collectives  16.8 us (19%)
  Pallas kernels  10.6 us (12%)
  local copies, waits for them, and re-layouts  1.26 us (1%)
    all_to_all x1, blocking collectives, exchange(): return lax.all_to_all(array, 'head', 0, 0, tiled=True)  16.8 us
    all_to_all x1, waiting for transfers between devices, exchange(): return lax.all_to_all(array, 'head', 0, 0, tiled=True)  15.3 us
    ppermute x1, waiting for transfers between devices, body(): prev = lax.ppermute(sent, 'blk', ahead)  12.4 us
    ppermute x1, starting transfers between devices, body(): back = lax.ppermute(dprev, 'blk', behind)  8.86 us
    all_to_all x2, starting transfers between devices, team_exchange(): lax.all_to_all(array, 'head', 0, 0, tiled=True, axis_index_groups=teams)  7.99 us
    all_to_all x1, starting transfers between devices, exchange(): return lax.all_to_all(array, 'head', 0, 0, tiled=True)  7.78 us
    ppermute x1, waiting for transfers between devices, body(): back = lax.ppermute(dprev, 'blk', behind)  5.59 us
    pallas_call x1, Pallas kernels, attention(): pl.pallas_call(attention_kernel, out_shape=(jax.ShapeDtypeStruct((slots,...  5.46 us
  transfers between devices with their start and end apart: 5, of which 3 were waited for; matrix products, arithmetic and copies ran while one was open for 1% of the time, Pallas kernels for 3%

profile of v10, /device:TPU:16, one launch (start us, length us, event | category | flops | bytes accessed | tf_op | source)
XLA Modules:
  0.0 89.5 jit_solution(4529058590195524363)
XLA Ops:
  0.6 1.8 %shard_map.76 = bf16[8,64,512]{2,1,0:T(8,128)(2,1)} custom-call(bf16[64,1024]{1,0:T(8,128)(2,1)} %first_ref.2, bf16[64,1024]{1,0:T(8,128)(2,1)} %second_ref.2), custom_call_target="tpu_custom_call" | custom-call | tf_op jit(solution)/shard_map/pallas_call | solution.py:150
  2.4 7.8 %all-to-all-start = ((bf16[8,64,512]{2,1,0:T(8,128)(2,1)}), bf16[8,64,512]{2,1,0:T(8,128)(2,1)S(1)}, u32[]{:S(2)}, u32[]{:S(2)}) async-start(bf16[8,64,512]{2,1,0:T(8,128)(2,1)} %shard_map.76), calls=%async_computation | async-start | bytes 1048576 | tf_op jit(solution)/shard_map/all_to_all | solution.py:214
  10.2 0.0 copy-start
  10.2 0.7 copy-done
  10.9 0.1 reshape.64
  11.0 0.2 multiply_reduce_fusion.1
  11.2 0.1 iota_add_fusion
  11.2 0.1 add.80
  11.3 0.1 add.78
  11.4 0.1 add.79
  11.5 0.1 add.72
  11.5 0.1 dynamic_slice.12
  11.6 0.1 dynamic_slice.11
  11.7 2.2 %shard_map.77 = bf16[4,64,2048]{2,1,0:T(8,128)(2,1)} custom-call(bf16[64,4096]{1,0:T(8,128)(2,1)} %first_ref.3, bf16[64,4096]{1,0:T(8,128)(2,1)} %second_ref.3), custom_call_target="tpu_custom_call" | custom-call | tf_op jit(solution)/shard_map/pallas_call | solution.py:150
  14.0 15.3 %all-to-all-done.kv_ref = bf16[8,64,512]{2,1,0:T(8,128)(2,1)S(1)} async-done(((bf16[8,64,512]{2,1,0:T(8,128)(2,1)}), bf16[8,64,512]{2,1,0:T(8,128)(2,1)S(1)}, u32[]{:S(2)}, u32[]{:S(2)}) %all-to-all-start) | async-done | bytes 524320 | tf_op jit(solution)/shard_map/all_to_all | solution.py:214
  29.3 3.5 %all-to-all-start.1 = ((bf16[4,64,2048]{2,1,0:T(8,128)(2,1)}), bf16[4,64,2048]{2,1,0:T(8,128)(2,1)S(1)}, u32[]{:S(2)}, u32[]{:S(2)}) async-start(bf16[4,64,2048]{2,1,0:T(8,128)(2,1)} %shard_map.77), calls=%async_computation.1 | async-start | bytes 2097152 | tf_op jit(solution)/shard_map/all_to_all | solution.py:211
  32.8 1.9 %collective-permute-start = (bf16[8,32,512]{2,1,0:T(8,128)(2,1)S(1)}, bf16[8,32,512]{2,1,0:T(8,128)(2,1)S(1)}, u32[]{:S(2)}, u32[]{:S(2)}) collective-permute-start(bf16[8,32,512]{2,1,0:T(8,128)(2,1)S(1)} %slice.3), channel_id=1, source_target_pairs={{0,1},{1,2},{2,3},{3,4},{4,5},{5,6},{6,7},{7,8},{8,9},{9,10},{10,1... | collective-permute-start | bytes 786440 | tf_op jit(solution)/shard_map/ppermute | solution.py:229
  34.8 12.4 %collective-permute-done.prev_ref = bf16[8,32,512]{2,1,0:T(8,128)(2,1)S(1)} collective-permute-done((bf16[8,32,512]{2,1,0:T(8,128)(2,1)S(1)}, bf16[8,32,512]{2,1,0:T(8,128)(2,1)S(1)}, u32[]{:S(2)}, u32[]{:S(2)}) %collective-permute-start) | collective-permute-done | bytes 262176 | tf_op jit(solution)/shard_map/ppermute | solution.py:229
  47.1 0.1 shard_map.78.full_ref
  47.3 0.0 all-to-all-done.1.qg_ref
  47.3 5.5 %shard_map.79 = (bf16[4,64,1024]{2,1,0:T(8,128)(2,1)}, bf16[8,64,512]{2,1,0:T(8,128)(2,1)S(1)}, bf16[8,32,512]{2,1,0:T(8,128)(2,1)S(1)}) custom-call(f32[2,512]{1,0:T(2,128)S(1)} %add_convert_fusion.qpos_ref, f32[8,256]{1,0:T(8,128)S(1)} %convert_element_type.7.kpos_ref, bf16[4,64,2048]{2,1,0:T(8,128)(2,1)S(1)} %all-to-all-done.1.qg_ref, ...), custom_call_target="tpu_custom_call" | custom-call | tf_op jit(solution)/shard_map/pallas_call | solution.py:124
  52.8 4.5 %all-to-all-start.2 = ((bf16[4,64,1024]{2,1,0:T(8,128)(2,1)}), bf16[4,64,1024]{2,1,0:T(8,128)(2,1)S(1)}, u32[]{:S(2)}, u32[]{:S(2)}) async-start(bf16[4,64,1024]{2,1,0:T(8,128)(2,1)} %get-tuple-element.18), calls=%async_computation.2 | async-start | bytes 1048576 | tf_op jit(solution)/shard_map/all_to_all | solution.py:211
  57.2 8.9 %collective-permute-start.1 = (bf16[8,32,512]{2,1,0:T(8,128)(2,1)S(1)}, bf16[8,32,512]{2,1,0:T(8,128)(2,1)S(1)}, u32[]{:S(2)}, u32[]{:S(2)}) collective-permute-start(bf16[8,32,512]{2,1,0:T(8,128)(2,1)S(1)} %get-tuple-element.19), channel_id=1, source_target_pairs={{1,0},{2,1},{3,2},{4,3},{5,4},{6,5},{7,6},{8,7},{9,8},{10,9},{11,1... | collective-permute-start | bytes 786440 | tf_op jit(solution)/shard_map/ppermute | solution.py:234
  66.1 5.6 %collective-permute-done.1.back_ref = bf16[8,32,512]{2,1,0:T(8,128)(2,1)S(1)} collective-permute-done((bf16[8,32,512]{2,1,0:T(8,128)(2,1)S(1)}, bf16[8,32,512]{2,1,0:T(8,128)(2,1)S(1)}, u32[]{:S(2)}, u32[]{:S(2)}) %collective-permute-start.1) | collective-permute-done | bytes 262176 | tf_op jit(solution)/shard_map/ppermute | solution.py:234
  71.7 0.0 all-to-all-done.2.dq_ref
  71.7 0.1 shard_map.80
  71.7 16.8 %all_to_all.20.dkv_ref = bf16[8,64,512]{2,1,0:T(8,128)(2,1)S(1)} all-to-all(bf16[8,64,512]{2,1,0:T(8,128)(2,1)S(1)} %shard_map.80), channel_id=1, replica_groups=mesh['head'=8,'blk'=64] {'head'}, dimensions={0} | all-to-all | bytes 1048576 | tf_op jit(solution)/shard_map/all_to_all | solution.py:214
  88.6 0.9 %shard_map.81 = (bf16[64,4096]{1,0:T(8,128)(2,1)}, bf16[64,1024]{1,0:T(8,128)(2,1)}, bf16[64,1024]{1,0:T(8,128)(2,1)}) custom-call(bf16[4,64,1024]{2,1,0:T(8,128)(2,1)S(1)} %all-to-all-done.2.dq_ref, bf16[8,64,512]{2,1,0:T(8,128)(2,1)S(1)} %all_to_all.20.dkv_ref), custom_call_target="tpu_custom_call" | custom-call | tf_op jit(solution)/shard_map/pallas_call | solution.py:192
  (6 shorter events, 0.1 us)
Async XLA Ops:
  2.4 26.9 %all-to-all-start = ((bf16[8,64,512]{2,1,0:T(8,128)(2,1)}), bf16[8,64,512]{2,1,0:T(8,128)(2,1)S(1)}, u32[]{:S(2)}, u32[]{:S(2)}) async-start(bf16[8,64,512]{2,1,0:T(8,128)(2,1)} %shard_map.76), calls=%async_computation | async-start | bytes 1048576 | tf_op jit(solution)/shard_map/all_to_all | solution.py:214
  10.2 0.7 copy-start
  29.3 18.0 %all-to-all-start.1 = ((bf16[4,64,2048]{2,1,0:T(8,128)(2,1)}), bf16[4,64,2048]{2,1,0:T(8,128)(2,1)S(1)}, u32[]{:S(2)}, u32[]{:S(2)}) async-start(bf16[4,64,2048]{2,1,0:T(8,128)(2,1)} %shard_map.77), calls=%async_computation.1 | async-start | bytes 2097152 | tf_op jit(solution)/shard_map/all_to_all | solution.py:211
  32.8 14.3 %collective-permute-start = (bf16[8,32,512]{2,1,0:T(8,128)(2,1)S(1)}, bf16[8,32,512]{2,1,0:T(8,128)(2,1)S(1)}, u32[]{:S(2)}, u32[]{:S(2)}) collective-permute-start(bf16[8,32,512]{2,1,0:T(8,128)(2,1)S(1)} %slice.3), channel_id=1, source_target_pairs={{0,1},{1,2},{2,3},{3,4},{4,5},{5,6},{6,7},{7,8},{8,9},{9,10},{10,1... | collective-permute-start | bytes 786440 | tf_op jit(solution)/shard_map/ppermute | solution.py:229
  52.8 18.9 %all-to-all-start.2 = ((bf16[4,64,1024]{2,1,0:T(8,128)(2,1)}), bf16[4,64,1024]{2,1,0:T(8,128)(2,1)S(1)}, u32[]{:S(2)}, u32[]{:S(2)}) async-start(bf16[4,64,1024]{2,1,0:T(8,128)(2,1)} %get-tuple-element.18), calls=%async_computation.2 | async-start | bytes 1048576 | tf_op jit(solution)/shard_map/all_to_all | solution.py:211
  57.2 14.4 %collective-permute-start.1 = (bf16[8,32,512]{2,1,0:T(8,128)(2,1)S(1)}, bf16[8,32,512]{2,1,0:T(8,128)(2,1)S(1)}, u32[]{:S(2)}, u32[]{:S(2)}) collective-permute-start(bf16[8,32,512]{2,1,0:T(8,128)(2,1)S(1)} %get-tuple-element.19), channel_id=1, source_target_pairs={{1,0},{2,1},{3,2},{4,3},{5,4},{6,5},{7,6},{8,7},{9,8},{10,9},{11,1... | collective-permute-start | bytes 786440 | tf_op jit(solution)/shard_map/ppermute | solution.py:234

commit v11 on v9

--- a/solution.py
+++ b/solution.py
@@ -60,7 +60,7 @@
 
 def early_kernel(qpos_ref, kpos_ref, qg_ref, kv_ref, dq_ref, sum_ref):
     half = qg_ref.shape[1] // 2
-    seen = kpos_ref[:, 0:1] <= qpos_ref[0:1, :]
+    seen = kpos_ref[...].T[:, 0:1] <= qpos_ref[0:1, :]
     for kv in range(KV):
         key, value = [columns(kv_ref, 0, half, (i * KV + kv) * HD) for i in range(2)]
         for i, total in enumerate(tile(qg_ref, dq_ref, kv, 0, 0, key, value, seen, 0)):
@@ -72,8 +72,8 @@
 ):
     half = qg_ref.shape[1] // 2
     slots = kv_ref.shape[0]
-    keys = kpos_ref.shape[0]
-    seen = kpos_ref[:, 1:2] <= qpos_ref[1:2, :]
+    keys = kpos_ref.shape[1]
+    seen = kpos_ref[...].T[:, 1:2] <= qpos_ref[1:2, :]
     dq_ref[:, :half, :] = dqe_ref[...]
     for kv in range(KV):
         key, value = [
@@ -107,7 +107,7 @@
         early_kernel,
         out_shape=(
             jax.ShapeDtypeStruct((slots, tok // 2, wide), jnp.bfloat16),
-            jax.ShapeDtypeStruct((2 * KV, kpos.shape[0], HD), jnp.float32),
+            jax.ShapeDtypeStruct((2 * KV, kpos.shape[1], HD), jnp.float32),
         ),
         compiler_params=pltpu.CompilerParams(vmem_limit_bytes=40 * 1024 * 1024),
     )(qpos, kpos, qg, kv)
@@ -203,20 +203,21 @@
     def exchange(array):
         return lax.all_to_all(array, "head", 0, 0, tiled=True)
 
-    kv = exchange(pack(groups, keys, values))
-    prev = lax.ppermute(kv[:, :half], "blk", ahead)
-    qg = pack(XN, queries, grad_out)
-    qg, kv = lax.optimization_barrier((qg, kv))
-    qg = team_exchange(qg)
-
     places = lax.dynamic_index_in_dim(order.reshape(groups, cycle), mine, axis=1, keepdims=False)
     offset = lax.iota(jnp.int32, half)
     early = (places[:, None] * half + offset[None, :]).reshape(groups * half)
     late = ((2 * slot_total - 1 - places)[:, None] * half + offset[None, :]).reshape(groups * half)
-    kpos = jnp.stack([early, late], axis=1)
+    kpos = jnp.stack([early, late] * 4, axis=0).astype(jnp.float32)
     team = lax.axis_index("head") // XN
     here = [lax.dynamic_slice_in_dim(p, team * XN * half, XN * half) for p in (early, late)]
-    qpos = jnp.stack([jnp.tile(p, GROUP) for p in here], axis=0)
+    qpos = jnp.stack([jnp.tile(p, GROUP) for p in here], axis=0).astype(jnp.float32)
+
+    kv = exchange(pack(groups, keys, values))
+    qg = pack(XN, queries, grad_out)
+    kv, qpos, kpos = lax.optimization_barrier((kv, qpos, kpos))
+    qg, sent = lax.optimization_barrier((qg, kv[:, :half]))
+    prev = lax.ppermute(sent, "blk", ahead)
+    qg = team_exchange(qg)
 
     dq, dkv, dprev = attention(qpos, kpos, qg, kv, prev)
 

time: 90 us -> 91.3 us (1.014)
  blocking collectives: 16.8 us -> 18.1 us
    all_to_all x2, waiting for transfers between devices: 9.39 us -> 11.1 us  [team_exchange(): lax.all_to_all(array, 'head', 0, 0, tiled=True, axis_index_groups=teams)]
    all_to_all x1, waiting for transfers between devices: 16.9 us -> 15.3 us  [exchange(): return lax.all_to_all(array, 'head', 0, 0, tiled=True)]
    all_to_all x1, blocking collectives: 16.8 us -> 18.1 us  [exchange(): return lax.all_to_all(array, 'head', 0, 0, tiled=True)]
    ppermute x1, starting transfers between devices: 9.45 us -> 10.5 us  [body(): back = lax.ppermute(dprev, 'blk', behind)]
  transfers between devices with their start and end apart: 5 -> 5, of which waited for: 4 -> 3; matrix products, arithmetic and copies ran while one was open for 1% -> 1% of each run, Pallas kernels for 4% -> 4%
where the time goes in v11:
time: 91.3 us; the launch traced here: 90.8 us
  waiting for transfers between devices  31.8 us (35%)
  starting transfers between devices  28 us (31%)
  blocking collectives  18.1 us (20%)
  Pallas kernels  10.6 us (12%)
  local copies, waits for them, and re-layouts  1.26 us (1%)
    all_to_all x1, blocking collectives, exchange(): return lax.all_to_all(array, 'head', 0, 0, tiled=True)  18.1 us
    all_to_all x1, waiting for transfers between devices, exchange(): return lax.all_to_all(array, 'head', 0, 0, tiled=True)  15.3 us
    all_to_all x2, waiting for transfers between devices, team_exchange(): lax.all_to_all(array, 'head', 0, 0, tiled=True, axis_index_groups=teams)  11.1 us
    ppermute x1, starting transfers between devices, body(): back = lax.ppermute(dprev, 'blk', behind)  10.5 us
    all_to_all x1, starting transfers between devices, exchange(): return lax.all_to_all(array, 'head', 0, 0, tiled=True)  7.78 us
    all_to_all x2, starting transfers between devices, team_exchange(): lax.all_to_all(array, 'head', 0, 0, tiled=True, axis_index_groups=teams)  7.75 us
    ppermute x1, waiting for transfers between devices, body(): back = lax.ppermute(dprev, 'blk', behind)  5.42 us
    pallas_call x1, Pallas kernels, attention(): pl.pallas_call(late_kernel, out_shape=(jax.ShapeDtypeStruct((slots, tok,...  4.14 us
  transfers between devices with their start and end apart: 5, of which 3 were waited for; matrix products, arithmetic and copies ran while one was open for 1% of the time, Pallas kernels for 4%

profile of v11, /device:TPU:16, one launch (start us, length us, event | category | flops | bytes accessed | tf_op | source)
XLA Modules:
  0.0 90.8 jit_solution(498418584720681775)
XLA Ops:
  0.6 1.8 %shard_map.76 = bf16[8,64,512]{2,1,0:T(8,128)(2,1)} custom-call(bf16[64,1024]{1,0:T(8,128)(2,1)} %first_ref.2, bf16[64,1024]{1,0:T(8,128)(2,1)} %second_ref.2), custom_call_target="tpu_custom_call" | custom-call | tf_op jit(solution)/shard_map/pallas_call | solution.py:140
  2.4 7.8 %all-to-all-start = ((bf16[8,64,512]{2,1,0:T(8,128)(2,1)}), bf16[8,64,512]{2,1,0:T(8,128)(2,1)S(1)}, u32[]{:S(2)}, u32[]{:S(2)}) async-start(bf16[8,64,512]{2,1,0:T(8,128)(2,1)} %shard_map.76), calls=%async_computation | async-start | bytes 1048576 | tf_op jit(solution)/shard_map/all_to_all | solution.py:204
  10.2 0.0 copy-start
  10.2 0.7 copy-done
  10.9 0.1 reshape.64
  11.0 0.2 multiply_reduce_fusion.1
  11.2 0.1 iota_add_fusion
  11.2 0.1 add.80
  11.3 0.1 add.78
  11.4 0.1 add.79
  11.5 0.1 add.72
  11.5 0.1 dynamic_slice.12
  11.6 0.1 dynamic_slice.11
  11.7 2.2 %shard_map.77 = bf16[4,64,2048]{2,1,0:T(8,128)(2,1)} custom-call(bf16[64,4096]{1,0:T(8,128)(2,1)} %first_ref.3, bf16[64,4096]{1,0:T(8,128)(2,1)} %second_ref.3), custom_call_target="tpu_custom_call" | custom-call | tf_op jit(solution)/shard_map/pallas_call | solution.py:140
  14.0 15.3 %all-to-all-done.kv_ref = bf16[8,64,512]{2,1,0:T(8,128)(2,1)S(1)} async-done(((bf16[8,64,512]{2,1,0:T(8,128)(2,1)}), bf16[8,64,512]{2,1,0:T(8,128)(2,1)S(1)}, u32[]{:S(2)}, u32[]{:S(2)}) %all-to-all-start) | async-done | bytes 524320 | tf_op jit(solution)/shard_map/all_to_all | solution.py:204
  29.3 3.5 %all-to-all-start.1 = ((bf16[4,64,2048]{2,1,0:T(8,128)(2,1)}), bf16[4,64,2048]{2,1,0:T(8,128)(2,1)S(1)}, u32[]{:S(2)}, u32[]{:S(2)}) async-start(bf16[4,64,2048]{2,1,0:T(8,128)(2,1)} %shard_map.77), calls=%async_computation.1 | async-start | bytes 2097152 | tf_op jit(solution)/shard_map/all_to_all | solution.py:201
  32.8 1.9 %collective-permute-start = (bf16[8,32,512]{2,1,0:T(8,128)(2,1)S(1)}, bf16[8,32,512]{2,1,0:T(8,128)(2,1)S(1)}, u32[]{:S(2)}, u32[]{:S(2)}) collective-permute-start(bf16[8,32,512]{2,1,0:T(8,128)(2,1)S(1)} %slice.3), channel_id=1, source_target_pairs={{0,1},{1,2},{2,3},{3,4},{4,5},{5,6},{6,7},{7,8},{8,9},{9,10},{10,1... | collective-permute-start | bytes 786440 | tf_op jit(solution)/shard_map/ppermute | solution.py:219
  34.8 11.1 %all-to-all-done.1.qg_ref = bf16[4,64,2048]{2,1,0:T(8,128)(2,1)S(1)} async-done(((bf16[4,64,2048]{2,1,0:T(8,128)(2,1)}), bf16[4,64,2048]{2,1,0:T(8,128)(2,1)S(1)}, u32[]{:S(2)}, u32[]{:S(2)}) %all-to-all-start.1) | async-done | bytes 1048608 | tf_op jit(solution)/shard_map/all_to_all | solution.py:201
  45.9 1.5 %shard_map.78 = (bf16[4,32,1024]{2,1,0:T(8,128)(2,1)S(1)}, f32[4,256,128]{2,1,0:T(8,128)S(1)}) custom-call(f32[2,512]{1,0:T(2,128)S(1)} %add_convert_fusion.qpos_ref, f32[8,256]{1,0:T(8,128)S(1)} %convert_element_type.7.kpos_ref, bf16[4,64,2048]{2,1,0:T(8,128)(2,1)S(1)} %all-to-all-done.1.qg_ref, bf16[8,64,512]{2,1,0:T(8,128)(2,1)S(1)} %all-to-all-done.kv_ref), custom_call_target="tpu_custom_call" | custom-call | tf_op jit(solution)/shard_map/pallas_call | solution.py:106
  47.4 0.0 collective-permute-done.prev_ref
  47.4 4.1 %shard_map.79 = (bf16[4,64,1024]{2,1,0:T(8,128)(2,1)}, bf16[8,64,512]{2,1,0:T(8,128)(2,1)S(1)}, bf16[8,32,512]{2,1,0:T(8,128)(2,1)S(1)}) custom-call(f32[2,512]{1,0:T(2,128)S(1)} %add_convert_fusion.qpos_ref, f32[8,256]{1,0:T(8,128)S(1)} %convert_element_type.7.kpos_ref, bf16[4,64,2048]{2,1,0:T(8,128)(2,1)S(1)} %all-to-all-done.1.qg_ref, ...), custom_call_target="tpu_custom_call" | custom-call | tf_op jit(solution)/shard_map/pallas_call | solution.py:114
  51.5 4.2 %all-to-all-start.2 = ((bf16[4,64,1024]{2,1,0:T(8,128)(2,1)}), bf16[4,64,1024]{2,1,0:T(8,128)(2,1)S(1)}, u32[]{:S(2)}, u32[]{:S(2)}) async-start(bf16[4,64,1024]{2,1,0:T(8,128)(2,1)} %get-tuple-element.22), calls=%async_computation.2 | async-start | bytes 1048576 | tf_op jit(solution)/shard_map/all_to_all | solution.py:201
  55.7 10.5 %collective-permute-start.1 = (bf16[8,32,512]{2,1,0:T(8,128)(2,1)S(1)}, bf16[8,32,512]{2,1,0:T(8,128)(2,1)S(1)}, u32[]{:S(2)}, u32[]{:S(2)}) collective-permute-start(bf16[8,32,512]{2,1,0:T(8,128)(2,1)S(1)} %get-tuple-element.23), channel_id=1, source_target_pairs={{1,0},{2,1},{3,2},{4,3},{5,4},{6,5},{7,6},{8,7},{9,8},{10,9},{11,1... | collective-permute-start | bytes 786440 | tf_op jit(solution)/shard_map/ppermute | solution.py:224
  66.3 5.4 %collective-permute-done.1.back_ref = bf16[8,32,512]{2,1,0:T(8,128)(2,1)S(1)} collective-permute-done((bf16[8,32,512]{2,1,0:T(8,128)(2,1)S(1)}, bf16[8,32,512]{2,1,0:T(8,128)(2,1)S(1)}, u32[]{:S(2)}, u32[]{:S(2)}) %collective-permute-start.1) | collective-permute-done | bytes 262176 | tf_op jit(solution)/shard_map/ppermute | solution.py:224
  71.7 0.0 all-to-all-done.2.dq_ref
  71.7 0.1 shard_map.80
  71.8 18.1 %all_to_all.20.dkv_ref = bf16[8,64,512]{2,1,0:T(8,128)(2,1)S(1)} all-to-all(bf16[8,64,512]{2,1,0:T(8,128)(2,1)S(1)} %shard_map.80), channel_id=1, replica_groups=mesh['head'=8,'blk'=64] {'head'}, dimensions={0} | all-to-all | bytes 1048576 | tf_op jit(solution)/shard_map/all_to_all | solution.py:204
  89.9 0.9 %shard_map.81 = (bf16[64,4096]{1,0:T(8,128)(2,1)}, bf16[64,1024]{1,0:T(8,128)(2,1)}, bf16[64,1024]{1,0:T(8,128)(2,1)}) custom-call(bf16[4,64,1024]{2,1,0:T(8,128)(2,1)S(1)} %all-to-all-done.2.dq_ref, bf16[8,64,512]{2,1,0:T(8,128)(2,1)S(1)} %all_to_all.20.dkv_ref), custom_call_target="tpu_custom_call" | custom-call | tf_op jit(solution)/shard_map/pallas_call | solution.py:182
  (6 shorter events, 0.1 us)
Async XLA Ops:
  2.4 26.9 %all-to-all-start = ((bf16[8,64,512]{2,1,0:T(8,128)(2,1)}), bf16[8,64,512]{2,1,0:T(8,128)(2,1)S(1)}, u32[]{:S(2)}, u32[]{:S(2)}) async-start(bf16[8,64,512]{2,1,0:T(8,128)(2,1)} %shard_map.76), calls=%async_computation | async-start | bytes 1048576 | tf_op jit(solution)/shard_map/all_to_all | solution.py:204
  10.2 0.7 copy-start
  29.3 16.6 %all-to-all-start.1 = ((bf16[4,64,2048]{2,1,0:T(8,128)(2,1)}), bf16[4,64,2048]{2,1,0:T(8,128)(2,1)S(1)}, u32[]{:S(2)}, u32[]{:S(2)}) async-start(bf16[4,64,2048]{2,1,0:T(8,128)(2,1)} %shard_map.77), calls=%async_computation.1 | async-start | bytes 2097152 | tf_op jit(solution)/shard_map/all_to_all | solution.py:201
  32.8 14.5 %collective-permute-start = (bf16[8,32,512]{2,1,0:T(8,128)(2,1)S(1)}, bf16[8,32,512]{2,1,0:T(8,128)(2,1)S(1)}, u32[]{:S(2)}, u32[]{:S(2)}) collective-permute-start(bf16[8,32,512]{2,1,0:T(8,128)(2,1)S(1)} %slice.3), channel_id=1, source_target_pairs={{0,1},{1,2},{2,3},{3,4},{4,5},{5,6},{6,7},{7,8},{8,9},{9,10},{10,1... | collective-permute-start | bytes 786440 | tf_op jit(solution)/shard_map/ppermute | solution.py:219
  51.5 20.2 %all-to-all-start.2 = ((bf16[4,64,1024]{2,1,0:T(8,128)(2,1)}), bf16[4,64,1024]{2,1,0:T(8,128)(2,1)S(1)}, u32[]{:S(2)}, u32[]{:S(2)}) async-start(bf16[4,64,1024]{2,1,0:T(8,128)(2,1)} %get-tuple-element.22), calls=%async_computation.2 | async-start | bytes 1048576 | tf_op jit(solution)/shard_map/all_to_all | solution.py:201
  55.7 16.0 %collective-permute-start.1 = (bf16[8,32,512]{2,1,0:T(8,128)(2,1)S(1)}, bf16[8,32,512]{2,1,0:T(8,128)(2,1)S(1)}, u32[]{:S(2)}, u32[]{:S(2)}) collective-permute-start(bf16[8,32,512]{2,1,0:T(8,128)(2,1)S(1)} %get-tuple-element.23), channel_id=1, source_target_pairs={{1,0},{2,1},{3,2},{4,3},{5,4},{6,5},{7,6},{8,7},{9,8},{10,9},{11,1... | collective-permute-start | bytes 786440 | tf_op jit(solution)/shard_map/ppermute | solution.py:224
